TPU v7x, 32 devices: a whole 2x2x4 slice. The times are simulated.
32 devices in a mesh: fsdp: 8 (over y, x, core), seq: 4 (over z).
Axes of the slice: x: 2, y: 2, z: 4, core: 2. Of those that a mesh axis runs over, the one named last changes fastest.
Arguments:
- inputs: bfloat16 [3, 8, 1024, 1024], P(None, 'fsdp', 'seq'), may hold values from -6 to 6
- segment_ids: int32 [3, 8, 1024], P(None, 'fsdp'), may hold values from 0 to 3, never falling along the last dimension, each value on 1 to 512 neighbouring positions
- buckets: int32 [1024], replicated, may hold values from 0 to 31, as said below
- ln1_gain: bfloat16 [1024], P('fsdp'), may hold values from 0.5 to 1.5
- ln1_bias: bfloat16 [1024], P('fsdp'), may hold values from -3 to 3
- w_query: bfloat16 [1024, 1024], P('fsdp'), may hold values from -0.1875 to 0.1875
- w_key: bfloat16 [1024, 1024], P('fsdp'), may hold values from -0.1875 to 0.1875
- w_value: bfloat16 [1024, 1024], P('fsdp'), may hold values from -0.1875 to 0.1875
- w_out: bfloat16 [1024, 1024], P('fsdp'), may hold values from -0.75 to 0.75
- rel_bias: bfloat16 [32, 16], P('fsdp'), may hold values from -4 to 4
- second_norm_gain: bfloat16 [1024], P('fsdp'), may hold values from 0.5 to 1.5
- ln2_bias: bfloat16 [1024], P('fsdp'), may hold values from -3 to 3
- w_up: bfloat16 [1024, 4096], P('fsdp'), may hold values from -0.1875 to 0.1875
- b_up: bfloat16 [4096], P('fsdp'), may hold values from -3 to 3
- w_down: bfloat16 [4096, 1024], P('fsdp'), may hold values from -0.09375 to 0.09375
- b_down: bfloat16 [1024], P('fsdp'), may hold values from -3 to 3
- cotangent: bfloat16 [3, 8, 1024, 1024], P(None, 'fsdp', 'seq'), may hold values from -6 to 6
Outputs:
- outputs: bfloat16 [3, 8, 1024, 1024], P(None, 'fsdp', 'seq')
- input_grad: bfloat16 [3, 8, 1024, 1024], P(None, 'fsdp', 'seq')
- grad_ln1_gain: float32 [1024], P('fsdp')
- grad_ln1_bias: float32 [1024], P('fsdp')
- grad_w_query: float32 [1024, 1024], P('fsdp')
- grad_w_key: float32 [1024, 1024], P('fsdp')
- grad_w_value: float32 [1024, 1024], P('fsdp')
- grad_w_out: float32 [1024, 1024], P('fsdp')
- grad_rel_bias: float32 [32, 16], P('fsdp')
- grad_ln2_gain: float32 [1024], P('fsdp')
- grad_ln2_bias: float32 [1024], P('fsdp')
- grad_w_up: float32 [1024, 4096], P('fsdp')
- grad_b_up: float32 [4096], P('fsdp')
- grad_w_down: float32 [4096, 1024], P('fsdp')
- grad_b_down: float32 [1024], P('fsdp')
Inputs may be any that keep to these rules, and one draw needn't show every extreme that they name: `segment_ids`: along a row the clip number never falls; each clip of a row has 1 to 512 tokens, and some clip has exactly 512. `buckets`: the bucket never falls as the distance grows; it is 0 at distance 0 and 31 at distance 1024 - 1.
All inputs are finite; a program needn't handle non-finite values.
Results may differ from a plain program's by a relative error of at most 0.025.
Values may be sent and summed in bfloat16 or wider, within the bound.
No kernel may reach another device: no remote copies, remote signals or barrier semaphores. Data moves between devices by JAX's collectives and lax.ppermute only.
A program may use at most 448 MiB of HBM per device.

v0:
```python
import jax
import jax.numpy as jnp
from jax import lax
from jax.sharding import PartitionSpec as P

epsilon = 1e-05
masked_out = -1e30
EXACT_PRECISION = lax.Precision.HIGHEST


def layer_norm(field, norm_gain, norm_shift):
    centre = field - jnp.mean(field, axis=-1, keepdims=True)
    spread = jnp.mean(centre * centre, axis=-1, keepdims=True)
    return centre * lax.rsqrt(spread + epsilon) * norm_gain + norm_shift


def gelu_exact(field):
    return jax.nn.gelu(field, approximate=False)


def token_dot(left, right):
    return lax.dot_general(
        left, right, (((0,), (0,)), ((), ())), preferred_element_type=jnp.float32
    )


def back_dot(left, right):
    return lax.dot_general(
        left, right, (((1,), (1,)), ((), ())), preferred_element_type=jnp.float32
    )


def bucket_onehot(distance, first_dist, bucket_ids):
    reached = (distance[None] >= first_dist[:, None, None]).astype(jnp.int32)
    bucket_rows = jnp.sum(reached[1:], axis=0)
    return (bucket_ids[:, None, None] == bucket_rows[None]).astype(jnp.float32)


def per_device(
    inputs,
    segment_ids,
    buckets,
    ln1_gain,
    ln1_bias,
    w_query,
    w_key,
    w_value,
    w_out,
    rel_bias,
    second_norm_gain,
    ln2_bias,
    w_up,
    b_up,
    w_down,
    b_down,
    cotangent,
):
    num_micro, num_rows, local_len, model_width = inputs.shape
    seq_len = segment_ids.shape[2]
    head_count = rel_bias.shape[1]
    head_dim = model_width // head_count
    score_scale = head_dim ** (-0.5)
    num_buckets = rel_bias.shape[0] * lax.axis_size("fsdp")
    num_tokens = num_rows * local_len
    first_pos = lax.axis_index("seq") * local_len
    query_pos = first_pos + jnp.arange(local_len, dtype=jnp.int32)
    key_pos = jnp.arange(seq_len, dtype=jnp.int32)
    distance = query_pos[:, None] - key_pos[None, :]
    causal = distance >= 0
    bucket_ids = jnp.arange(num_buckets, dtype=jnp.int32)
    first_dist = jnp.sum((buckets[None, :] < bucket_ids[:, None]).astype(jnp.int32), axis=1)
    bucket_onehot_matrix = bucket_onehot(distance, first_dist, bucket_ids)
    summed = None
    result_list = []
    grad_list = []
    for micro_step in range(num_micro):
        gathered = (
            lax.all_gather(ln1_gain, "fsdp", axis=0, tiled=True),
            lax.all_gather(ln1_bias, "fsdp", axis=0, tiled=True),
            lax.all_gather(w_query, "fsdp", axis=0, tiled=True),
            lax.all_gather(w_key, "fsdp", axis=0, tiled=True),
            lax.all_gather(w_value, "fsdp", axis=0, tiled=True),
            lax.all_gather(w_out, "fsdp", axis=0, tiled=True),
            lax.all_gather(rel_bias, "fsdp", axis=0, tiled=True),
            lax.all_gather(second_norm_gain, "fsdp", axis=0, tiled=True),
            lax.all_gather(ln2_bias, "fsdp", axis=0, tiled=True),
            lax.all_gather(w_up, "fsdp", axis=0, tiled=True),
            lax.all_gather(b_up, "fsdp", axis=0, tiled=True),
            lax.all_gather(w_down, "fsdp", axis=0, tiled=True),
            lax.all_gather(b_down, "fsdp", axis=0, tiled=True),
        )
        (
            norm1_gain,
            norm1_shift,
            query_mat,
            key_mat,
            value_mat,
            out_mat,
            rel_table,
            norm2_gain,
            norm2_shift,
            up_mat,
            up_bias,
            down_mat,
            down_bias,
        ) = gathered
        relative_float_bias = rel_table.astype(jnp.float32)
        score_position_bias = jnp.einsum(
            "uia,uw->wia", bucket_onehot_matrix, relative_float_bias, precision=EXACT_PRECISION
        )
        row_x = inputs[micro_step].reshape(num_tokens, model_width).astype(jnp.float32)
        normed_one, norm1_pull = jax.vjp(
            layer_norm, row_x, norm1_gain.astype(jnp.float32), norm1_shift.astype(jnp.float32)
        )
        normed_low = normed_one.astype(jnp.bfloat16)
        queries = jnp.dot(normed_low, query_mat, preferred_element_type=jnp.float32).astype(
            jnp.bfloat16
        )
        keys_local = jnp.dot(normed_low, key_mat, preferred_element_type=jnp.float32).astype(
            jnp.bfloat16
        )
        values_local = jnp.dot(normed_low, value_mat, preferred_element_type=jnp.float32).astype(
            jnp.bfloat16
        )
        keys_all, values_all = (
            lax.all_gather(
                keys_local.reshape(num_rows, local_len, model_width), "seq", axis=1, tiled=True
            ),
            lax.all_gather(
                values_local.reshape(num_rows, local_len, model_width), "seq", axis=1, tiled=True
            ),
        )
        row_segment_ids = segment_ids[micro_step]
        query_segs = lax.dynamic_slice_in_dim(row_segment_ids, first_pos, local_len, 1)
        seg_mask = (query_segs[:, :, None] == row_segment_ids[:, None, :]) & causal[None]
        query_four = queries.reshape(num_rows, local_len, head_count, head_dim)
        keys_four = keys_all.reshape(num_rows, seq_len, head_count, head_dim)
        values_four = values_all.reshape(num_rows, seq_len, head_count, head_dim)

        def make_logits():
            raw_scores = (
                jnp.einsum(
                    "rqhd,rkhd->rhqk", query_four, keys_four, preferred_element_type=jnp.float32
                )
                * score_scale
                + score_position_bias[None]
            )
            return jnp.where(seg_mask[:, None], raw_scores, masked_out)

        logits = make_logits()
        row_peak = jnp.max(logits, axis=-1, keepdims=True)
        expo = jnp.exp(logits - row_peak)
        row_total = jnp.sum(expo, axis=-1, keepdims=True)
        soft_probs = expo / row_total
        log_total = row_peak + jnp.log(row_total)
        attended = jnp.einsum(
            "rhqk,rkhd->rqhd",
            soft_probs.astype(jnp.bfloat16),
            values_four,
            preferred_element_type=jnp.float32,
        )
        attended = attended.reshape(num_tokens, model_width).astype(jnp.bfloat16)
        middle = row_x + jnp.dot(attended, out_mat, preferred_element_type=jnp.float32)
        normed_two, norm2_pull = jax.vjp(
            layer_norm, middle, norm2_gain.astype(jnp.float32), norm2_shift.astype(jnp.float32)
        )
        normed_two_low = normed_two.astype(jnp.bfloat16)
        pre_act = jnp.dot(
            normed_two_low, up_mat, preferred_element_type=jnp.float32
        ) + up_bias.astype(jnp.float32)
        activation, gelu_pull = jax.vjp(gelu_exact, pre_act)
        activation_low = activation.astype(jnp.bfloat16)
        result_row = (
            middle
            + jnp.dot(activation_low, down_mat, preferred_element_type=jnp.float32)
            + down_bias.astype(jnp.float32)
        )
        result_list.append(
            result_row.astype(jnp.bfloat16).reshape(num_rows, local_len, model_width)
        )
        grad_out = cotangent[micro_step].reshape(num_tokens, model_width)
        grad_out_f = grad_out.astype(jnp.float32)
        grad_w_down = token_dot(activation_low, grad_out)
        grad_b_down = jnp.sum(grad_out_f, axis=0)
        grad_act = back_dot(grad_out, down_mat)
        grad_pre = gelu_pull(grad_act)[0].astype(jnp.bfloat16)
        grad_b_up = jnp.sum(grad_pre.astype(jnp.float32), axis=0)
        grad_w_up = token_dot(normed_two_low, grad_pre)
        grad_norm2 = back_dot(grad_pre, up_mat)
        grad_mid_norm, grad_ln2_gain, grad_ln2_bias = norm2_pull(grad_norm2)
        grad_middle = grad_out_f + grad_mid_norm
        grad_branch = grad_middle.astype(jnp.bfloat16)
        grad_w_out = token_dot(attended, grad_branch)
        grad_attended = (
            back_dot(grad_branch, out_mat)
            .astype(jnp.bfloat16)
            .reshape(num_rows, local_len, head_count, head_dim)
        )
        again_probs = jnp.exp(make_logits() - log_total)
        grad_probs = jnp.einsum(
            "rqhd,rkhd->rhqk", grad_attended, values_four, preferred_element_type=jnp.float32
        )
        row_delta = jnp.sum(grad_probs * again_probs, axis=-1, keepdims=True)
        grad_scores = (again_probs * (grad_probs - row_delta)).astype(jnp.bfloat16)
        grad_queries = (
            jnp.einsum(
                "rhqk,rkhd->rqhd", grad_scores, keys_four, preferred_element_type=jnp.float32
            )
            * score_scale
        ).astype(jnp.bfloat16)
        grad_rel = jnp.einsum(
            "vlp,glp->vg",
            bucket_onehot_matrix,
            jnp.sum(grad_scores.astype(jnp.float32), axis=0),
            precision=EXACT_PRECISION,
        )
        grad_values = jnp.einsum(
            "rhqk,rqhd->rkhd",
            again_probs.astype(jnp.bfloat16),
            grad_attended,
            preferred_element_type=jnp.float32,
        )
        grad_keys = (
            jnp.einsum(
                "rhqk,rqhd->rkhd", grad_scores, query_four, preferred_element_type=jnp.float32
            )
            * score_scale
        )
        key_grads, value_grads = (
            lax.psum_scatter(
                grad_keys.reshape(num_rows, seq_len, model_width).astype(jnp.bfloat16),
                "seq",
                scatter_dimension=1,
                tiled=True,
            ).astype(jnp.float32),
            lax.psum_scatter(
                grad_values.reshape(num_rows, seq_len, model_width).astype(jnp.bfloat16),
                "seq",
                scatter_dimension=1,
                tiled=True,
            ).astype(jnp.float32),
        )
        key_grads = key_grads.astype(jnp.bfloat16).reshape(num_tokens, model_width)
        value_grads = value_grads.astype(jnp.bfloat16).reshape(num_tokens, model_width)
        grad_queries = grad_queries.reshape(num_tokens, model_width)
        grad_w_query = token_dot(normed_low, grad_queries)
        grad_w_key = token_dot(normed_low, key_grads)
        grad_w_value = token_dot(normed_low, value_grads)
        gradient_first_norm = (
            back_dot(grad_queries, query_mat)
            + back_dot(key_grads, key_mat)
            + back_dot(value_grads, value_mat)
        )
        grad_x_norm, grad_ln1_gain, grad_ln1_bias = norm1_pull(gradient_first_norm)
        grad_list.append(
            (grad_middle + grad_x_norm)
            .astype(jnp.bfloat16)
            .reshape(num_rows, local_len, model_width)
        )
        local_grads = (
            grad_ln1_gain,
            grad_ln1_bias,
            grad_w_query,
            grad_w_key,
            grad_w_value,
            grad_w_out,
            grad_rel,
            grad_ln2_gain,
            grad_ln2_bias,
            grad_w_up,
            grad_b_up,
            grad_w_down,
            grad_b_down,
        )
        shard_part = (
            lax.psum_scatter(
                local_grads[0].astype(jnp.bfloat16), "fsdp", scatter_dimension=0, tiled=True
            ).astype(jnp.float32),
            lax.psum_scatter(
                local_grads[1].astype(jnp.bfloat16), "fsdp", scatter_dimension=0, tiled=True
            ).astype(jnp.float32),
            lax.psum_scatter(
                local_grads[2].astype(jnp.bfloat16), "fsdp", scatter_dimension=0, tiled=True
            ).astype(jnp.float32),
            lax.psum_scatter(
                local_grads[3].astype(jnp.bfloat16), "fsdp", scatter_dimension=0, tiled=True
            ).astype(jnp.float32),
            lax.psum_scatter(
                local_grads[4].astype(jnp.bfloat16), "fsdp", scatter_dimension=0, tiled=True
            ).astype(jnp.float32),
            lax.psum_scatter(
                local_grads[5].astype(jnp.bfloat16), "fsdp", scatter_dimension=0, tiled=True
            ).astype(jnp.float32),
            lax.psum_scatter(
                local_grads[6].astype(jnp.bfloat16), "fsdp", scatter_dimension=0, tiled=True
            ).astype(jnp.float32),
            lax.psum_scatter(
                local_grads[7].astype(jnp.bfloat16), "fsdp", scatter_dimension=0, tiled=True
            ).astype(jnp.float32),
            lax.psum_scatter(
                local_grads[8].astype(jnp.bfloat16), "fsdp", scatter_dimension=0, tiled=True
            ).astype(jnp.float32),
            lax.psum_scatter(
                local_grads[9].astype(jnp.bfloat16), "fsdp", scatter_dimension=0, tiled=True
            ).astype(jnp.float32),
            lax.psum_scatter(
                local_grads[10].astype(jnp.bfloat16), "fsdp", scatter_dimension=0, tiled=True
            ).astype(jnp.float32),
            lax.psum_scatter(
                local_grads[11].astype(jnp.bfloat16), "fsdp", scatter_dimension=0, tiled=True
            ).astype(jnp.float32),
            lax.psum_scatter(
                local_grads[12].astype(jnp.bfloat16), "fsdp", scatter_dimension=0, tiled=True
            ).astype(jnp.float32),
        )
        summed = shard_part if summed is None else jax.tree.map(jnp.add, summed, shard_part)
    totals = (
        lax.psum(summed[0].astype(jnp.bfloat16), "seq").astype(jnp.float32),
        lax.psum(summed[1].astype(jnp.bfloat16), "seq").astype(jnp.float32),
        lax.psum(summed[2].astype(jnp.bfloat16), "seq").astype(jnp.float32),
        lax.psum(summed[3].astype(jnp.bfloat16), "seq").astype(jnp.float32),
        lax.psum(summed[4].astype(jnp.bfloat16), "seq").astype(jnp.float32),
        lax.psum(summed[5].astype(jnp.bfloat16), "seq").astype(jnp.float32),
        lax.psum(summed[6].astype(jnp.bfloat16), "seq").astype(jnp.float32),
        lax.psum(summed[7].astype(jnp.bfloat16), "seq").astype(jnp.float32),
        lax.psum(summed[8].astype(jnp.bfloat16), "seq").astype(jnp.float32),
        lax.psum(summed[9].astype(jnp.bfloat16), "seq").astype(jnp.float32),
        lax.psum(summed[10].astype(jnp.bfloat16), "seq").astype(jnp.float32),
        lax.psum(summed[11].astype(jnp.bfloat16), "seq").astype(jnp.float32),
        lax.psum(summed[12].astype(jnp.bfloat16), "seq").astype(jnp.float32),
    )
    return (
        jnp.stack(result_list),
        jnp.stack(grad_list),
        totals[0],
        totals[1],
        totals[2],
        totals[3],
        totals[4],
        totals[5],
        totals[6],
        totals[7],
        totals[8],
        totals[9],
        totals[10],
        totals[11],
        totals[12],
    )


def solution(mesh):
    return jax.shard_map(
        per_device,
        mesh=mesh,
        in_specs=(
            P(None, "fsdp", "seq", None),
            P(None, "fsdp", None),
            P(),
            P("fsdp"),
            P("fsdp"),
            P("fsdp", None),
            P("fsdp", None),
            P("fsdp", None),
            P("fsdp", None),
            P("fsdp", None),
            P("fsdp"),
            P("fsdp"),
            P("fsdp", None),
            P("fsdp"),
            P("fsdp", None),
            P("fsdp"),
            P(None, "fsdp", "seq", None),
        ),
        out_specs=(
            P(None, "fsdp", "seq", None),
            P(None, "fsdp", "seq", None),
            P("fsdp"),
            P("fsdp"),
            P("fsdp", None),
            P("fsdp", None),
            P("fsdp", None),
            P("fsdp", None),
            P("fsdp", None),
            P("fsdp"),
            P("fsdp"),
            P("fsdp", None),
            P("fsdp"),
            P("fsdp", None),
            P("fsdp"),
        ),
        check_vma=False,
    )
```

profile of v0, /device:TPU:0, one launch (start us, length us, event | category | flops | bytes accessed | tf_op | source)
XLA Modules:
  0.0 2055.5 jit_solution(9363248587604546310)
XLA Ops:
  197.7 43.8 %all-gather.46.cloned.1.call-done = bf16[1024,1024]{1,0:T(8,128)(2,1)} async-done(((bf16[256,1024]{1,0:T(8,128)(2,1)}), bf16[1024,1024]{1,0:T(8,128)(2,1)}) %all-gather.46.cloned.1.call-update) | async-done | bytes 2097168 | tf_op jit(solution)/shard_map/all_gather | solution.py:129
  245.5 42.9 %all-gather.38.cloned.1.call-done = bf16[1024,1024]{1,0:T(8,128)(2,1)} async-done(((bf16[256,1024]{1,0:T(8,128)(2,1)}), bf16[1024,1024]{1,0:T(8,128)(2,1)}) %all-gather.38.cloned.1.call-update) | async-done | bytes 2097168 | tf_op jit(solution)/shard_map/all_gather | solution.py:129
  593.6 41.8 %reduce-scatter.25.cloned.1.call-done = bf16[1,256,1024]{1,2,0:T(8,128)(2,1)} async-done(((bf16[1,1024,1024]{1,2,0:T(8,128)(2,1)}), bf16[1,256,1024]{1,2,0:T(8,128)(2,1)}) %reduce-scatter.25.cloned.1.call-update) | async-done | bytes 524304 | tf_op jit(solution)/shard_map/reduce_scatter | solution.py:230
  638.9 42.0 %reduce-scatter.27.cloned.1.call-done = bf16[1,256,1024]{1,2,0:T(8,128)(2,1)} async-done(((bf16[1,1024,1024]{1,2,0:T(8,128)(2,1)}), bf16[1,256,1024]{1,2,0:T(8,128)(2,1)}) %reduce-scatter.27.cloned.1.call-update) | async-done | bytes 524304 | tf_op jit(solution)/shard_map/reduce_scatter | solution.py:236
  693.6 39.5 %all-gather.44.cloned.1.call-done = bf16[1024,1024]{1,0:T(8,128)(2,1)} async-done(((bf16[256,1024]{1,0:T(8,128)(2,1)}), bf16[1024,1024]{1,0:T(8,128)(2,1)}) %all-gather.44.cloned.1.call-update) | async-done | bytes 2097168 | tf_op jit(solution)/shard_map/all_gather | solution.py:126
  897.1 27.6 %reduce-scatter.29.cloned.1.call-done = bf16[1,256,1024]{1,2,0:T(8,128)(2,1)} async-done(((bf16[1,1024,1024]{1,2,0:T(8,128)(2,1)}), bf16[1,256,1024]{1,2,0:T(8,128)(2,1)}) %reduce-scatter.29.cloned.1.call-update) | async-done | bytes 524304 | tf_op jit(solution)/shard_map/reduce_scatter | solution.py:230
  1033.5 24.4 %reduce-scatter.57.cloned.1.call-done = bf16[128,1024]{1,0:T(8,128)(2,1)} async-done(((bf16[1024,1024]{1,0:T(8,128)(2,1)}), bf16[128,1024]{1,0:T(8,128)(2,1)}) %reduce-scatter.57.cloned.1.call-update) | async-done | bytes 262160 | tf_op jit(solution)/shard_map/reduce_scatter | solution.py:291
  1059.8 42.9 %reduce-scatter.41.cloned.1.call-done = bf16[128,1024]{1,0:T(8,128)(2,1)} async-done(((bf16[1024,1024]{1,0:T(8,128)(2,1)}), bf16[128,1024]{1,0:T(8,128)(2,1)}) %reduce-scatter.41.cloned.1.call-update) | async-done | bytes 262160 | tf_op jit(solution)/shard_map/reduce_scatter | solution.py:282
  1102.7 44.5 %reduce-scatter.37.cloned.1.call-done = bf16[128,1024]{1,0:T(8,128)(2,1)} async-done(((bf16[1024,1024]{1,0:T(8,128)(2,1)}), bf16[128,1024]{1,0:T(8,128)(2,1)}) %reduce-scatter.37.cloned.1.call-update) | async-done | bytes 262160 | tf_op jit(solution)/shard_map/reduce_scatter | solution.py:282
  1147.2 44.7 %reduce-scatter.39.cloned.1.call-done = bf16[128,1024]{1,0:T(8,128)(2,1)} async-done(((bf16[1024,1024]{1,0:T(8,128)(2,1)}), bf16[128,1024]{1,0:T(8,128)(2,1)}) %reduce-scatter.39.cloned.1.call-update) | async-done | bytes 262160 | tf_op jit(solution)/shard_map/reduce_scatter | solution.py:282
  1197.7 38.8 %reduce-scatter.49.cloned.1.call-done = bf16[128,1024]{1,0:T(8,128)(2,1)} async-done(((bf16[1024,1024]{1,0:T(8,128)(2,1)}), bf16[128,1024]{1,0:T(8,128)(2,1)}) %reduce-scatter.49.cloned.1.call-update) | async-done | bytes 262160 | tf_op jit(solution)/shard_map/reduce_scatter | solution.py:288
  1236.5 44.7 %reduce-scatter.53.cloned.1.call-done = bf16[128,1024]{1,0:T(8,128)(2,1)} async-done(((bf16[1024,1024]{1,0:T(8,128)(2,1)}), bf16[128,1024]{1,0:T(8,128)(2,1)}) %reduce-scatter.53.cloned.1.call-update) | async-done | bytes 262160 | tf_op jit(solution)/shard_map/reduce_scatter | solution.py:288
  1281.3 44.4 %reduce-scatter.51.cloned.1.call-done = bf16[128,1024]{1,0:T(8,128)(2,1)} async-done(((bf16[1024,1024]{1,0:T(8,128)(2,1)}), bf16[128,1024]{1,0:T(8,128)(2,1)}) %reduce-scatter.51.cloned.1.call-update) | async-done | bytes 262160 | tf_op jit(solution)/shard_map/reduce_scatter | solution.py:288
  1327.6 43.0 %reduce-scatter.47.cloned.1.call-done = bf16[128,1024]{1,0:T(8,128)(2,1)} async-done(((bf16[1024,1024]{1,0:T(8,128)(2,1)}), bf16[128,1024]{1,0:T(8,128)(2,1)}) %reduce-scatter.47.cloned.1.call-update) | async-done | bytes 262160 | tf_op jit(solution)/shard_map/reduce_scatter | solution.py:285
  1370.5 44.5 %reduce-scatter.43.cloned.1.call-done = bf16[128,1024]{1,0:T(8,128)(2,1)} async-done(((bf16[1024,1024]{1,0:T(8,128)(2,1)}), bf16[128,1024]{1,0:T(8,128)(2,1)}) %reduce-scatter.43.cloned.1.call-update) | async-done | bytes 262160 | tf_op jit(solution)/shard_map/reduce_scatter | solution.py:285
  1415.1 44.7 %reduce-scatter.45.cloned.1.call-done = bf16[128,1024]{1,0:T(8,128)(2,1)} async-done(((bf16[1024,1024]{1,0:T(8,128)(2,1)}), bf16[128,1024]{1,0:T(8,128)(2,1)}) %reduce-scatter.45.cloned.1.call-update) | async-done | bytes 262160 | tf_op jit(solution)/shard_map/reduce_scatter | solution.py:285
  1461.7 72.8 %reduce-scatter.65.cloned.1.call-done = bf16[128,4096]{1,0:T(8,128)(2,1)} async-done(((bf16[1024,4096]{1,0:T(8,128)(2,1)}), bf16[128,4096]{1,0:T(8,128)(2,1)}) %reduce-scatter.65.cloned.1.call-update) | async-done | bytes 1048592 | tf_op jit(solution)/shard_map/reduce_scatter | solution.py:303
  1534.6 75.2 %reduce-scatter.61.cloned.1.call-done = bf16[128,4096]{1,0:T(8,128)(2,1)} async-done(((bf16[1024,4096]{1,0:T(8,128)(2,1)}), bf16[128,4096]{1,0:T(8,128)(2,1)}) %reduce-scatter.61.cloned.1.call-update) | async-done | bytes 1048592 | tf_op jit(solution)/shard_map/reduce_scatter | solution.py:303
  1609.8 74.6 %reduce-scatter.63.cloned.1.call-done = bf16[128,4096]{1,0:T(8,128)(2,1)} async-done(((bf16[1024,4096]{1,0:T(8,128)(2,1)}), bf16[128,4096]{1,0:T(8,128)(2,1)}) %reduce-scatter.63.cloned.1.call-update) | async-done | bytes 1048592 | tf_op jit(solution)/shard_map/reduce_scatter | solution.py:303
  1687.7 71.9 %reduce-scatter.71.cloned.1.call-done = bf16[512,1024]{1,0:T(8,128)(2,1)} async-done(((bf16[4096,1024]{1,0:T(8,128)(2,1)}), bf16[512,1024]{1,0:T(8,128)(2,1)}) %reduce-scatter.71.cloned.1.call-update) | async-done | bytes 1048592 | tf_op jit(solution)/shard_map/reduce_scatter | solution.py:309
  1759.6 74.8 %reduce-scatter.67.cloned.1.call-done = bf16[512,1024]{1,0:T(8,128)(2,1)} async-done(((bf16[4096,1024]{1,0:T(8,128)(2,1)}), bf16[512,1024]{1,0:T(8,128)(2,1)}) %reduce-scatter.67.cloned.1.call-update) | async-done | bytes 1048592 | tf_op jit(solution)/shard_map/reduce_scatter | solution.py:309
  1834.3 75.0 %reduce-scatter.69.cloned.1.call-done = bf16[512,1024]{1,0:T(8,128)(2,1)} async-done(((bf16[4096,1024]{1,0:T(8,128)(2,1)}), bf16[512,1024]{1,0:T(8,128)(2,1)}) %reduce-scatter.69.cloned.1.call-update) | async-done | bytes 1048592 | tf_op jit(solution)/shard_map/reduce_scatter | solution.py:309
  1919.6 25.7 %all-reduce.21 = (bf16[1024]{0:T(1024)(128)(2,1)S(1)}, bf16[1024]{0:T(1024)(128)(2,1)S(1)}, bf16[1024]{0:T(1024)(128)(2,1)S(1)}, bf16[1024]{0:T(1024)(128)(2,1)S...) all-reduce(bf16[1024]{0:T(1024)(128)(2,1)S(1)} %get-tuple-element.1, ...), channel_id=16, replica_groups=mesh['fsdp'=8,'seq'=4] {'fsdp'}, use_global_device_ids=true, to_apply=%region_46.47.clone | all-reduce | flops 29184 | bytes 116736
  1966.4 70.2 %all-reduce.26.cloned.1.call-done = (bf16[128,1024]{1,0:T(8,128)(2,1)}, bf16[128,1024]{1,0:T(8,128)(2,1)}, bf16[128,1024]{1,0:T(8,128)(2,1)}, bf16[128,1024]{1,0...) async-done(((bf16[128,1024]{1,0:T(8,128)(2,1)}, bf16[128,1024]{1,0:T(8,128)(2,1)}, bf16[128,1024]{1,0:T(8,128)(2,1)}, bf16[128,1024]{1,0:T(8,128)(2,1)}, ...) | async-done | bytes 3145744 | tf_op jit(solution)/shard_map/psum | solution.py:320
  (623 shorter events, 841.6 us)
Async XLA Ops:
  47.1 194.4 %all-gather.46.cloned.1.call-start = ((), (), s32[]{:S(2)}) async-start(), calls=%async_computation.58 | async-start | bytes 2621440 | tf_op jit(solution)/shard_map/all_gather | solution.py:129
  73.6 214.8 %all-gather.38.cloned.1.call-start = ((), (), s32[]{:S(2)}) async-start(), calls=%async_computation.54 | async-start | bytes 2621440 | tf_op jit(solution)/shard_map/all_gather | solution.py:129
  76.8 240.1 %all-gather.32.cloned.1.call-start = ((), (), s32[]{:S(2)}) async-start(), calls=%async_computation.27 | async-start | bytes 2359296 | tf_op jit(solution)/shard_map/all_gather | solution.py:83
  77.5 295.7 %all-gather.34.cloned.1.call-start = ((), (), s32[]{:S(2)}) async-start(), calls=%async_computation.28 | async-start | bytes 9437184 | tf_op jit(solution)/shard_map/all_gather | solution.py:87
  78.3 351.1 %all-gather.36.cloned.1.call-start = ((), (), s32[]{:S(2)}) async-start(), calls=%async_computation.29 | async-start | bytes 9437184 | tf_op jit(solution)/shard_map/all_gather | solution.py:89
  78.8 489.5 %reduce-scatter.33.cloned.1.call-start = ((), (), s32[]{:S(2)}) async-start(), calls=%async_computation.34 | async-start | bytes 2621440 | tf_op jit(solution)/shard_map/reduce_scatter | solution.py:230
  690.9 197.3 %reduce-scatter.31.cloned.1.call-start = ((), (), s32[]{:S(2)}) async-start(), calls=%async_computation.33 | async-start | bytes 2621440 | tf_op jit(solution)/shard_map/reduce_scatter | solution.py:236
  862.8 195.1 %reduce-scatter.57.cloned.1.call-start = ((), (), s32[]{:S(2)}) async-start(), calls=%async_computation.46 | async-start | bytes 2359296 | tf_op jit(solution)/shard_map/reduce_scatter | solution.py:291
  864.9 237.8 %reduce-scatter.41.cloned.1.call-start = ((), (), s32[]{:S(2)}) async-start(), calls=%async_computation.38 | async-start | bytes 2359296 | tf_op jit(solution)/shard_map/reduce_scatter | solution.py:282
  868.2 279.0 %reduce-scatter.37.cloned.1.call-start = ((), (), s32[]{:S(2)}) async-start(), calls=%async_computation.36 | async-start | bytes 2359296 | tf_op jit(solution)/shard_map/reduce_scatter | solution.py:282
  871.9 320.1 %reduce-scatter.39.cloned.1.call-start = ((), (), s32[]{:S(2)}) async-start(), calls=%async_computation.37 | async-start | bytes 2359296 | tf_op jit(solution)/shard_map/reduce_scatter | solution.py:282
  882.5 354.0 %reduce-scatter.49.cloned.1.call-start = ((), (), s32[]{:S(2)}) async-start(), calls=%async_computation.42 | async-start | bytes 2359296 | tf_op jit(solution)/shard_map/reduce_scatter | solution.py:288
  885.9 395.4 %reduce-scatter.53.cloned.1.call-start = ((), (), s32[]{:S(2)}) async-start(), calls=%async_computation.44 | async-start | bytes 2359296 | tf_op jit(solution)/shard_map/reduce_scatter | solution.py:288
  888.2 437.5 %reduce-scatter.51.cloned.1.call-start = ((), (), s32[]{:S(2)}) async-start(), calls=%async_computation.43 | async-start | bytes 2359296 | tf_op jit(solution)/shard_map/reduce_scatter | solution.py:288
  891.5 479.0 %reduce-scatter.47.cloned.1.call-start = ((), (), s32[]{:S(2)}) async-start(), calls=%async_computation.41 | async-start | bytes 2359296 | tf_op jit(solution)/shard_map/reduce_scatter | solution.py:285
  893.8 521.3 %reduce-scatter.43.cloned.1.call-start = ((), (), s32[]{:S(2)}) async-start(), calls=%async_computation.39 | async-start | bytes 2359296 | tf_op jit(solution)/shard_map/reduce_scatter | solution.py:285
  897.1 562.7 %reduce-scatter.45.cloned.1.call-start = ((), (), s32[]{:S(2)}) async-start(), calls=%async_computation.40 | async-start | bytes 2359296 | tf_op jit(solution)/shard_map/reduce_scatter | solution.py:285
  928.0 606.6 %reduce-scatter.65.cloned.1.call-start = ((), (), s32[]{:S(2)}) async-start(), calls=%async_computation.50 | async-start | bytes 9437184 | tf_op jit(solution)/shard_map/reduce_scatter | solution.py:303
  935.8 673.9 %reduce-scatter.61.cloned.1.call-start = ((), (), s32[]{:S(2)}) async-start(), calls=%async_computation.48 | async-start | bytes 9437184 | tf_op jit(solution)/shard_map/reduce_scatter | solution.py:303
  944.4 740.0 %reduce-scatter.63.cloned.1.call-start = ((), (), s32[]{:S(2)}) async-start(), calls=%async_computation.49 | async-start | bytes 9437184 | tf_op jit(solution)/shard_map/reduce_scatter | solution.py:303
  952.5 807.0 %reduce-scatter.71.cloned.1.call-start = ((), (), s32[]{:S(2)}) async-start(), calls=%async_computation.53 | async-start | bytes 9437184 | tf_op jit(solution)/shard_map/reduce_scatter | solution.py:309
  961.3 873.1 %reduce-scatter.67.cloned.1.call-start = ((), (), s32[]{:S(2)}) async-start(), calls=%async_computation.51 | async-start | bytes 9437184 | tf_op jit(solution)/shard_map/reduce_scatter | solution.py:309
  968.8 940.6 %reduce-scatter.69.cloned.1.call-start = ((), (), s32[]{:S(2)}) async-start(), calls=%async_computation.52 | async-start | bytes 9437184 | tf_op jit(solution)/shard_map/reduce_scatter | solution.py:309
  976.2 1060.4 %all-reduce.26.cloned.1.call-start = ((), (), s32[]{:S(2)}) async-start(), calls=%async_computation.60 | async-start | bytes 6291456 | tf_op jit(solution)/shard_map/psum | solution.py:320
  (185 other events, 6866.7 us)
Sparse Core Ops, SparseCore 0:
  102.2 45.9 all-gather.47
  150.1 44.6 all-gather.39
  196.8 44.6 all-gather.45
  243.7 44.6 all-gather.37
  318.8 54.3 all-gather.33
  374.9 54.3 all-gather.35
  500.5 43.6 reduce-scatter.32
  546.5 43.2 reduce-scatter.34
  592.1 43.1 reduce-scatter.24
  637.6 43.1 reduce-scatter.26
  687.8 45.2 all-gather.43
  735.1 44.6 all-gather.41
  836.7 42.4 reduce-scatter.30
  881.5 43.1 reduce-scatter.28
  972.0 41.2 reduce-scatter.58
  1061.5 41.2 reduce-scatter.40
  1240.0 41.2 reduce-scatter.52
  1463.3 71.2 reduce-scatter.64
  1538.4 71.2 reduce-scatter.60
  1613.1 71.2 reduce-scatter.62
  1688.2 71.2 reduce-scatter.70
  1763.0 71.2 reduce-scatter.66
  1838.0 71.2 reduce-scatter.68
  1913.2 123.3 all-reduce.25
  (13 shorter events, 482.4 us)
where the time goes:
time: 2060 us
  waiting for transfers between devices  1320 us (64%)
  matrix products  479 us (23%)
  blocking collectives  99.5 us (5%)
  other arithmetic  98.5 us (5%)
  local copies, waits for them, and re-layouts  42 us (2%)
    reduce_scatter x3, waiting for transfers between devices, per_device(): lax.psum_scatter(local_grads[9].astype(jnp.bfloat16), 'fsdp', scatter_dim...  223 us
    reduce_scatter x3, waiting for transfers between devices, per_device(): lax.psum_scatter(local_grads[11].astype(jnp.bfloat16), 'fsdp', scatter_di...  222 us
    reduce_scatter x3, waiting for transfers between devices, per_device(): lax.psum_scatter(local_grads[3].astype(jnp.bfloat16), 'fsdp', scatter_dim...  132 us
    reduce_scatter x3, waiting for transfers between devices, per_device(): lax.psum_scatter(local_grads[2].astype(jnp.bfloat16), 'fsdp', scatter_dim...  132 us
    reduce_scatter x3, waiting for transfers between devices, per_device(): lax.psum_scatter(local_grads[4].astype(jnp.bfloat16), 'fsdp', scatter_dim...  128 us
    all_gather x3, waiting for transfers between devices, per_device(): lax.all_gather(values_local.reshape(num_rows, local_len, model_width), 's...  100 us
    dot_general x18, matrix products, back_dot(): lax.dot_general(left, right, (((1,), (1,)), ((), ())), preferred_element_...  84.1 us
    dot_general x18, matrix products, token_dot(): lax.dot_general(left, right, (((0,), (0,)), ((), ())), preferred_element_...  78.6 us
  transfers between devices with their start and end apart: 37, of which 32 were waited for; matrix products, arithmetic and copies ran while one was open for 22% of the time, Pallas kernels for 0%

commit v1 on v0

v1 whole, which is shorter than its diff:
```python
import functools

import jax
import jax.numpy as jnp
from jax import lax
from jax.experimental import pallas as pl
from jax.experimental.pallas import tpu as pltpu
from jax.sharding import PartitionSpec as P

EPS = 1e-05
NEG = -1e30
CLIP = 512
F32 = jnp.float32
BF16 = jnp.bfloat16
HIGHEST = lax.Precision.HIGHEST
MIB = 1 << 20

ERFC_P = 0.4375
ERFC_C = (
    0.24679607152938843,
    0.24772192537784576,
    0.2143726497888565,
    0.22321343421936035,
    -0.03611995279788971,
    0.3185710310935974,
    -0.2865786552429199,
    0.07202363014221191,
)


def params(vmem=56):
    return pltpu.CompilerParams(vmem_limit_bytes=vmem * MIB)


def cost(flops, nbytes, trans=0):
    return pl.CostEstimate(flops=int(flops), bytes_accessed=int(nbytes), transcendentals=int(trans))


def gelu_parts(u):
    tail = jnp.exp(u * u * -0.5)
    t = 1.0 / (1.0 + jnp.abs(u) * (ERFC_P * 0.5**0.5))
    poly = jnp.full_like(u, 0.5 * ERFC_C[-1])
    for c in ERFC_C[-2::-1]:
        poly = poly * t + 0.5 * c
    half = poly * t * tail
    cdf = jnp.where(u >= 0, 1.0 - half, half)
    return u * cdf, cdf + u * tail * 0.3989422804014327


def dot_nn(a, b):
    return lax.dot_general(a, b, (((1,), (0,)), ((), ())), preferred_element_type=F32)


def dot_nt(a, b):
    return lax.dot_general(a, b, (((1,), (1,)), ((), ())), preferred_element_type=F32)


def dot_tn(a, b):
    return lax.dot_general(a, b, (((0,), (0,)), ((), ())), preferred_element_type=F32)


def bias_kernel(qb, row_ref, out_ref):
    width = row_ref.shape[-1]
    block = jnp.broadcast_to(row_ref[0], (8, width))
    sub = lax.broadcasted_iota(jnp.int32, (8, width), 0)
    for bit in range(3):
        block = jnp.where((sub >> bit) & 1 == 1, pltpu.roll(block, 1 << bit, 1), block)
    rows = 8
    while rows < qb:
        block = jnp.concatenate([block, pltpu.roll(block, rows, 1)], axis=0)
        rows *= 2
    out_ref[0] = block[:, : out_ref.shape[-1]]


def make_bias(row, qb, kw):
    heads, width = row.shape
    return pl.pallas_call(
        functools.partial(bias_kernel, qb),
        grid=(heads,),
        in_specs=[pl.BlockSpec((1, 1, width), lambda h: (h, 0, 0))],
        out_specs=pl.BlockSpec((1, qb, kw), lambda h: (h, 0, 0)),
        out_shape=jax.ShapeDtypeStruct((heads, qb, kw), F32),
        compiler_params=params(),
        cost_estimate=cost(0, heads * qb * kw * 4),
        name="bias_table",
    )(row[:, None, :])


def diagonal_sums(block, width):
    qb, kw = block.shape
    if width > kw:
        block = jnp.concatenate([block, jnp.zeros((qb, width - kw), F32)], axis=1)
    rows = qb
    while rows > 8:
        rows //= 2
        block = block[:rows] + pltpu.roll(block[rows:], width - rows, 1)
    sub = lax.broadcasted_iota(jnp.int32, (8, width), 0)
    for bit in range(3):
        block = jnp.where((sub >> bit) & 1 == 1, pltpu.roll(block, width - (1 << bit), 1), block)
    return jnp.sum(block, axis=0, keepdims=True)


def norm_kernel(hops, *refs):
    gain = refs[hops + 1][...]
    shift = refs[hops + 2][...]
    out_ref = refs[hops + 3]
    size = refs[0].shape[1]
    for b in range(hops + 1):
        field = refs[b][0].astype(F32)
        centre = field - jnp.mean(field, axis=-1, keepdims=True)
        spread = jnp.mean(centre * centre, axis=-1, keepdims=True)
        out_ref[0, b * size : (b + 1) * size] = (centre * lax.rsqrt(spread + EPS) * gain + shift).astype(BF16)


def norm_window(blocks, gain, shift):
    rows, size, width = blocks[0].shape
    n = len(blocks)
    return pl.pallas_call(
        functools.partial(norm_kernel, n - 1),
        grid=(rows,),
        in_specs=[pl.BlockSpec((1, size, width), lambda r: (r, 0, 0))] * n
        + [pl.BlockSpec((1, width), lambda r: (0, 0))] * 2,
        out_specs=pl.BlockSpec((1, n * size, width), lambda r: (r, 0, 0)),
        out_shape=jax.ShapeDtypeStruct((rows, n * size, width), BF16),
        compiler_params=params(),
        cost_estimate=cost(10 * rows * n * size * width, rows * n * size * width * 4),
        name="norm_window",
    )(*blocks, gain, shift)


def proj_kernel(scale, x_ref, w_ref, o_ref):
    out = dot_nn(x_ref[...], w_ref[...]).astype(BF16)
    o_ref[...] = out * scale if scale != 1.0 else out


def project(x, w, block_rows, row_step, row_first, col_first, cols, bn, scale, name):
    depth = x.shape[1]
    count = x.shape[0] // (block_rows * row_step)
    return pl.pallas_call(
        functools.partial(proj_kernel, scale),
        grid=(cols // bn, count),
        in_specs=[
            pl.BlockSpec((block_rows, depth), lambda n, r: (r * row_step + row_first, 0)),
            pl.BlockSpec((depth, bn), lambda n, r: (0, n + col_first // bn)),
        ],
        out_specs=pl.BlockSpec((block_rows, bn), lambda n, r: (r, n)),
        out_shape=jax.ShapeDtypeStruct((count * block_rows, cols), BF16),
        compiler_params=params(),
        cost_estimate=cost(2 * count * block_rows * depth * cols, 2 * (x.size + depth * cols + count * block_rows * cols)),
        name=name,
    )(x, w)


def split_pair(field, even):
    zero = jnp.zeros_like(field)
    return jnp.concatenate([jnp.where(even, field, zero), jnp.where(even, zero, field)], axis=0)


def join_pair(field, even):
    half = field.shape[0] // 2
    return jnp.where(even, field[:half], field[half:])


def attn_fwd_kernel(qb, q_ref, k_ref, v_ref, bias_ref, mask_ref, o_ref, inv_ref, e_ref):
    blocks = q_ref.shape[0] // qb
    kw = bias_ref.shape[-1]
    even = lax.broadcasted_iota(jnp.int32, (qb, 128), 1) < 64
    for b in range(blocks):
        rows = slice(b * qb, (b + 1) * qb)
        keys = slice(b * qb, b * qb + kw)
        scores = dot_nt(split_pair(q_ref[rows], even), k_ref[keys])
        mask = mask_ref[0, b]
        scores = jnp.concatenate(
            [scores[:qb] + (bias_ref[0] + mask), scores[qb:] + (bias_ref[1] + mask)], axis=0
        )
        peak = jnp.max(scores, axis=-1, keepdims=True)
        expo = jnp.exp(scores - peak)
        inv = 1.0 / jnp.sum(expo, axis=-1, keepdims=True)
        expo = expo.astype(BF16)
        e_ref[0, 0, b] = expo
        inv = join_pair(jnp.broadcast_to(inv, (2 * qb, 128)), even)
        mixed = join_pair(dot_nn(expo, v_ref[keys]), even)
        inv_ref[rows] = inv
        o_ref[rows] = (mixed * inv).astype(BF16)


def attn_fwd(q, kv, bias, mask):
    heads, qb, kw = bias.shape
    pairs = heads // 2
    rows, blocks = mask.shape[:2]
    size = blocks * qb
    window = kv.shape[0] // rows
    cells = rows * blocks * heads * qb * kw
    return pl.pallas_call(
        functools.partial(attn_fwd_kernel, qb),
        grid=(rows, pairs),
        in_specs=[
            pl.BlockSpec((size, 128), lambda r, p: (r, p)),
            pl.BlockSpec((window, 128), lambda r, p: (r, p)),
            pl.BlockSpec((window, 128), lambda r, p: (r, p + pairs)),
            pl.BlockSpec((2, qb, kw), lambda r, p: (p, 0, 0)),
            pl.BlockSpec((1, blocks, qb, kw), lambda r, p: (r, 0, 0, 0)),
        ],
        out_specs=[
            pl.BlockSpec((size, 128), lambda r, p: (r, p)),
            pl.BlockSpec((size, 128), lambda r, p: (r, p)),
            pl.BlockSpec((1, 1, blocks, 2 * qb, kw), lambda r, p: (r, p, 0, 0, 0)),
        ],
        out_shape=[
            jax.ShapeDtypeStruct(q.shape, BF16),
            jax.ShapeDtypeStruct(q.shape, F32),
            jax.ShapeDtypeStruct((rows, pairs, blocks, 2 * qb, kw), BF16),
        ],
        compiler_params=params(),
        cost_estimate=cost(cells * 256, cells * 4, cells),
        name="attn_fwd",
    )(q, kv, kv, bias, mask)


def attn_bwd_kernel(qb, width, q_ref, k_ref, v_ref, e_ref, inv_ref, o_ref, g_ref, dq_ref, dk_ref, dv_ref, diag_ref, sums, dk_acc, dv_acc):
    blocks = q_ref.shape[0] // qb
    kw = e_ref.shape[-1]
    row, pair = pl.program_id(0), pl.program_id(1)
    even = lax.broadcasted_iota(jnp.int32, (qb, 128), 1) < 64
    dk_acc[...] = jnp.zeros_like(dk_acc)
    dv_acc[...] = jnp.zeros_like(dv_acc)

    @pl.when(row == 0)
    def _():
        sums[pair] = jnp.zeros(sums.shape[1:], F32)

    for b in range(blocks):
        rows = slice(b * qb, (b + 1) * qb)
        keys = slice(b * qb, b * qb + kw)
        grad = (g_ref[rows].astype(F32) * inv_ref[rows]).astype(BF16)
        weigh = grad.astype(F32) * o_ref[rows].astype(F32)
        delta = jnp.sum(split_pair(weigh, even), axis=-1, keepdims=True)
        grad = split_pair(grad, even)
        expo = e_ref[0, 0, b]
        dscore = expo.astype(F32) * (dot_nt(grad, v_ref[keys]) - delta)
        sums[pair] += dscore
        dscore = dscore.astype(BF16)
        dq_ref[rows] = (join_pair(dot_nn(dscore, k_ref[keys]), even) * 0.125).astype(BF16)
        dk_acc[:, keys] += dot_tn(split_pair(q_ref[rows], even), dscore)
        dv_acc[:, keys] += dot_tn(grad, expo)

    dk_ref[0] = dk_acc[...].astype(BF16)
    dv_ref[0] = dv_acc[...].astype(BF16)

    @pl.when(row == pl.num_programs(0) - 1)
    def _():
        diag_ref[0, 0:1] = diagonal_sums(sums[pair, :qb], width)
        diag_ref[0, 1:2] = diagonal_sums(sums[pair, qb:], width)


def attn_bwd(q, kv, e, inv, o, g, width):
    rows, pairs, blocks, qb2, kw = e.shape
    qb = qb2 // 2
    size = blocks * qb
    window = kv.shape[0] // rows
    model = q.shape[1]
    cells = e.size
    return pl.pallas_call(
        functools.partial(attn_bwd_kernel, qb, width),
        grid=(rows, pairs),
        in_specs=[
            pl.BlockSpec((size, 128), lambda r, p: (r, p)),
            pl.BlockSpec((window, 128), lambda r, p: (r, p)),
            pl.BlockSpec((window, 128), lambda r, p: (r, p + pairs)),
            pl.BlockSpec((1, 1, blocks, qb2, kw), lambda r, p: (r, p, 0, 0, 0)),
            pl.BlockSpec((size, 128), lambda r, p: (r, p)),
            pl.BlockSpec((size, 128), lambda r, p: (r, p)),
            pl.BlockSpec((size, 128), lambda r, p: (r, p)),
        ],
        out_specs=[
            pl.BlockSpec((size, 128), lambda r, p: (r, p)),
            pl.BlockSpec((1, 128, window), lambda r, p: (r, p, 0)),
            pl.BlockSpec((1, 128, window), lambda r, p: (r, p, 0)),
            pl.BlockSpec((1, 8, width), lambda r, p: (p, 0, 0)),
        ],
        out_shape=[
            jax.ShapeDtypeStruct(q.shape, BF16),
            jax.ShapeDtypeStruct((rows, model, window), BF16),
            jax.ShapeDtypeStruct((rows, model, window), BF16),
            jax.ShapeDtypeStruct((pairs, 8, width), F32),
        ],
        scratch_shapes=[pltpu.VMEM((pairs, qb2, kw), F32)] + [pltpu.VMEM((128, window), F32)] * 2,
        compiler_params=params(),
        cost_estimate=cost(cells * 512, cells * 4),
        name="attn_bwd",
    )(q, kv, kv, e, inv, o, g)


def middle_kernel(a_ref, w_ref, x_ref, gain_ref, shift_ref, mid_ref, norm_ref):
    middle = x_ref[...].astype(F32) + dot_nn(a_ref[...], w_ref[...])
    mid_ref[...] = middle
    centre = middle - jnp.mean(middle, axis=-1, keepdims=True)
    spread = jnp.mean(centre * centre, axis=-1, keepdims=True)
    norm_ref[...] = (centre * lax.rsqrt(spread + EPS) * gain_ref[...] + shift_ref[...]).astype(BF16)


def middle_block(attended, w_out, x, gain, shift, bm):
    tokens, model = x.shape
    tile = pl.BlockSpec((bm, model), lambda i: (i, 0))
    line = pl.BlockSpec((1, model), lambda i: (0, 0))
    return pl.pallas_call(
        middle_kernel,
        grid=(tokens // bm,),
        in_specs=[tile, pl.BlockSpec((model, model), lambda i: (0, 0)), tile, line, line],
        out_specs=[tile, tile],
        out_shape=[jax.ShapeDtypeStruct((tokens, model), F32), jax.ShapeDtypeStruct((tokens, model), BF16)],
        compiler_params=params(),
        cost_estimate=cost(2 * tokens * model * model, tokens * model * 10 + model * model * 2),
        name="middle_block",
    )(attended, w_out, x, gain, shift)


def ffn_kernel(bm, n2_ref, cot_ref, wu_ref, bu_ref, wd_ref, out_ref, gn_ref, gwu_ref, gwd_ref, gbu_ref, act_s, gpre_s):
    step = pl.program_id(0)
    tokens = n2_ref.shape[0]

    @pl.when(step == 0)
    def _():
        out_ref[...] = jnp.zeros_like(out_ref)
        gn_ref[...] = jnp.zeros_like(gn_ref)

    gbu_ref[...] = jnp.zeros_like(gbu_ref)

    @pl.loop(0, tokens // bm)
    def _(i):
        rows = pl.ds(pl.multiple_of(i * bm, bm), bm)
        act, slope = gelu_parts(dot_nn(n2_ref[rows, :], wu_ref[...]) + bu_ref[...])
        gpre = (dot_nt(cot_ref[rows, :], wd_ref[...]) * slope).astype(BF16)
        act = act.astype(BF16)
        act_s[rows, :] = act
        gpre_s[rows, :] = gpre
        gbu_ref[...] += jnp.sum(gpre.astype(F32), axis=0, keepdims=True)
        out_ref[rows, :] += dot_nn(act, wd_ref[...])
        gn_ref[rows, :] += dot_nt(gpre, wu_ref[...])

    gwd_ref[...] = dot_tn(act_s[...], cot_ref[...]).astype(BF16)
    gwu_ref[...] = dot_tn(n2_ref[...], gpre_s[...]).astype(BF16)


def ffn_block(n2, cot, w_up, b_up, w_down, fc, bm):
    tokens, model = n2.shape
    hidden = w_up.shape[1]
    whole = pl.BlockSpec((tokens, model), lambda j: (0, 0))
    return pl.pallas_call(
        functools.partial(ffn_kernel, bm),
        grid=(hidden // fc,),
        in_specs=[
            whole,
            whole,
            pl.BlockSpec((model, fc), lambda j: (0, j)),
            pl.BlockSpec((1, fc), lambda j: (0, j)),
            pl.BlockSpec((fc, model), lambda j: (j, 0)),
        ],
        out_specs=[
            whole,
            whole,
            pl.BlockSpec((model, fc), lambda j: (0, j)),
            pl.BlockSpec((fc, model), lambda j: (j, 0)),
            pl.BlockSpec((1, fc), lambda j: (0, j)),
        ],
        out_shape=[
            jax.ShapeDtypeStruct((tokens, model), F32),
            jax.ShapeDtypeStruct((tokens, model), F32),
            jax.ShapeDtypeStruct((model, hidden), BF16),
            jax.ShapeDtypeStruct((hidden, model), BF16),
            jax.ShapeDtypeStruct((1, hidden), F32),
        ],
        scratch_shapes=[pltpu.VMEM((tokens, fc), BF16), pltpu.VMEM((tokens, fc), BF16)],
        compiler_params=params(),
        cost_estimate=cost(12 * tokens * model * hidden, tokens * model * 12 + model * hidden * 8, 2 * tokens * hidden),
        name="ffn_block",
    )(n2, cot, w_up, b_up, w_down)


def norm_back(field, gain, e):
    centre = field - jnp.mean(field, axis=-1, keepdims=True)
    rate = lax.rsqrt(jnp.mean(centre * centre, axis=-1, keepdims=True) + EPS)
    n = centre * rate
    eg = e * gain
    grad = rate * (eg - jnp.mean(eg, axis=-1, keepdims=True) - n * jnp.mean(eg * n, axis=-1, keepdims=True))
    return grad, jnp.sum(e * n, axis=0, keepdims=True), jnp.sum(e, axis=0, keepdims=True)


def middle_back_kernel(gn_ref, mid_ref, cot_ref, w_ref, gain_ref, gm_ref, gb_ref, ga_ref, gg_ref, gs_ref):
    @pl.when(pl.program_id(0) == 0)
    def _():
        gg_ref[...] = jnp.zeros_like(gg_ref)
        gs_ref[...] = jnp.zeros_like(gs_ref)

    grad, gg, gs = norm_back(mid_ref[...], gain_ref[...], gn_ref[...])
    gg_ref[...] += gg
    gs_ref[...] += gs
    grad = cot_ref[...].astype(F32) + grad
    gm_ref[...] = grad
    branch = grad.astype(BF16)
    gb_ref[...] = branch
    ga_ref[...] = dot_nt(branch, w_ref[...]).astype(BF16)


def middle_back(gn2, middle, cot, w_out, gain, bm):
    tokens, model = middle.shape
    tile = pl.BlockSpec((bm, model), lambda i: (i, 0))
    line = pl.BlockSpec((1, model), lambda i: (0, 0))
    return pl.pallas_call(
        middle_back_kernel,
        grid=(tokens // bm,),
        in_specs=[tile, tile, tile, pl.BlockSpec((model, model), lambda i: (0, 0)), line],
        out_specs=[tile, tile, tile, line, line],
        out_shape=[
            jax.ShapeDtypeStruct((tokens, model), F32),
            jax.ShapeDtypeStruct((tokens, model), BF16),
            jax.ShapeDtypeStruct((tokens, model), BF16),
            jax.ShapeDtypeStruct((1, model), F32),
            jax.ShapeDtypeStruct((1, model), F32),
        ],
        compiler_params=params(),
        cost_estimate=cost(2 * tokens * model * model, tokens * model * 18 + model * model * 2),
        name="middle_back",
    )(gn2, middle, cot, w_out, gain)


def first_back_kernel(dn_ref, x_ref, gm_ref, gain_ref, out_ref, gg_ref, gs_ref):
    @pl.when(pl.program_id(0) == 0)
    def _():
        gg_ref[...] = jnp.zeros_like(gg_ref)
        gs_ref[...] = jnp.zeros_like(gs_ref)

    grad, gg, gs = norm_back(x_ref[...].astype(F32), gain_ref[...], dn_ref[...])
    gg_ref[...] += gg
    gs_ref[...] += gs
    out_ref[...] = (gm_ref[...] + grad).astype(BF16)


def first_back(dn, x, gm, gain, bm):
    tokens, model = x.shape
    tile = pl.BlockSpec((bm, model), lambda i: (i, 0))
    line = pl.BlockSpec((1, model), lambda i: (0, 0))
    return pl.pallas_call(
        first_back_kernel,
        grid=(tokens // bm,),
        in_specs=[tile, tile, tile, line],
        out_specs=[tile, line, line],
        out_shape=[
            jax.ShapeDtypeStruct((tokens, model), BF16),
            jax.ShapeDtypeStruct((1, model), F32),
            jax.ShapeDtypeStruct((1, model), F32),
        ],
        compiler_params=params(),
        cost_estimate=cost(20 * tokens * model, tokens * model * 12),
        name="first_back",
    )(dn, x, gm, gain)


def per_device(
    inputs,
    segment_ids,
    buckets,
    ln1_gain,
    ln1_bias,
    w_query,
    w_key,
    w_value,
    w_out,
    rel_bias,
    second_norm_gain,
    ln2_bias,
    w_up,
    b_up,
    w_down,
    b_down,
    cotangent,
):
    num_micro, num_rows, size, model = inputs.shape
    rows = num_micro * num_rows
    seq_len = segment_ids.shape[2]
    heads = rel_bias.shape[1]
    shards = lax.axis_size("fsdp")
    ranges = lax.axis_size("seq")
    num_buckets = rel_bias.shape[0] * shards
    hidden = w_up.shape[1]
    tokens = rows * size
    hops = min(-(-(CLIP - 1) // size), ranges - 1)
    halo = hops * size
    window = halo + size
    qb = min(128, size)
    blocks = size // qb
    kw = halo + qb
    width = -(-(kw + qb) // 128) * 128
    tile = min(256, tokens)

    gather = functools.partial(lax.all_gather, axis_name="fsdp", axis=0, tiled=True)
    w_qkv = gather(jnp.concatenate([w_query, w_key, w_value], axis=1))
    vectors = (ln1_gain, ln1_bias, second_norm_gain, ln2_bias, b_up, b_down, rel_bias.reshape(-1))
    packed = gather(jnp.concatenate(vectors)[None])
    parts, at = [], 0
    for v in vectors:
        parts.append(packed[:, at : at + v.size].reshape(1, -1))
        at += v.size
    gain1, shift1, gain2, shift2, bias_up, bias_down = (p.astype(F32) for p in parts[:6])
    table = parts[6].reshape(num_buckets, heads)
    out_mat = gather(w_out)
    up_mat = gather(w_up)
    down_mat = gather(w_down)

    x = inputs.reshape(rows, size, model)
    near = [x]
    for _ in range(hops):
        near.insert(0, lax.ppermute(near[0], "seq", [(i, i + 1) for i in range(ranges - 1)]))

    place = lax.axis_index("seq") * size
    column = jnp.arange(width, dtype=jnp.int32)
    gap = halo - column
    inside = (gap >= 0) & (column > 0)
    bucket_of = jnp.where(inside, jnp.flip(jnp.pad(buckets[: halo + 1], (width - halo - 1, 0))), -1)
    onehot = bucket_of[:, None] == jnp.arange(num_buckets, dtype=jnp.int32)[None]
    by_gap = dot_nn(onehot.astype(BF16), table) + jnp.where(inside, 0.0, NEG)[:, None]
    bias = make_bias(by_gap.T, qb, kw)
    segs = segment_ids.reshape(rows, seq_len)
    segs = lax.dynamic_slice_in_dim(jnp.pad(segs, ((0, 0), (halo, 0)), constant_values=-1), place, window, 1)
    mask = jnp.stack(
        [
            jnp.where(
                segs[:, halo + b * qb : halo + (b + 1) * qb, None] == segs[:, None, b * qb : b * qb + kw], 0.0, NEG
            )
            for b in range(blocks)
        ],
        axis=1,
    ).astype(F32)

    x = x.reshape(tokens, model)
    normed = norm_window(near, gain1, shift1).reshape(rows * window, model)
    kv = project(normed, w_qkv, window, 1, 0, model, 2 * model, 512, 1.0, "keys_values")
    q = project(normed, w_qkv, size, hops + 1, hops, 0, model, 512, 0.125, "queries")
    attended, inv, expo = attn_fwd(q, kv, bias, mask)
    middle, normed_two = middle_block(attended, out_mat, x, gain2, shift2, tile)

    cot = cotangent.reshape(tokens, model)
    ff_out, grad_norm2, grad_w_up, grad_w_down, grad_b_up = ffn_block(
        normed_two, cot, up_mat, bias_up, down_mat, min(512, hidden), tile
    )
    outputs = (middle + ff_out + bias_down).astype(BF16)
    grad_b_down = jnp.sum(cot.astype(F32), axis=0, keepdims=True)

    def scatter(field):
        return lax.psum_scatter(field.astype(BF16), "fsdp", scatter_dimension=0, tiled=True)

    def total(field):
        return lax.psum(field, "seq").astype(F32)

    grad_w_up = scatter(grad_w_up)
    grad_w_down = scatter(grad_w_down)

    grad_middle, grad_branch, grad_attended, grad_gain2, grad_shift2 = middle_back(
        grad_norm2, middle, cot, out_mat, gain2, tile
    )
    grad_w_out = dot_tn(attended, grad_branch).astype(BF16)
    grad_q, grad_k, grad_v, diagonal = attn_bwd(q, kv, expo, inv, attended, grad_attended, width)
    normed = normed.reshape(rows, window, model)
    normed_own = normed[:, halo:].reshape(tokens, model)
    weight_grads = [
        dot_tn(normed_own, grad_q).astype(BF16),
        jnp.einsum("rti,rft->if", normed, grad_k, preferred_element_type=F32).astype(BF16),
        jnp.einsum("rti,rft->if", normed, grad_v, preferred_element_type=F32).astype(BF16),
        grad_w_out,
    ]
    grad_attn = scatter(jnp.concatenate(weight_grads, axis=1))
    grad_norm = jnp.einsum("rft,if->rti", grad_k, w_qkv[:, model : 2 * model], preferred_element_type=F32)
    grad_norm += jnp.einsum("rft,if->rti", grad_v, w_qkv[:, 2 * model :], preferred_element_type=F32)
    grad_own = dot_nt(grad_q, w_qkv[:, :model]) + grad_norm[:, halo:].reshape(tokens, model)
    carry = None
    for hop in range(hops):
        piece = grad_norm[:, hop * size : (hop + 1) * size]
        piece = piece if carry is None else piece + carry.astype(F32)
        carry = lax.ppermute(piece.astype(BF16), "seq", [(i + 1, i) for i in range(ranges - 1)])
    if carry is not None:
        grad_own += carry.astype(F32).reshape(tokens, model)
    input_grad, grad_gain1, grad_shift1 = first_back(grad_own, x, grad_middle, gain1, tile)

    diagonal = diagonal[:, :2].reshape(heads, width)
    grad_table = lax.dot_general(onehot.astype(F32), diagonal, (((0,), (1,)), ((), ())), precision=HIGHEST)

    small = (grad_gain1, grad_shift1, grad_gain2, grad_shift2, grad_b_up, grad_b_down, grad_table)
    small = jnp.concatenate([s.reshape(shards, -1) for s in small], axis=1)
    small = lax.psum(small, ("fsdp", "seq"))
    small = lax.dynamic_slice_in_dim(small, lax.axis_index("fsdp"), 1, 0)[0]
    finals, at = [], 0
    for v in vectors:
        finals.append(small[at : at + v.size].reshape(v.shape))
        at += v.size
    finals[6] = finals[6].reshape(rel_bias.shape)

    grad_w_up = total(grad_w_up)
    grad_w_down = total(grad_w_down)
    grad_attn = total(grad_attn)
    return (
        outputs.reshape(inputs.shape),
        input_grad.reshape(inputs.shape),
        finals[0],
        finals[1],
        grad_attn[:, :model],
        grad_attn[:, model : 2 * model],
        grad_attn[:, 2 * model : 3 * model],
        grad_attn[:, 3 * model :],
        finals[6],
        finals[2],
        finals[3],
        grad_w_up,
        finals[4],
        grad_w_down,
        finals[5],
    )


def solution(mesh):
    token = P(None, "fsdp", "seq", None)
    vector = P("fsdp")
    matrix = P("fsdp", None)
    return jax.shard_map(
        per_device,
        mesh=mesh,
        in_specs=(
            token, P(None, "fsdp", None), P(), vector, vector, matrix, matrix, matrix, matrix, matrix,
            vector, vector, matrix, vector, matrix, vector, token,
        ),
        out_specs=(
            token, token, vector, vector, matrix, matrix, matrix, matrix, matrix,
            vector, vector, matrix, vector, matrix, vector,
        ),
        check_vma=False,
    )
```

time: 2060 us -> 705 us (0.34)
  waiting for transfers between devices: 1320 us -> 316 us
  matrix products: 479 us -> 41.5 us
  Pallas kernels: 0 us -> 194 us
  other arithmetic: 98.5 us -> 22.4 us
  blocking collectives: 99.5 us -> 67.9 us
    reduce_scatter x24 -> x2, waiting for transfers between devices: 991 us -> 148 us  [scatter(): lax.psum_scatter(field.astype(BF16), 'fsdp', scatter_dimension=0, tiled=T...]
    dot_general x76 -> x9, matrix products: 479 us -> 41.5 us  [the longest x1 8.54 us: per_device(): jnp.einsum('rft,if->rti', grad_v, w_qkv[:, 2 * model:], preferred_element...]
    all_gather x12 -> x4, waiting for transfers between devices: 250 us -> 27.1 us  [the longest x1 27.1 us: per_device(): down_mat = gather(w_down)]
    pallas_call x0 -> x10, Pallas kernels: none -> 194 us  [the longest x1 60 us: ffn_block(): pl.pallas_call(functools.partial(ffn_kernel, bm), grid=(hidden // fc,), i...]
    ppermute x0 -> x4, waiting for transfers between devices: none -> 70.7 us  [the longest x2 37.1 us: per_device(): lax.ppermute(piece.astype(BF16), 'seq', [(i + 1, i) for i in range(ranges...]
    all_gather x7 -> x0, blocking collectives: 61 us -> none  [the longest x1 10.3 us: per_device(): lax.all_gather(ln1_gain, 'fsdp', axis=0, tiled=True)]
    convert_element_type x37 -> x5, other arithmetic: 54.4 us -> 12.2 us  [the longest x2 4.32 us: total(): return lax.psum(field, 'seq').astype(F32)]
    reduce_sum x14 -> x1, other arithmetic: 35.9 us -> 1.68 us  [per_device(): grad_b_down = jnp.sum(cot.astype(F32), axis=0, keepdims=True)]
  transfers between devices with their start and end apart: 37 -> 12, of which waited for: 32 -> 7; matrix products, arithmetic and copies ran while one was open for 22% -> 7% of each run, Pallas kernels for 0% -> 13%
where the time goes in v1:
time: 705 us; the launch traced here: 702 us
  waiting for transfers between devices  316 us (45%)
  Pallas kernels  194 us (28%)
  blocking collectives  67.9 us (10%)
  matrix products  41.5 us (6%)
  local copies, waits for them, and re-layouts  32.1 us (5%)
  other arithmetic  22.4 us (3%)
  between operations  15.3 us (2%)
  starting transfers between devices  12.7 us (2%)
    reduce_scatter x2, waiting for transfers between devices, scatter(): lax.psum_scatter(field.astype(BF16), 'fsdp', scatter_dimension=0, tiled=T...  148 us
    pallas_call x1, Pallas kernels, ffn_block(): pl.pallas_call(functools.partial(ffn_kernel, bm), grid=(hidden // fc,), i...  60 us
    psum x1, waiting for transfers between devices, total(): return lax.psum(field, 'seq').astype(F32)  57.3 us
    psum x1, blocking collectives, per_device(): small = lax.psum(small, ('fsdp', 'seq'))  44.9 us
    ppermute x2, waiting for transfers between devices, per_device(): lax.ppermute(piece.astype(BF16), 'seq', [(i + 1, i) for i in range(ranges...  37.1 us
    pallas_call x1, Pallas kernels, attn_fwd(): pl.pallas_call(functools.partial(attn_fwd_kernel, qb), grid=(rows, pairs)...  33.7 us
    ppermute x2, waiting for transfers between devices, per_device(): lax.ppermute(near[0], 'seq', [(i, i + 1) for i in range(ranges - 1)])  33.5 us
    pallas_call x1, Pallas kernels, attn_bwd(): pl.pallas_call(functools.partial(attn_bwd_kernel, qb, width), grid=(rows,...  33.3 us
  transfers between devices with their start and end apart: 12, of which 7 were waited for; matrix products, arithmetic and copies ran while one was open for 7% of the time, Pallas kernels for 13%

profile of v1, /device:TPU:0, one launch (start us, length us, event | category | flops | bytes accessed | tf_op | source)
XLA Modules:
  0.0 701.7 jit_solution(12340107630665589083)
XLA Ops:
  16.7 33.5 %collective-permute-done.refs_1_ = bf16[3,256,1024]{2,1,0:T(8,128)(2,1)S(1)} collective-permute-done((bf16[3,256,1024]{2,1,0:T(8,128)(2,1)S(1)}, bf16[3,256,1024]{2,1,0:T(8,128)(2,1)S(1)}, u32[]{:S(2)}, u32[]{:S(2)}) %collective-permute-start) | collective-permute-done | bytes 1572896 | tf_op jit(solution)/shard_map/ppermute | solution.py:513
  57.8 23.1 %all-reduce.2 = bf16[9728]{0:T(1024)(128)(2,1)S(1)} all-reduce(bf16[9728]{0:T(1024)(128)(2,1)S(1)} %dynamic-update-slice), channel_id=2, replica_groups=mesh['fsdp'=8,'seq'=4] {'fsdp'}, use_global_device_ids=true, to_apply=%add.2 | all-reduce | flops 9728 | bytes 38912
  82.3 11.7 %bias_table.1.bias_ref = f32[16,128,640]{2,1,0:T(8,128)} custom-call(f32[16,1,768]{2,1,0:T(1,128)} %broadcast_in_dim.39.row_ref), custom_call_target="tpu_custom_call" | custom-call | bytes 5242880 | tf_op jit(solution)/shard_map/bias_table/pallas_call | solution.py:77
  98.0 6.9 norm_window.1
  107.6 6.7 queries.1.q_ref
  114.3 19.9 %keys_values.1.k_ref.v_ref = bf16[2304,2048]{1,0:T(8,128)(2,1)} custom-call(bf16[2304,1024]{1,0:T(8,128)(2,1)} %bitcast.78, bf16[1024,3072]{1,0:T(8,128)(2,1)} %all-gather.6.cloned.1.call-done.w_ref), custom_call_target="tpu_custom_call" | custom-call | flops 9663676416 | bytes 18350080 | tf_op jit(solution)/shard_map/keys_values/pallas_call | solution.py:139
  134.2 33.7 %attn_fwd.1 = (bf16[768,1024]{1,0:T(8,128)(2,1)}, f32[768,1024]{1,0:T(8,128)}, bf16[3,8,2,256,640]{4,3,2,1,0:T(8,128)(2,1)}) custom-call(bf16[768,1024]{1,0:T(8,128)(2,1)} %queries.1.q_ref, bf16[2304,2048]{1,0:T(8,128)(2,1)} %keys_values.1.k_ref.v_ref, bf16[2304,2048]{1,0:T(8,128)(2,1)} %keys_values.1.k_ref.v_ref, f32[16,128,640]{2,1,0:T(8,128)} %bias_table.1.bias_ref, ...), custom_call_target="tpu_custom_call" | custom-call | flops 2013265920 | bytes 31457280 | tf_op jit(solution)/shard_map/attn_fwd/pallas_call | solution.py:194
  167.9 6.3 middle_block.1
  174.2 27.1 %all-gather.12.cloned.1.call-done.wd_ref = bf16[4096,1024]{1,0:T(8,128)(2,1)} async-done(((bf16[512,1024]{1,0:T(8,128)(2,1)}), bf16[4096,1024]{1,0:T(8,128)(2,1)}) %all-gather.12.cloned.1.call-update) | async-done | bytes 8388624 | tf_op jit(solution)/shard_map/all_gather | solution.py:508
  201.4 60.0 %ffn_block.1 = (f32[768,1024]{1,0:T(8,128)}, f32[768,1024]{1,0:T(8,128)}, bf16[1024,4096]{1,0:T(8,128)(2,1)}, bf16[4096,1024]{1,0:T(8,128)(2,1)}, f32[1,4096]{1,0:T(1,128)}) custom-call(bf16[768,1024]{1,0:T(8,128)(2,1)} %get-tuple-element.39.n2_ref, bf16[768,1024]{1,0:T(8,128)(2,1)} %bitcast.81, bf16[1024,4096]{1,0:T(8,128)(2,1)} %all-gather.10.cloned.1.call-done.wu_ref, ...), custom_call_target="tpu_custom_call" | custom-call | flops 38654705664 | bytes 42991616 | tf_op jit(solution)/shard_map/ffn_block/pallas_call | solution.py:349
  261.4 9.1 %middle_back.1 = (f32[768,1024]{1,0:T(8,128)}, bf16[768,1024]{1,0:T(8,128)(2,1)}, bf16[768,1024]{1,0:T(8,128)(2,1)}, f32[1,1024]{1,0:T(1,128)}, f32[1,1024]{1,0:T(1,128)}) custom-call(f32[768,1024]{1,0:T(8,128)} %get-tuple-element.43.gn_ref, f32[768,1024]{1,0:T(8,128)} %get-tuple-element.38.mid_ref, bf16[768,1024]{1,0:T(8,128)(2,1)} %bitcast.82, ...), custom_call_target="tpu_custom_call" | custom-call | flops 1610612736 | bytes 16252928 | tf_op jit(solution)/shard_map/middle_back/pallas_call | solution.py:409
  274.4 33.3 %attn_bwd.1 = (bf16[768,1024]{1,0:T(8,128)(2,1)}, bf16[3,1024,768]{2,1,0:T(8,128)(2,1)}, bf16[3,1024,768]{2,1,0:T(8,128)(2,1)}, f32[8,8,768]{2,1,0:T(8,128)}) custom-call(bf16[768,1024]{1,0:T(8,128)(2,1)} %queries.1.q_ref, bf16[2304,2048]{1,0:T(8,128)(2,1)} %keys_values.1.k_ref.v_ref, bf16[2304,2048]{1,0:T(8,128)(2,1)} %keys_values.1.k_ref.v_ref, ...), custom_call_target="tpu_custom_call" | custom-call | flops 4026531840 | bytes 31457280 | tf_op jit(solution)/shard_map/attn_bwd/pallas_call | solution.py:263
  307.7 7.7 %bitcast_convert_fusion = bf16[1024,1024]{0,1:T(8,128)(2,1)S(1)} fusion(bf16[3,1024,768]{2,1,0:T(8,128)(2,1)} %get-tuple-element.47, bf16[3,768,1024]{2,1,0:T(8,128)(2,1)S(1)} %bitcast.80), kind=kOutput, calls=%fused_computation.1 | convolution fusion | flops 4832886784 | bytes 11534336 | tf_op jit(solution)/shard_map/rti,rft->if/dot_general | solution.py:568
  326.7 11.3 %copy.61 = bf16[1024,4096]{1,0:T(8,128)(2,1)} copy(bf16[1024,4096]{0,1:T(8,128)(2,1)} %pad_maximum_fusion) | data formatting | bytes 16777216
  339.3 7.7 %fusion.1 = f32[3,768,1024]{2,1,0:T(8,128)S(1)} fusion(bf16[3,1024,768]{2,1,0:T(8,128)(2,1)} %get-tuple-element.46, bf16[1024,3072]{1,0:T(8,128)(2,1)} %all-gather.6.cloned.1.call-done.w_ref), kind=kOutput, calls=%fused_computation.13 | convolution fusion | flops 4831838208 | bytes 16252928 | tf_op jit(solution)/shard_map/rft,if->rti/dot_general | solution.py:572
  347.0 8.5 %convolution_add_fusion = f32[3,768,1024]{2,1,0:T(8,128)S(1)} fusion(f32[3,768,1024]{2,1,0:T(8,128)S(1)} %fusion.1, bf16[3,1024,768]{2,1,0:T(8,128)(2,1)} %get-tuple-element.47, bf16[1024,3072]{1,0:T(8,128)(2,1)} %all-gather.6.cloned.1.call-done.w_ref), kind=kOutput, calls=%fused_computation.10 | convolution fusion | flops 4834197504 | bytes 25690112 | tf_op jit(solution)/shard_map/rft,if->rti/dot_general | solution.py:573
  357.1 37.1 %collective-permute-done.2 = bf16[3,256,1024]{2,1,0:T(8,128)(2,1)S(1)} collective-permute-done((bf16[3,256,1024]{2,1,0:T(8,128)(2,1)S(1)}, bf16[3,256,1024]{2,1,0:T(8,128)(2,1)S(1)}, u32[]{:S(2)}, u32[]{:S(2)}) %collective-permute-start.2) | collective-permute-done | bytes 1572896 | tf_op jit(solution)/shard_map/ppermute | solution.py:579
  399.1 10.3 %reduce-scatter.10.cloned.1.call-done = bf16[128,4096]{1,0:T(8,128)(2,1)} async-done(((bf16[1024,4096]{1,0:T(8,128)(2,1)}), bf16[128,4096]{1,0:T(8,128)(2,1)}) %reduce-scatter.10.cloned.1.call-update) | async-done | bytes 1048592
  411.7 72.7 %reduce-scatter.6.cloned.1.call-done = bf16[128,4096]{1,0:T(8,128)(2,1)} async-done(((bf16[1024,4096]{1,0:T(8,128)(2,1)}), bf16[128,4096]{1,0:T(8,128)(2,1)}) %reduce-scatter.6.cloned.1.call-update) | async-done | bytes 1048592 | tf_op jit(solution)/shard_map/reduce_scatter | solution.py:550
  484.4 74.8 %reduce-scatter.8.cloned.1.call-done = bf16[512,1024]{1,0:T(8,128)(2,1)} async-done(((bf16[4096,1024]{1,0:T(8,128)(2,1)}), bf16[512,1024]{1,0:T(8,128)(2,1)}) %reduce-scatter.8.cloned.1.call-update) | async-done | bytes 1048592 | tf_op jit(solution)/shard_map/reduce_scatter | solution.py:550
  567.7 5.7 convert_add_fusion.dn_ref
  573.5 6.2 first_back.1
  581.1 44.9 %psum.28 = f32[8,1216]{1,0:T(8,128)S(1)} all-reduce(f32[8,1216]{1,0:T(8,128)S(1)} %constant_dynamic-update-slice_fusion), channel_id=1, replica_groups=mesh['fsdp'=8,'seq'=4] {'fsdp','seq'}, use_global_device_ids=true, to_apply=%region_1.2 | all-reduce | flops 9728 | bytes 77824 | tf_op jit(solution)/shard_map/psum | solution.py:589
  628.0 57.3 %all-reduce.6.cloned.1.call-done = (bf16[128,4096]{0,1:T(8,128)(2,1)}, bf16[128,4096]{1,0:T(8,128)(2,1)}, bf16[512,1024]{1,0:T(8,128)(2,1)}) async-done(((bf16[128,4096]{0,1:T(8,128)(2,1)}, bf16[128,4096]{1,0:T(8,128)(2,1)}, bf16[512,1024]{1,0:T(8,128)(2,1)}), (bf16[128,4096]{0,1:T(8,128)(2,1)}, bf16[128,4096]{1,0:T(8,128)(2,1)}, bf16[512,1024]{1,0:T(8,128)(2,1)})) %all-reduce.6.cloned.1.call-update) | async-done | bytes 3145744 | tf_op jit(solution)/shard_map/psum | solution.py:553
  (145 shorter events, 70.8 us)
Async XLA Ops:
  7.2 48.7 %copy-start.24 = (u32[32]{0:T(128)S(1)}, u32[32]{0:T(128)}, u32[]{:S(2)}) copy-start(u32[32]{0:T(128)} %constant.36) | copy-start | bytes 388
  7.2 47.6 %copy-start.15 = (bf16[128]{0:T(256)(128)(2,1)S(1)}, bf16[128]{0:T(256)(128)(2,1)}, u32[]{:S(2)}) copy-start(bf16[128]{0:T(256)(128)(2,1)} %param.20) | copy-start | bytes 772
  7.2 47.8 %copy-start.16 = (bf16[128]{0:T(256)(128)(2,1)S(1)}, bf16[128]{0:T(256)(128)(2,1)}, u32[]{:S(2)}) copy-start(bf16[128]{0:T(256)(128)(2,1)} %param.21) | copy-start | bytes 772
  7.2 48.0 %copy-start.17 = (bf16[128]{0:T(256)(128)(2,1)S(1)}, bf16[128]{0:T(256)(128)(2,1)}, u32[]{:S(2)}) copy-start(bf16[128]{0:T(256)(128)(2,1)} %param.27) | copy-start | bytes 772
  7.2 48.2 %copy-start.18 = (bf16[128]{0:T(256)(128)(2,1)S(1)}, bf16[128]{0:T(256)(128)(2,1)}, u32[]{:S(2)}) copy-start(bf16[128]{0:T(256)(128)(2,1)} %param.28) | copy-start | bytes 772
  7.3 48.4 %copy-start.14 = (bf16[512]{0:T(512)(128)(2,1)S(1)}, bf16[512]{0:T(512)(128)(2,1)}, u32[]{:S(2)}) copy-start(bf16[512]{0:T(512)(128)(2,1)} %param.30) | copy-start | bytes 3076
  7.3 49.9 %copy-start.19 = (bf16[128]{0:T(256)(128)(2,1)S(1)}, bf16[128]{0:T(256)(128)(2,1)}, u32[]{:S(2)}) copy-start(bf16[128]{0:T(256)(128)(2,1)} %param.32) | copy-start | bytes 772
  7.3 73.8 %copy-start.9 = (s32[1024]{0:T(1024)S(1)}, s32[1024]{0:T(1024)}, u32[]{:S(2)}) copy-start(s32[1024]{0:T(1024)} %param.19) | copy-start | bytes 12292
  7.3 100.3 %all-gather.6.cloned.1.call-start = ((), (), s32[]{:S(2)}) async-start(), calls=%async_computation.3 | async-start | bytes 7077888 | tf_op jit(solution)/shard_map/all_gather | solution.py:497
  9.5 158.4 %all-gather.8.cloned.1.call-start = ((), (), s32[]{:S(2)}) async-start(), calls=%async_computation.4 | async-start | bytes 2359296 | tf_op jit(solution)/shard_map/all_gather | solution.py:506
  10.2 164.0 %all-gather.10.cloned.1.call-start = ((), (), s32[]{:S(2)}) async-start(), calls=%async_computation.5 | async-start | bytes 9437184 | tf_op jit(solution)/shard_map/all_gather | solution.py:507
  11.0 83.0 %copy-start.8 = (s32[3,1,1024]{2,1,0:T(1,128)S(1)}, s32[3,1,1024]{2,1,0:T(1,128)}, u32[]{:S(2)}) copy-start(s32[3,1,1024]{2,1,0:T(1,128)} %param.18) | copy-start | bytes 36868
  11.0 190.4 %all-gather.12.cloned.1.call-start = ((), (), s32[]{:S(2)}) async-start(), calls=%async_computation.6 | async-start | bytes 9437184 | tf_op jit(solution)/shard_map/all_gather | solution.py:508
  11.6 397.8 %reduce-scatter.10.cloned.1.call-start = ((), (), s32[]{:S(2)}) async-start(), calls=%async_computation.9 | async-start | bytes 9437184
  11.6 38.6 %collective-permute-start = (bf16[3,256,1024]{2,1,0:T(8,128)(2,1)S(1)}, bf16[3,256,1024]{2,1,0:T(8,128)(2,1)S(1)}, u32[]{:S(2)}, u32[]{:S(2)}) collective-permute-start(bf16[3,256,1024]{2,1,0:T(8,128)(2,1)S(1)} %bitcast.86), channel_id=1, source_target_pairs={{0,1},{1,2},{2,3},{4,5},{5,6},{6,7},{8,9},{9,10},{10,11},{12,13},{... | collective-permute-start | bytes 4718600 | tf_op jit(solution)/shard_map/ppermute | solution.py:513
  50.2 46.7 %collective-permute-start.1 = (bf16[3,256,1024]{2,1,0:T(8,128)(2,1)S(1)}, bf16[3,256,1024]{2,1,0:T(8,128)(2,1)S(1)}, u32[]{:S(2)}, u32[]{:S(2)}) collective-permute-start(bf16[3,256,1024]{2,1,0:T(8,128)(2,1)S(1)} %collective-permute-done.refs_1_), channel_id=1, source_target_pairs={{0,1},{1,2},{2,3},{4,5},{5,6},{6,7},{8,9},{9,10},{10,11},{12,13},{... | collective-permute-start | bytes 4718600 | tf_op jit(solution)/shard_map/ppermute | solution.py:513
  338.0 146.4 %reduce-scatter.6.cloned.1.call-start = ((), (), s32[]{:S(2)}) async-start(), calls=%async_computation.7 | async-start | bytes 9437184 | tf_op jit(solution)/shard_map/reduce_scatter | solution.py:550
  338.5 220.7 %reduce-scatter.8.cloned.1.call-start = ((), (), s32[]{:S(2)}) async-start(), calls=%async_computation.8 | async-start | bytes 9437184 | tf_op jit(solution)/shard_map/reduce_scatter | solution.py:550
  339.3 345.9 %all-reduce.6.cloned.1.call-start = ((), (), s32[]{:S(2)}) async-start(), calls=%async_computation.10 | async-start | bytes 6291456 | tf_op jit(solution)/shard_map/psum | solution.py:553
  355.8 38.4 %collective-permute-start.2 = (bf16[3,256,1024]{2,1,0:T(8,128)(2,1)S(1)}, bf16[3,256,1024]{2,1,0:T(8,128)(2,1)S(1)}, u32[]{:S(2)}, u32[]{:S(2)}) collective-permute-start(bf16[3,256,1024]{2,1,0:T(8,128)(2,1)S(1)} %slice.186), channel_id=1, source_target_pairs={{1,0},{2,1},{3,2},{5,4},{6,5},{7,6},{9,8},{10,9},{11,10},{13,12},{... | collective-permute-start | bytes 4718600 | tf_op jit(solution)/shard_map/ppermute | solution.py:579
  397.6 163.9 %copy-start.7 = (f32[1,4096]{1,0:T(1,128)S(1)}, f32[1,4096]{1,0:T(1,128)}, u32[]{:S(2)}) copy-start(f32[1,4096]{1,0:T(1,128)} %get-tuple-element.54) | copy-start | bytes 49156
  397.6 165.5 %copy-start.11 = (s32[768]{0:T(1024)S(1)}, s32[768]{0:T(1024)}, u32[]{:S(2)}) copy-start(s32[768]{0:T(1024)} %copy-done.10) | copy-start | bytes 9220
  397.6 166.1 %copy-start = (f32[768,1024]{1,0:T(8,128)S(1)}, f32[768,1024]{1,0:T(8,128)}, u32[]{:S(2)}) copy-start(f32[768,1024]{1,0:T(8,128)} %get-tuple-element.38.mid_ref) | copy-start | bytes 9437188
  397.6 170.1 %collective-permute-start.3 = (bf16[3,256,1024]{2,1,0:T(8,128)(2,1)}, bf16[3,256,1024]{2,1,0:T(8,128)(2,1)}, u32[]{:S(2)}, u32[]{:S(2)}) collective-permute-start(bf16[3,256,1024]{2,1,0:T(8,128)(2,1)} %get-tuple-element.107), channel_id=1, source_target_pairs={{1,0},{2,1},{3,2},{5,4},{6,5},{7,6},{9,8},{10,9},{11,10},{13,12},{... | collective-permute-start | bytes 4718600 | tf_op jit(solution)/shard_map/ppermute | solution.py:579
  (15 other events, 216.4 us)
Sparse Core Ops, SparseCore 0:
  10.6 48.2 all-gather.5
  60.7 28.0 all-gather.7
  90.7 54.4 all-gather.9
  146.9 54.4 all-gather.11
  338.1 71.2 reduce-scatter.9
  413.1 71.2 reduce-scatter.5
  487.9 71.2 reduce-scatter.7
  562.5 122.6 all-reduce.5

commit v2 on v1

v2 whole, which is shorter than its diff:
```python
import functools

import jax
import jax.numpy as jnp
from jax import lax
from jax.experimental import pallas as pl
from jax.experimental.pallas import tpu as pltpu
from jax.sharding import PartitionSpec as P

EPS = 1e-05
NEG = -1e30
CLIP = 512
F32 = jnp.float32
BF16 = jnp.bfloat16
HIGHEST = lax.Precision.HIGHEST
MIB = 1 << 20
COST = 30.0
LIGHT = 1.0

ERFC_P = 0.4375
ERFC_C = (
    0.24679607152938843,
    0.24772192537784576,
    0.2143726497888565,
    0.22321343421936035,
    -0.03611995279788971,
    0.3185710310935974,
    -0.2865786552429199,
    0.07202363014221191,
)


def params(vmem=56):
    return pltpu.CompilerParams(vmem_limit_bytes=vmem * MIB)


def cost(flops, nbytes, weight=COST):
    return pl.CostEstimate(flops=int(flops * weight), bytes_accessed=int(nbytes * weight), transcendentals=0)


def gelu_parts(u):
    tail = jnp.exp(u * u * -0.5)
    t = 1.0 / (1.0 + jnp.abs(u) * (ERFC_P * 0.5**0.5))
    poly = jnp.full_like(u, 0.5 * ERFC_C[-1])
    for c in ERFC_C[-2::-1]:
        poly = poly * t + 0.5 * c
    half = poly * t * tail
    cdf = jnp.where(u >= 0, 1.0 - half, half)
    return u * cdf, cdf + u * tail * 0.3989422804014327


def dot_nn(a, b):
    return lax.dot_general(a, b, (((1,), (0,)), ((), ())), preferred_element_type=F32)


def dot_nt(a, b):
    return lax.dot_general(a, b, (((1,), (1,)), ((), ())), preferred_element_type=F32)


def dot_tn(a, b):
    return lax.dot_general(a, b, (((0,), (0,)), ((), ())), preferred_element_type=F32)


def bias_kernel(qb, row_ref, out_ref):
    width = row_ref.shape[-1]
    block = jnp.broadcast_to(row_ref[0], (8, width))
    sub = lax.broadcasted_iota(jnp.int32, (8, width), 0)
    for bit in range(3):
        block = jnp.where((sub >> bit) & 1 == 1, pltpu.roll(block, 1 << bit, 1), block)
    rows = 8
    while rows < qb:
        block = jnp.concatenate([block, pltpu.roll(block, rows, 1)], axis=0)
        rows *= 2
    out_ref[0] = block[:, : out_ref.shape[-1]]


def make_bias(row, qb, kw):
    heads, width = row.shape
    return pl.pallas_call(
        functools.partial(bias_kernel, qb),
        grid=(heads,),
        in_specs=[pl.BlockSpec((1, 1, width), lambda h: (h, 0, 0))],
        out_specs=pl.BlockSpec((1, qb, kw), lambda h: (h, 0, 0)),
        out_shape=jax.ShapeDtypeStruct((heads, qb, kw), F32),
        compiler_params=params(),
        cost_estimate=cost(0, heads * qb * kw * 4),
        name="bias_table",
    )(row[:, None, :])


def diagonal_sums(block, width):
    qb, kw = block.shape
    if width > kw:
        block = jnp.concatenate([block, jnp.zeros((qb, width - kw), F32)], axis=1)
    rows = qb
    while rows > 8:
        rows //= 2
        block = block[:rows] + pltpu.roll(block[rows:], width - rows, 1)
    sub = lax.broadcasted_iota(jnp.int32, (8, width), 0)
    for bit in range(3):
        block = jnp.where((sub >> bit) & 1 == 1, pltpu.roll(block, width - (1 << bit), 1), block)
    return jnp.sum(block, axis=0, keepdims=True)


def norm_kernel(order_ref, x_ref, gain_ref, shift_ref, out_ref, turned_ref, scratch):
    shards = order_ref.shape[0]
    part = scratch.shape[0] // shards
    field = x_ref[0].astype(F32)
    centre = field - jnp.mean(field, axis=-1, keepdims=True)
    spread = jnp.mean(centre * centre, axis=-1, keepdims=True)
    normed = (centre * lax.rsqrt(spread + EPS) * gain_ref[...] + shift_ref[...]).astype(BF16)
    out_ref[0] = normed
    scratch[...] = normed.T
    for t in range(shards):
        source = pl.ds(pl.multiple_of(order_ref[t] * part, part), part)
        turned_ref[0, t * part : (t + 1) * part] = scratch[source, :]


def norm_block(order, x, gain, shift):
    rows, size, width = x.shape
    line = pl.BlockSpec((1, width), lambda r, o: (0, 0))
    tile = pl.BlockSpec((1, size, width), lambda r, o: (r, 0, 0))
    normed, turned = pl.pallas_call(
        norm_kernel,
        grid_spec=pltpu.PrefetchScalarGridSpec(
            num_scalar_prefetch=1,
            grid=(rows,),
            in_specs=[tile, line, line],
            out_specs=[tile, pl.BlockSpec((1, width, size), lambda r, o: (r, 0, 0))],
            scratch_shapes=[pltpu.VMEM((width, size), BF16)],
        ),
        out_shape=[
            jax.ShapeDtypeStruct((rows, size, width), BF16),
            jax.ShapeDtypeStruct((rows, width, size), BF16),
        ],
        compiler_params=params(),
        cost_estimate=cost(10 * rows * size * width, rows * size * width * 6),
        name="norm_block",
    )(order, x, gain, shift)
    return normed.reshape(rows * size, width), turned


def proj_kernel(scaled, x_ref, w_ref, o_ref):
    out = dot_nn(x_ref[...], w_ref[...]).astype(BF16)
    o_ref[...] = jnp.where(pl.program_id(0) < scaled, out * 0.125, out) if scaled else out


def project(x, w, first, cols, scaled, bn=256):
    tokens, model = x.shape
    return pl.pallas_call(
        functools.partial(proj_kernel, scaled // bn),
        grid=(cols // bn,),
        in_specs=[
            pl.BlockSpec((tokens, model), lambda n: (0, 0), pipeline_mode=pl.Buffered(1)),
            pl.BlockSpec((model, bn), lambda n: (0, n + first // bn)),
        ],
        out_specs=pl.BlockSpec((tokens, bn), lambda n: (0, n)),
        out_shape=jax.ShapeDtypeStruct((tokens, cols), BF16),
        compiler_params=params(),
        cost_estimate=cost(2 * tokens * model * cols, 2 * (tokens * model + model * cols + tokens * cols)),
        name="project",
    )(x, w)


def split_pair(field, even):
    zero = jnp.zeros_like(field)
    return jnp.concatenate([jnp.where(even, field, zero), jnp.where(even, zero, field)], axis=0)


def join_pair(field, even):
    half = field.shape[0] // 2
    return jnp.where(even, field[:half], field[half:])


def attn_fwd_kernel(qb, n, q_ref, *refs):
    bias_ref, mask_ref, o_ref, inv_ref, e_ref = refs[2 * n :]
    k = jnp.concatenate([r[...] for r in refs[:n]], axis=0)
    v = jnp.concatenate([r[...] for r in refs[n : 2 * n]], axis=0)
    blocks = q_ref.shape[0] // qb
    kw = bias_ref.shape[-1]
    even = lax.broadcasted_iota(jnp.int32, (qb, 128), 1) < 64
    for b in range(blocks):
        rows = slice(b * qb, (b + 1) * qb)
        keys = slice(b * qb, b * qb + kw)
        scores = dot_nt(split_pair(q_ref[rows], even), k[keys])
        mask = mask_ref[0, b]
        scores = jnp.concatenate(
            [scores[:qb] + (bias_ref[0] + mask), scores[qb:] + (bias_ref[1] + mask)], axis=0
        )
        peak = jnp.max(scores, axis=-1, keepdims=True)
        expo = jnp.exp(scores - peak)
        inv = 1.0 / jnp.sum(expo, axis=-1, keepdims=True)
        expo = expo.astype(BF16)
        e_ref[0, 0, b] = expo
        inv = join_pair(jnp.broadcast_to(inv, (2 * qb, 128)), even)
        mixed = join_pair(dot_nn(expo, v[keys]), even)
        inv_ref[rows] = inv
        o_ref[rows] = (mixed * inv).astype(BF16)


def key_specs(n, size, pairs, first):
    near = [pl.BlockSpec((size, 128), lambda r, p: (r, p))] * (n - 1)
    far = [pl.BlockSpec((size, 128), lambda r, p: (r, p + pairs))] * (n - 1)
    return [
        *near,
        pl.BlockSpec((size, 128), lambda r, p: (r, p + first)),
        *far,
        pl.BlockSpec((size, 128), lambda r, p: (r, p + pairs + first)),
    ]


def attn_fwd(kvs, bias, mask):
    heads, qb, kw = bias.shape
    pairs = heads // 2
    rows, blocks = mask.shape[:2]
    size = blocks * qb
    n = len(kvs)
    q_shape = (rows * size, heads * 64)
    cells = rows * blocks * heads * qb * kw
    return pl.pallas_call(
        functools.partial(attn_fwd_kernel, qb, n),
        grid=(rows, pairs),
        in_specs=[
            pl.BlockSpec((size, 128), lambda r, p: (r, p)),
            *key_specs(n, size, pairs, pairs),
            pl.BlockSpec((2, qb, kw), lambda r, p: (p, 0, 0)),
            pl.BlockSpec((1, blocks, qb, kw), lambda r, p: (r, 0, 0, 0)),
        ],
        out_specs=[
            pl.BlockSpec((size, 128), lambda r, p: (r, p)),
            pl.BlockSpec((size, 128), lambda r, p: (r, p)),
            pl.BlockSpec((1, 1, blocks, 2 * qb, kw), lambda r, p: (r, p, 0, 0, 0)),
        ],
        out_shape=[
            jax.ShapeDtypeStruct(q_shape, BF16),
            jax.ShapeDtypeStruct(q_shape, F32),
            jax.ShapeDtypeStruct((rows, pairs, blocks, 2 * qb, kw), BF16),
        ],
        compiler_params=params(),
        cost_estimate=cost(cells * 256, cells * 4),
        name="attn_fwd",
    )(kvs[-1], *kvs, *kvs, bias, mask)


def attn_bwd_kernel(qb, width, n, q_ref, *refs):
    e_ref, inv_ref, o_ref, g_ref, dq_ref, dk_ref, dv_ref, diag_ref, sums, dk_acc, dv_acc = refs[2 * n :]
    k = jnp.concatenate([r[...] for r in refs[:n]], axis=0)
    v = jnp.concatenate([r[...] for r in refs[n : 2 * n]], axis=0)
    blocks = q_ref.shape[0] // qb
    kw = e_ref.shape[-1]
    row, pair = pl.program_id(0), pl.program_id(1)
    even = lax.broadcasted_iota(jnp.int32, (qb, 128), 1) < 64
    dk_acc[...] = jnp.zeros_like(dk_acc)
    dv_acc[...] = jnp.zeros_like(dv_acc)

    @pl.when(row == 0)
    def _():
        sums[pair] = jnp.zeros(sums.shape[1:], F32)

    for b in range(blocks):
        rows = slice(b * qb, (b + 1) * qb)
        keys = slice(b * qb, b * qb + kw)
        grad = (g_ref[rows].astype(F32) * inv_ref[rows]).astype(BF16)
        weigh = grad.astype(F32) * o_ref[rows].astype(F32)
        delta = jnp.sum(split_pair(weigh, even), axis=-1, keepdims=True)
        grad = split_pair(grad, even)
        expo = e_ref[0, 0, b]
        dscore = expo.astype(F32) * (dot_nt(grad, v[keys]) - delta)
        sums[pair] += dscore
        dscore = dscore.astype(BF16)
        dq_ref[rows] = (join_pair(dot_nn(dscore, k[keys]), even) * 0.125).astype(BF16)
        dk_acc[:, keys] += dot_tn(split_pair(q_ref[rows], even), dscore)
        dv_acc[:, keys] += dot_tn(grad, expo)

    dk_ref[0] = dk_acc[...].astype(BF16)
    dv_ref[0] = dv_acc[...].astype(BF16)

    @pl.when(row == pl.num_programs(0) - 1)
    def _():
        diag_ref[0, 0:1] = diagonal_sums(sums[pair, :qb], width)
        diag_ref[0, 1:2] = diagonal_sums(sums[pair, qb:], width)


def attn_bwd(kvs, e, inv, o, g, width):
    rows, pairs, blocks, qb2, kw = e.shape
    qb = qb2 // 2
    size = blocks * qb
    n = len(kvs)
    window = n * size
    model = o.shape[1]
    cells = e.size
    return pl.pallas_call(
        functools.partial(attn_bwd_kernel, qb, width, n),
        grid=(rows, pairs),
        in_specs=[
            pl.BlockSpec((size, 128), lambda r, p: (r, p)),
            *key_specs(n, size, pairs, pairs),
            pl.BlockSpec((1, 1, blocks, qb2, kw), lambda r, p: (r, p, 0, 0, 0)),
            pl.BlockSpec((size, 128), lambda r, p: (r, p)),
            pl.BlockSpec((size, 128), lambda r, p: (r, p)),
            pl.BlockSpec((size, 128), lambda r, p: (r, p)),
        ],
        out_specs=[
            pl.BlockSpec((size, 128), lambda r, p: (r, p)),
            pl.BlockSpec((1, 128, window), lambda r, p: (r, p, 0)),
            pl.BlockSpec((1, 128, window), lambda r, p: (r, p, 0)),
            pl.BlockSpec((1, 8, width), lambda r, p: (p, 0, 0)),
        ],
        out_shape=[
            jax.ShapeDtypeStruct(o.shape, BF16),
            jax.ShapeDtypeStruct((rows, model, window), BF16),
            jax.ShapeDtypeStruct((rows, model, window), BF16),
            jax.ShapeDtypeStruct((pairs, 8, width), F32),
        ],
        scratch_shapes=[pltpu.VMEM((pairs, qb2, kw), F32)] + [pltpu.VMEM((128, window), F32)] * 2,
        compiler_params=params(),
        cost_estimate=cost(cells * 512, cells * 4),
        name="attn_bwd",
    )(kvs[-1], *kvs, *kvs, e, inv, o, g)


def middle_kernel(order_ref, a_ref, w_ref, x_ref, gain_ref, shift_ref, mid_ref, norm_ref, turned_ref, mixed_ref, scratch):
    shards = order_ref.shape[0]
    part = scratch.shape[0] // shards

    def turn(field, out_ref):
        scratch[...] = field.T
        for t in range(shards):
            out_ref[t * part : (t + 1) * part] = scratch[pl.ds(pl.multiple_of(order_ref[t] * part, part), part), :]

    middle = x_ref[...].astype(F32) + dot_nn(a_ref[...], w_ref[...])
    mid_ref[...] = middle
    centre = middle - jnp.mean(middle, axis=-1, keepdims=True)
    spread = jnp.mean(centre * centre, axis=-1, keepdims=True)
    normed = (centre * lax.rsqrt(spread + EPS) * gain_ref[...] + shift_ref[...]).astype(BF16)
    norm_ref[...] = normed
    turn(normed, turned_ref)
    turn(a_ref[...], mixed_ref)


def middle_block(order, attended, w_attn, x, gain, shift, bm):
    tokens, model = x.shape
    tile = pl.BlockSpec((bm, model), lambda i, o: (i, 0))
    turned = pl.BlockSpec((model, bm), lambda i, o: (0, i))
    line = pl.BlockSpec((1, model), lambda i, o: (0, 0))
    return pl.pallas_call(
        middle_kernel,
        grid_spec=pltpu.PrefetchScalarGridSpec(
            num_scalar_prefetch=1,
            grid=(tokens // bm,),
            in_specs=[tile, pl.BlockSpec((model, model), lambda i, o: (0, w_attn.shape[1] // model - 1)), tile, line, line],
            out_specs=[tile, tile, turned, turned],
            scratch_shapes=[pltpu.VMEM((model, bm), BF16)],
        ),
        out_shape=[
            jax.ShapeDtypeStruct((tokens, model), F32),
            jax.ShapeDtypeStruct((tokens, model), BF16),
            jax.ShapeDtypeStruct((model, tokens), BF16),
            jax.ShapeDtypeStruct((model, tokens), BF16),
        ],
        compiler_params=params(),
        cost_estimate=cost(2 * tokens * model * model, tokens * model * 14 + model * model * 2),
        name="middle_block",
    )(order, attended, w_attn, x, gain, shift)


def ffn_kernel(
    bm, first, last, chip_ref, n2_ref, n2t_ref, cot_ref, acc_ref, gin_ref, wu_ref, bu_ref, d0_ref, d1_ref, bd_ref, *refs
):
    out_ref, gn_ref, us_ref, uk_ref, ds_ref, dk_ref, gbu_ref, sums, wd, act_s, gpre_s, spare = refs[-12:]
    step = pl.program_id(0)
    tokens = n2_ref.shape[0]
    part = d0_ref.shape[0] // 2
    core = chip_ref[chip_ref.shape[0] - 1]

    @pl.when(step == 0)
    def _():
        if first:
            sums[...] = acc_ref[...] + bd_ref[...]
            gn_ref[...] = jnp.zeros_like(gn_ref)
        else:
            sums[...] = acc_ref[...]
            gn_ref[...] = gin_ref[...]

    for c in range(2):
        for i, d_ref in enumerate((d0_ref, d1_ref)):
            wd[(2 * c + i) * part : (2 * c + i + 1) * part] = d_ref[c * part : (c + 1) * part]
    gbu_ref[...] = jnp.zeros_like(gbu_ref)

    def tile(rows):
        act, slope = gelu_parts(dot_nn(n2_ref[rows, :], wu_ref[...]) + bu_ref[...])
        gpre = (dot_nt(cot_ref[rows, :], wd[...]) * slope).astype(BF16)
        act = act.astype(BF16)
        act_s[rows, :] = act
        gpre_s[rows, :] = gpre
        gbu_ref[...] += jnp.sum(gpre.astype(F32), axis=0, keepdims=True)
        sums[rows, :] += dot_nn(act, wd[...])
        gn_ref[rows, :] += dot_nt(gpre, wu_ref[...])

    for i in range(tokens // bm):
        tile(slice(i * bm, (i + 1) * bm))

    spare[...] = dot_tn(act_s[...], cot_ref[...]).astype(BF16).reshape(spare.shape)
    ds_ref[0] = spare[1 - core]
    dk_ref[0] = spare[core]
    half = n2t_ref.shape[0] // 2
    us_ref[...] = dot_nn(n2t_ref[:half], gpre_s[...]).astype(BF16).reshape(us_ref.shape)
    uk_ref[...] = dot_nn(n2t_ref[half:], gpre_s[...]).astype(BF16).reshape(uk_ref.shape)

    @pl.when(step == pl.num_programs(0) - 1)
    def _():
        out_ref[...] = sums[...].astype(out_ref.dtype)


def ffn_block(chips, n2, n2t, cot, acc, gin, w, b_up, b_down, begin, end, first, last, bm, grads=()):
    tokens, model = n2.shape
    pairs = chips.shape[0] - 1
    shards = 2 * pairs
    part = model // shards
    hidden = b_up.shape[1]
    fc = hidden // pairs
    once = pl.Buffered(1)
    whole = pl.BlockSpec((tokens, model), lambda j, o: (0, 0), pipeline_mode=once)
    by_col = pl.BlockSpec((pairs, part, fc), lambda j, o: (0, 0, o[j + begin]))
    by_row = pl.BlockSpec((1, fc // 2, model), lambda j, o: (j + begin, 0, 0))
    return pl.pallas_call(
        functools.partial(ffn_kernel, bm, first, last),
        grid_spec=pltpu.PrefetchScalarGridSpec(
            num_scalar_prefetch=1,
            grid=(end - begin,),
            in_specs=[
                whole,
                pl.BlockSpec((model, tokens), lambda j, o: (0, 0), pipeline_mode=once),
                whole,
                whole,
                pl.BlockSpec((8, model), lambda j, o: (0, 0)) if first else whole,
                pl.BlockSpec((model, fc), lambda j, o: (0, o[j + begin])),
                pl.BlockSpec((1, fc), lambda j, o: (0, o[j + begin])),
                pl.BlockSpec((2 * part, model), lambda j, o: (o[j + begin], hidden // model)),
                pl.BlockSpec((2 * part, model), lambda j, o: (o[j + begin], hidden // model + 1)),
                pl.BlockSpec((1, model), lambda j, o: (0, 0)),
                *[pl.BlockSpec(memory_space=pl.ANY)] * len(grads),
            ],
            out_specs=[
                pl.BlockSpec((tokens, model), lambda j, o: (0, 0)),
                pl.BlockSpec((tokens, model), lambda j, o: (0, 0)),
                by_col,
                by_col,
                by_row,
                by_row,
                pl.BlockSpec((1, fc), lambda j, o: (0, o[j + begin])),
            ],
            scratch_shapes=[
                pltpu.VMEM((tokens, model), F32),
                pltpu.VMEM((fc, model), BF16),
                pltpu.VMEM((tokens, fc), BF16),
                pltpu.VMEM((tokens, fc), BF16),
                pltpu.VMEM((2, fc // 2, model), BF16),
            ],
        ),
        out_shape=[
            jax.ShapeDtypeStruct((tokens, model), BF16 if last else F32),
            jax.ShapeDtypeStruct((tokens, model), F32),
            jax.ShapeDtypeStruct((pairs, part, hidden), BF16),
            jax.ShapeDtypeStruct((pairs, part, hidden), BF16),
            jax.ShapeDtypeStruct((pairs, fc // 2, model), BF16),
            jax.ShapeDtypeStruct((pairs, fc // 2, model), BF16),
            jax.ShapeDtypeStruct((1, hidden), F32),
        ],
        input_output_aliases={11 + i: 2 + i for i in range(len(grads))},
        compiler_params=params(),
        cost_estimate=cost(
            12 * tokens * model * fc * (end - begin),
            tokens * model * 20 + model * fc * (end - begin) * 8,
        ),
        name="ffn_block",
    )(chips, n2, n2t, cot, acc, gin, w, b_up, w, w, b_down, *grads)


def norm_back(field, gain, e):
    centre = field - jnp.mean(field, axis=-1, keepdims=True)
    rate = lax.rsqrt(jnp.mean(centre * centre, axis=-1, keepdims=True) + EPS)
    n = centre * rate
    eg = e * gain
    grad = rate * (eg - jnp.mean(eg, axis=-1, keepdims=True) - n * jnp.mean(eg * n, axis=-1, keepdims=True))
    return grad, jnp.sum(e * n, axis=0, keepdims=True), jnp.sum(e, axis=0, keepdims=True)


def middle_back_kernel(gn_ref, mid_ref, cot_ref, w_ref, gain_ref, gm_ref, gb_ref, ga_ref, gg_ref, gs_ref):
    @pl.when(pl.program_id(0) == 0)
    def _():
        gg_ref[...] = jnp.zeros_like(gg_ref)
        gs_ref[...] = jnp.zeros_like(gs_ref)

    grad, gg, gs = norm_back(mid_ref[...], gain_ref[...], gn_ref[...])
    gg_ref[...] += gg
    gs_ref[...] += gs
    grad = cot_ref[...].astype(F32) + grad
    gm_ref[...] = grad
    branch = grad.astype(BF16)
    gb_ref[...] = branch
    ga_ref[...] = dot_nt(branch, w_ref[...]).astype(BF16)


def middle_back(gn2, middle, cot, w_attn, gain, bm):
    tokens, model = middle.shape
    tile = pl.BlockSpec((bm, model), lambda i: (i, 0))
    line = pl.BlockSpec((1, model), lambda i: (0, 0))
    return pl.pallas_call(
        middle_back_kernel,
        grid=(tokens // bm,),
        in_specs=[tile, tile, tile, pl.BlockSpec((model, model), lambda i: (0, w_attn.shape[1] // model - 1)), line],
        out_specs=[tile, tile, tile, line, line],
        out_shape=[
            jax.ShapeDtypeStruct((tokens, model), F32),
            jax.ShapeDtypeStruct((tokens, model), BF16),
            jax.ShapeDtypeStruct((tokens, model), BF16),
            jax.ShapeDtypeStruct((1, model), F32),
            jax.ShapeDtypeStruct((1, model), F32),
        ],
        compiler_params=params(),
        cost_estimate=cost(2 * tokens * model * model, tokens * model * 18 + model * model * 2),
        name="middle_back",
    )(gn2, middle, cot, w_attn, gain)


def attn_weights_kernel(n, *refs):
    turned = refs[:n]
    at_ref, dq_ref, dk_ref, dv_ref, gb_ref, first_ref, last_ref = refs[n:]
    model = gb_ref.shape[1]
    rows, _, size = turned[0].shape
    half, part = first_ref.shape[:2]

    def store(ref, side, value):
        ref[:, :, side * model : (side + 1) * model] = value.astype(BF16).reshape(half, part, model)

    def over_window(ref):
        return sum(
            dot_nt(turned[b][r], ref[r, :, b * size : (b + 1) * size]) for r in range(rows) for b in range(n)
        )

    store(first_ref, 0, sum(dot_nn(turned[-1][r], dq_ref[r]) for r in range(rows)))
    store(first_ref, 1, over_window(dk_ref))
    store(last_ref, 0, over_window(dv_ref))
    store(last_ref, 1, dot_nn(at_ref[...], gb_ref[...]))


def attn_weights(side, turned, mixed, dq, dk, dv, branch, shards):
    rows, model, size = turned[0].shape
    tokens = branch.shape[0]
    n = len(turned)
    window = n * size
    half = shards // 2
    part = model // shards

    def full(*shape):
        return pl.BlockSpec(shape, lambda i: (0,) * len(shape))

    out = jax.ShapeDtypeStruct((half, part, 2 * model), BF16)
    return pl.pallas_call(
        functools.partial(attn_weights_kernel, n),
        grid=(1,),
        in_specs=[
            *[pl.BlockSpec((rows, model // 2, size), lambda i: (0, side, 0))] * n,
            pl.BlockSpec((model // 2, tokens), lambda i: (side, 0)),
            full(rows, size, model),
            full(rows, model, window),
            full(rows, model, window),
            full(tokens, model),
        ],
        out_specs=[full(half, part, 2 * model)] * 2,
        out_shape=[out, out],
        compiler_params=params(),
        cost_estimate=cost(2 * model * model * (tokens + rows * window), 2 * (4 * rows * model * window + 4 * model * model), COST if side else LIGHT),
        name="attn_weights",
    )(*turned, mixed, dq.reshape(rows, size, model), dk, dv, branch)


def norm_grad_kernel(own, dk_ref, dv_ref, w_ref, *refs):
    model = w_ref.shape[0]
    out_ref = refs[-1]
    grad = dot_nn(w_ref[:, model : 2 * model], dk_ref[0]) + dot_nn(w_ref[:, 2 * model :], dv_ref[0])
    if own:
        out_ref[0] = grad.T + dot_nt(refs[0][0], w_ref[:, :model])
    elif len(refs) == 2:
        out_ref[0] = (grad.T + refs[0][0].astype(F32)).astype(BF16)
    else:
        out_ref[0] = grad.astype(BF16).T


def norm_grad(dk, dv, w_attn, block, size, dq=None, carry=None):
    rows, model, window = dk.shape
    tile = pl.BlockSpec((1, size, model), lambda r: (r, 0, 0))
    if size % 128 == 0 or size == window:
        side = pl.BlockSpec((1, model, size), lambda r: (r, 0, block))
    else:
        side = pl.BlockSpec((1, model, size), lambda r: (r, 0, 0))
        dk, dv = (lax.slice_in_dim(d, block * size, (block + 1) * size, axis=2) for d in (dk, dv))
    more = [x.reshape(rows, size, model) for x in (dq, carry) if x is not None]
    return pl.pallas_call(
        functools.partial(norm_grad_kernel, dq is not None),
        grid=(rows,),
        in_specs=[
            side,
            side,
            pl.BlockSpec((model, 3 * model), lambda r: (0, 0), pipeline_mode=pl.Buffered(1)),
            *[tile] * len(more),
        ],
        out_specs=tile,
        out_shape=jax.ShapeDtypeStruct((rows, size, model), F32 if dq is not None else BF16),
        compiler_params=params(),
        cost_estimate=cost((6 if dq is not None else 4) * rows * model * model * size, rows * model * size * 8 + 6 * model * model, LIGHT),
        name="norm_grad",
    )(dk, dv, w_attn, *more)


def first_back_kernel(dn_ref, back_ref, x_ref, gm_ref, gain_ref, out_ref, gg_ref, gs_ref):
    @pl.when(pl.program_id(0) == 0)
    def _():
        gg_ref[...] = jnp.zeros_like(gg_ref)
        gs_ref[...] = jnp.zeros_like(gs_ref)

    e = dn_ref[...] + back_ref[...].astype(F32)
    grad, gg, gs = norm_back(x_ref[...].astype(F32), gain_ref[...], e)
    gg_ref[...] += gg
    gs_ref[...] += gs
    out_ref[...] = (gm_ref[...] + grad).astype(BF16)


def first_back(dn, back, x, gm, gain, bm):
    tokens, model = x.shape
    tile = pl.BlockSpec((bm, model), lambda i: (i, 0))
    line = pl.BlockSpec((1, model), lambda i: (0, 0))
    return pl.pallas_call(
        first_back_kernel,
        grid=(tokens // bm,),
        in_specs=[tile, tile, tile, tile, line],
        out_specs=[tile, line, line],
        out_shape=[
            jax.ShapeDtypeStruct((tokens, model), BF16),
            jax.ShapeDtypeStruct((1, model), F32),
            jax.ShapeDtypeStruct((1, model), F32),
        ],
        compiler_params=params(),
        cost_estimate=cost(20 * tokens * model, tokens * model * 14),
        name="first_back",
    )(dn, back, x, gm, gain)


def flip(axis, count, bit):
    return functools.partial(lax.ppermute, axis_name=axis, perm=[(i, i ^ bit) for i in range(count)])


def add_low(a, b):
    return (a.astype(F32) + b.astype(F32)).astype(BF16)


def merge_kernel(n, *refs):
    ins, outs = refs[: 2 * n], refs[2 * n :]
    for i, out in enumerate(outs):
        out[...] = (ins[2 * i][...].astype(F32) + ins[2 * i + 1][...].astype(F32)).astype(out.dtype)


def merge(pairs, backwards, final):
    ins, in_specs, out_shape, out_specs = [], [], [], []
    count = pairs[0][0].shape[0]
    half = max(count // 2, 1)
    tiles = 4
    for (a, b), back in zip(pairs, backwards):
        _, rows, cols = a.shape
        shape = (1, rows // tiles, cols)
        if final:
            picks = [lambda q, t: (0, t, 0)]
        elif back:
            picks = [lambda q, t: (q, t, 0), lambda q, t: (q + half, t, 0)]
        else:
            picks = [lambda q, t: (2 * q, t, 0), lambda q, t: (2 * q + 1, t, 0)]
        for pick in picks:
            ins += [a, b]
            in_specs += [pl.BlockSpec(shape, pick)] * 2
            out_specs.append(pl.BlockSpec(shape, lambda q, t: (q, t, 0)))
            out_shape.append(jax.ShapeDtypeStruct((half, rows, cols), BF16))
    size = sum(a.size for a, _ in pairs)
    outs = pl.pallas_call(
        functools.partial(merge_kernel, len(out_shape)),
        grid=(half, tiles),
        in_specs=in_specs,
        out_specs=out_specs,
        out_shape=out_shape,
        compiler_params=params(),
        cost_estimate=cost(size, size * 6, LIGHT),
        name="merge",
    )(*ins)
    return list(outs) if final else list(zip(outs[0::2], outs[1::2]))


class ShardSum:
    def __init__(self, sends, keeps, shards):
        self.shards = shards
        self.bits = list(range(1, shards.bit_length() - 1))
        self.stage = 0
        self.back = [i % 2 == 1 for i in range(len(keeps))]
        self.flying = [(k, flip("fsdp", shards, 1)(s)) for k, s in zip(keeps, sends)]

    def land(self):
        return merge(self.flying, self.back, self.stage == len(self.bits))

    def launch(self, landed):
        self.flying = []
        for back, (kept, sent) in zip(self.back, landed):
            bit = (self.bits[::-1] if back else self.bits)[self.stage]
            self.flying.append((kept, flip("fsdp", self.shards, 1 << bit)(sent)))
        self.stage += 1

    def step(self, *others):
        landed, others = lax.optimization_barrier((self.land(), others))
        self.launch(landed)
        return others if len(others) != 1 else others[0]

    def finish(self):
        while self.stage < len(self.bits):
            self.launch(self.land())
        return [f[0] for f in self.land()]


def add_everywhere(field, axes):
    for axis, count in axes:
        bit = 1
        while bit < count:
            field = field + flip(axis, count, bit)(field)
            bit *= 2
    return field


def per_device(
    inputs,
    segment_ids,
    buckets,
    ln1_gain,
    ln1_bias,
    w_query,
    w_key,
    w_value,
    w_out,
    rel_bias,
    second_norm_gain,
    ln2_bias,
    w_up,
    b_up,
    w_down,
    b_down,
    cotangent,
):
    num_micro, num_rows, size, model = inputs.shape
    rows = num_micro * num_rows
    seq_len = segment_ids.shape[2]
    heads = rel_bias.shape[1]
    shards = lax.axis_size("fsdp")
    ranges = lax.axis_size("seq")
    num_buckets = rel_bias.shape[0] * shards
    hidden = w_up.shape[1]
    tokens = rows * size
    hops = min(-(-(CLIP - 1) // size), ranges - 1)
    halo = hops * size
    window = halo + size
    qb = min(128, size)
    blocks = size // qb
    kw = halo + qb
    width = -(-(kw + qb) // 128) * 128
    tile = min(256, tokens)

    me = lax.axis_index("fsdp")
    order = me ^ jnp.array([*range(1, shards, 2), *range(0, shards, 2)], jnp.int32)
    chips = jnp.append((me // 2) ^ jnp.arange(shards // 2, dtype=jnp.int32), me % 2)

    gather = functools.partial(lax.all_gather, axis_name="fsdp", axis=0, tiled=True)
    w_local = jnp.concatenate([w_query, w_key, w_value], axis=1)
    x = inputs.reshape(rows, size, model)
    w_local, x, w_out, w_up, w_down = lax.optimization_barrier((w_local, x, w_out, w_up, w_down))
    w_attn = gather(w_local)
    up = [(i, i + 1) for i in range(ranges - 1)]
    near = [x]
    if hops:
        near.insert(0, lax.ppermute(x, "seq", up))
    vectors = (ln1_gain, ln1_bias, second_norm_gain, ln2_bias, b_up, b_down, rel_bias.reshape(-1))
    packed = jnp.concatenate(vectors)[None].astype(F32)
    packed = jnp.where(jnp.arange(shards)[:, None] == me, packed, 0.0)
    packed = add_everywhere(packed, (("fsdp", shards),))
    parts, at = [], 0
    for v in vectors:
        parts.append(packed[:, at : at + v.size].reshape(1, -1))
        at += v.size
    gain1, shift1, gain2, shift2, bias_up, bias_down = parts[:6]
    table = parts[6].reshape(num_buckets, heads).astype(BF16)
    fine = hidden // shards // 2
    columns = w_up.reshape(w_up.shape[0], shards, 2, fine)
    w_ff = []
    for side in range(2):
        pieces = [columns[:, :, side].reshape(w_up.shape[0], -1)]
        down = w_down[side * fine : (side + 1) * fine].reshape(-1, w_up.shape[0], model)
        pieces += [down[i] for i in range(down.shape[0])]
        if side == 0:
            pieces.append(w_out)
        w_ff.append(gather(jnp.concatenate(pieces, axis=1)))

    place = lax.axis_index("seq") * size
    column = jnp.arange(width, dtype=jnp.int32)
    gap = halo - column
    inside = (gap >= 0) & (column > 0)
    bucket_of = jnp.where(inside, jnp.flip(jnp.pad(buckets[: halo + 1], (width - halo - 1, 0))), -1)
    onehot = bucket_of[:, None] == jnp.arange(num_buckets, dtype=jnp.int32)[None]
    by_gap = dot_nn(onehot.astype(BF16), table) + jnp.where(inside, 0.0, NEG)[:, None]
    bias = make_bias(by_gap.T, qb, kw)
    segs = segment_ids.reshape(rows, seq_len)
    segs = lax.dynamic_slice_in_dim(jnp.pad(segs, ((0, 0), (halo, 0)), constant_values=-1), place, window, 1)
    mask = jnp.stack(
        [
            jnp.where(
                segs[:, halo + b * qb : halo + (b + 1) * qb, None] == segs[:, None, b * qb : b * qb + kw], 0.0, NEG
            )
            for b in range(blocks)
        ],
        axis=1,
    ).astype(F32)

    for hop in range(hops - 1):
        moved = near[0]
        if hop == 0:
            moved, bias, mask, gain1 = lax.optimization_barrier((moved, bias, mask, gain1))
        near.insert(0, lax.ppermute(moved, "seq", up))

    normed, turned, kvs = [None] * (hops + 1), [None] * (hops + 1), [None] * (hops + 1)
    for b in range(hops, -1, -1):
        if b == hops - 2:
            near[: b + 1], kvs[b + 1 :] = lax.optimization_barrier((near[: b + 1], kvs[b + 1 :]))
        normed[b], turned[b] = norm_block(order, near[b], gain1, shift1)
        first, cols, scaled = (0, 3 * model, model) if b == hops else (model, 2 * model, 0)
        kvs[b] = project(normed[b], w_attn, first, cols, scaled)
    attended, inv, expo = attn_fwd(kvs, bias, mask)
    x = x.reshape(tokens, model)
    middle, normed_two, two_turned, mixed_turned = middle_block(order, attended, w_ff[0], x, gain2, shift2, tile)

    cot = cotangent.reshape(tokens, model)
    bias_up = bias_up.reshape(shards, 2, fine)
    tile_ff = tokens // 2 if tokens % 32 == 0 else tokens
    pairs = shards // 2
    ffn = functools.partial(ffn_block, chips, normed_two, two_turned, cot, b_down=bias_down, bm=tile_ff)
    bias_a, bias_b = (bias_up[:, side].reshape(1, -1) for side in range(2))
    part_out, part_grad, us, uk, ds, dk, grad_b_a = ffn(
        middle, jnp.zeros((8, model), F32), w_ff[0], bias_a, begin=0, end=pairs, first=True, last=False
    )
    sum_a = ShardSum([us, ds], [uk, dk], shards)
    part_out, part_grad, *grads = ffn(
        part_out, part_grad, w_ff[1], bias_b, begin=0, end=pairs // 2, first=False, last=False
    )
    part_grad = sum_a.step(part_grad)
    outputs, grad_norm2, us, uk, ds, dk, grad_b_b = ffn(
        part_out, part_grad, w_ff[1], bias_b, begin=pairs // 2, end=pairs, first=False, last=True, grads=grads
    )
    sum_b = ShardSum([us, ds], [uk, dk], shards)
    grad_b_up = jnp.stack([grad_b_a.reshape(shards, fine), grad_b_b.reshape(shards, fine)], axis=1)
    grad_b_down = jnp.sum(cot.astype(F32), axis=0, keepdims=True)

    def total(fields):
        return lax.psum(tuple(fields), "seq")

    if sum_a.stage < len(sum_a.bits):
        grad_norm2 = sum_a.step(grad_norm2)
    grad_middle, grad_branch, grad_attended, grad_gain2, grad_shift2 = middle_back(
        grad_norm2, middle, cot, w_ff[0], gain2, tile
    )
    grad_attended = sum_b.step(grad_attended)
    done_a = sum_a.finish()
    grad_attended, done_a = lax.optimization_barrier((grad_attended, done_a))
    total_a = total(done_a)
    grad_q, grad_k, grad_v, diagonal = attn_bwd(kvs, expo, inv, attended, grad_attended, width)
    if sum_b.stage < len(sum_b.bits):
        grad_q = sum_b.step(grad_q)
    back = None
    down = [(i + 1, i) for i in range(ranges - 1)]
    if hops:
        grad_far = norm_grad(grad_k, grad_v, w_attn, 0, size)
        grad_far, grad_q = lax.optimization_barrier((grad_far, grad_q))
        back = lax.ppermute(grad_far, "seq", down)
    first_send, last_send = attn_weights(0, turned, mixed_turned, grad_q, grad_k, grad_v, grad_branch, shards)
    done_b = sum_b.finish()
    done_b, grad_q, first_send, total_a = lax.optimization_barrier((done_b, grad_q, first_send, total_a))
    up_b, down_b = done_b
    total_b = jnp.concatenate([*jnp.split(up_b, up_b.shape[1] // model, axis=1), down_b], axis=0)
    total_b = lax.psum_scatter(total_b, "seq", scatter_dimension=0, tiled=True)
    total_b = lax.all_gather(total_b, "seq", axis=0, tiled=True)
    first_keep, last_keep = attn_weights(1, turned, mixed_turned, grad_q, grad_k, grad_v, grad_branch, shards)
    sum_c = ShardSum([first_send, last_send], [first_keep, last_keep], shards)
    grad_k, grad_v, grad_q = sum_c.step(grad_k, grad_v, grad_q)
    for hop in range(1, hops):
        grad_far = norm_grad(grad_k, grad_v, w_attn, hop, size, carry=back)
        grad_far, grad_q = lax.optimization_barrier((grad_far, grad_q))
        back = lax.ppermute(grad_far, "seq", down)
    grad_q, total_b = lax.optimization_barrier((grad_q, total_b))
    grad_own = norm_grad(grad_k, grad_v, w_attn, hops, size, dq=grad_q)
    done_c = sum_c.finish()
    done_c, total_b, grad_own = lax.optimization_barrier((done_c, total_b, grad_own))
    grad_first, grad_last = (f.astype(F32) for f in total(done_c))
    up_a, down_a = (f.astype(F32) for f in total_a)
    total_b = total_b.astype(F32)
    count = up_b.shape[0] * (up_b.shape[1] // model)
    up_b = jnp.concatenate(jnp.split(total_b[:count], up_b.shape[1] // model, axis=0), axis=1)
    down_b = total_b[count:]
    grad_w_up = jnp.stack([up_a.reshape(-1, shards, fine), up_b.reshape(-1, shards, fine)], axis=2).reshape(w_up.shape)
    grad_w_down = jnp.concatenate([down_a, down_b], axis=0)
    if back is None:
        back = jnp.zeros((rows, size, model), BF16)
    input_grad, grad_gain1, grad_shift1 = first_back(
        grad_own.reshape(tokens, model), back.reshape(tokens, model), x, grad_middle, gain1, tile
    )

    diagonal = diagonal[:, :2].reshape(heads, width)
    grad_table = lax.dot_general(onehot.astype(F32), diagonal, (((0,), (1,)), ((), ())), precision=HIGHEST)

    small = (grad_gain1, grad_shift1, grad_gain2, grad_shift2, grad_b_up, grad_b_down, grad_table)
    small = jnp.concatenate([s.reshape(shards, -1) for s in small], axis=1)
    small = add_everywhere(small, (("fsdp", shards), ("seq", ranges)))
    small = lax.dynamic_slice_in_dim(small, lax.axis_index("fsdp"), 1, 0)[0]
    finals, at = [], 0
    for v in vectors:
        finals.append(small[at : at + v.size].reshape(v.shape))
        at += v.size
    finals[6] = finals[6].reshape(rel_bias.shape)

    return (
        outputs.reshape(inputs.shape),
        input_grad.reshape(inputs.shape),
        finals[0],
        finals[1],
        grad_first[:, :model],
        grad_first[:, model:],
        grad_last[:, :model],
        grad_last[:, model:],
        finals[6],
        finals[2],
        finals[3],
        grad_w_up,
        finals[4],
        grad_w_down,
        finals[5],
    )


def solution(mesh):
    token = P(None, "fsdp", "seq", None)
    vector = P("fsdp")
    matrix = P("fsdp", None)
    return jax.shard_map(
        per_device,
        mesh=mesh,
        in_specs=(
            token, P(None, "fsdp", None), P(), vector, vector, matrix, matrix, matrix, matrix, matrix,
            vector, vector, matrix, vector, matrix, vector, token,
        ),
        out_specs=(
            token, token, vector, vector, matrix, matrix, matrix, matrix, matrix,
            vector, vector, matrix, vector, matrix, vector,
        ),
        check_vma=False,
    )
```

time: 705 us -> 547 us (0.78)
  waiting for transfers between devices: 316 us -> 104 us
  Pallas kernels: 194 us -> 329 us
  blocking collectives: 67.9 us -> 0 us
  matrix products: 41.5 us -> 0.79 us
  starting transfers between devices: 12.7 us -> 39.1 us
  other arithmetic: 22.4 us -> 12.7 us
    pallas_call x7 -> x26, Pallas kernels: 167 us -> 302 us  [the longest x3 81 us: ffn_block(): pl.pallas_call(functools.partial(ffn_kernel, bm, first, last), grid_spec=...]
    reduce_scatter x2 -> x1, waiting for transfers between devices: 148 us -> 23.2 us  [per_device(): total_b = lax.psum_scatter(total_b, 'seq', scatter_dimension=0, tiled=True)]
    psum x1 -> x0, blocking collectives: 44.9 us -> none  [per_device(): small = lax.psum(small, ('fsdp', 'seq'))]
    dot_general x7 -> x0, matrix products: 40.7 us -> none  [the longest x1 8.54 us: per_device(): jnp.einsum('rft,if->rti', grad_v, w_qkv[:, 2 * model:], preferred_element...]
    ppermute x4 -> x30, waiting for transfers between devices: 70.7 us -> 32.8 us  [the longest x8 12.8 us: add_everywhere(): field = field + flip(axis, count, bit)(field)]
    ppermute x4 -> x30, starting transfers between devices: 12.3 us -> 38.8 us  [the longest x12 14.1 us: launch(): self.flying.append((kept, flip('fsdp', self.shards, 1 << bit)(sent)))]
    psum x1 -> x2, waiting for transfers between devices: 57.3 us -> 31.5 us  [total(): return lax.psum(tuple(fields), 'seq')]
    unnamed x1 -> x0, blocking collectives: 23.1 us -> none
  transfers between devices with their start and end apart: 12 -> 37, of which waited for: 7 -> 16; matrix products, arithmetic and copies ran while one was open for 7% -> 6% of each run, Pallas kernels for 13% -> 57%
where the time goes in v2:
time: 547 us; the launch traced here: 538 us
  Pallas kernels  329 us (60%)
  waiting for transfers between devices  104 us (19%)
  starting transfers between devices  39.1 us (7%)
  local copies, waits for them, and re-layouts  36.6 us (7%)
  between operations  15 us (3%)
  other arithmetic  12.7 us (2%)
    pallas_call x3, Pallas kernels, ffn_block(): pl.pallas_call(functools.partial(ffn_kernel, bm, first, last), grid_spec=...  81 us
    pallas_call x9, Pallas kernels, merge(): pl.pallas_call(functools.partial(merge_kernel, len(out_shape)), grid=(hal...  46.3 us
    pallas_call x1, Pallas kernels, attn_bwd(): pl.pallas_call(functools.partial(attn_bwd_kernel, qb, width, n), grid=(ro...  34.1 us
    pallas_call x1, Pallas kernels, attn_fwd(): pl.pallas_call(functools.partial(attn_fwd_kernel, qb, n), grid=(rows, pai...  33 us
    psum x2, waiting for transfers between devices, total(): return lax.psum(tuple(fields), 'seq')  31.5 us
    pallas_call x3, Pallas kernels, project(): pl.pallas_call(functools.partial(proj_kernel, scaled // bn), grid=(cols /...  30.9 us
    pallas_call x2, Pallas kernels, attn_weights(): pl.pallas_call(functools.partial(attn_weights_kernel, n), grid=(1,), in_s...  27 us
    pallas_call x3, Pallas kernels, norm_grad(): pl.pallas_call(functools.partial(norm_grad_kernel, dq is not None), grid=...  26.7 us
  transfers between devices with their start and end apart: 37, of which 16 were waited for; matrix products, arithmetic and copies ran while one was open for 6% of the time, Pallas kernels for 57%

profile of v2, /device:TPU:0, one launch (start us, length us, event | category | flops | bytes accessed | tf_op | source)
XLA Modules:
  0.0 537.5 jit_solution(8853781911919472710)
XLA Ops:
  37.5 11.7 %bias_table.1.refs_6_ = f32[16,128,640]{2,1,0:T(8,128)} custom-call(f32[16,1,768]{2,1,0:T(1,128)} %broadcast_in_dim.63.row_ref), custom_call_target="tpu_custom_call" | custom-call | bytes 157286400 | tf_op jit(solution)/shard_map/bias_table/pallas_call | solution.py:79
  51.1 6.7 %collective-permute-done.x_ref = bf16[3,256,1024]{2,1,0:T(8,128)(2,1)} collective-permute-done((bf16[3,256,1024]{2,1,0:T(8,128)(2,1)S(1)}, bf16[3,256,1024]{2,1,0:T(8,128)(2,1)}, u32[]{:S(2)}, u32[]{:S(2)}) %collective-permute-start) | collective-permute-done | bytes 1572896 | tf_op jit(solution)/shard_map/ppermute | solution.py:784
  73.7 12.7 %project.4.q_ref.refs_2_.refs_5_ = bf16[768,3072]{1,0:T(8,128)(2,1)} custom-call(bf16[768,1024]{1,0:T(8,128)(2,1)} %bitcast.142, bf16[1024,3072]{1,0:T(8,128)(2,1)} %all-gather.5.cloned.1.call-done.w_ref), custom_call_target="tpu_custom_call" | custom-call | flops 144955146240 | bytes 377487360 | tf_op jit(solution)/shard_map/project/pallas_call | solution.py:150
  86.4 9.2 %project.3.refs_1_.refs_4_ = bf16[768,2048]{1,0:T(8,128)(2,1)} custom-call(bf16[768,1024]{1,0:T(8,128)(2,1)} %bitcast.143, bf16[1024,3072]{1,0:T(8,128)(2,1)} %all-gather.5.cloned.1.call-done.w_ref), custom_call_target="tpu_custom_call" | custom-call | flops 96636764160 | bytes 267386880 | tf_op jit(solution)/shard_map/project/pallas_call | solution.py:150
  101.0 9.0 %project.5.refs_0_.refs_3_ = bf16[768,2048]{1,0:T(8,128)(2,1)} custom-call(bf16[768,1024]{1,0:T(8,128)(2,1)} %bitcast.144, bf16[1024,3072]{1,0:T(8,128)(2,1)} %all-gather.5.cloned.1.call-done.w_ref), custom_call_target="tpu_custom_call" | custom-call | flops 96636764160 | bytes 267386880 | tf_op jit(solution)/shard_map/project/pallas_call | solution.py:150
  110.0 33.0 %attn_fwd.1 = (bf16[768,1024]{1,0:T(8,128)(2,1)}, f32[768,1024]{1,0:T(8,128)}, bf16[3,8,2,256,640]{4,3,2,1,0:T(8,128)(2,1)}) custom-call(bf16[768,3072]{1,0:T(8,128)(2,1)} %project.4.q_ref.refs_2_.refs_5_, bf16[768,2048]{1,0:T(8,128)(2,1)} %project.5.refs_0_.refs_3_, bf16[768,2048]{1,0:T(8,128)(2,1)} %project.3.refs_1_.refs_4_, ...), custom_call_target="tpu_custom_call" | custom-call | flops 60397977600 | bytes 943718400 | tf_op jit(solution)/shard_map/attn_fwd/pallas_call | solution.py:220
  143.1 7.7 %middle_block.1 = (f32[768,1024]{1,0:T(8,128)}, bf16[768,1024]{1,0:T(8,128)(2,1)}, bf16[1024,768]{1,0:T(8,128)(2,1)}, bf16[1024,768]{1,0:T(8,128)(2,1)}) custom-call(s32[8]{0:T(128)} %broadcast_xor_fusion.order_ref, bf16[768,1024]{1,0:T(8,128)(2,1)} %get-tuple-element.165.a_ref.refs_8_, ...), custom_call_target="tpu_custom_call" | custom-call | flops 48318382080 | bytes 393216000 | tf_op jit(solution)/shard_map/middle_block/pallas_call | solution.py:346
  151.4 36.0 %ffn_block.3 = (f32[768,1024]{1,0:T(8,128)}, f32[768,1024]{1,0:T(8,128)}, bf16[4,128,2048]{2,1,0:T(8,128)(2,1)}, bf16[4,128,2048]{2,1,0:T(8,128)(2,1)}, bf16[4,2...) custom-call(s32[5]{0:T(128)} %pad_add_fusion.chip_ref, ...), custom_call_target="tpu_custom_call" | custom-call | flops 579820584960 | bytes 975175680 | tf_op jit(solution)/shard_map/ffn_block/pallas_call | solution.py:426
  188.0 22.6 %ffn_block.4 = (f32[768,1024]{1,0:T(8,128)}, f32[768,1024]{1,0:T(8,128)}, bf16[4,128,2048]{2,1,0:T(8,128)(2,1)}, bf16[4,128,2048]{2,1,0:T(8,128)(2,1)}, bf16[4,2...) custom-call(s32[5]{0:T(128)} %pad_add_fusion.chip_ref, ...), custom_call_target="tpu_custom_call" | custom-call | flops 289910292480 | bytes 723517440 | tf_op jit(solution)/shard_map/ffn_block/pallas_call | solution.py:426
  210.6 7.5 %merge.9 = (bf16[2,128,2048]{2,1,0:T(8,128)(2,1)}, bf16[2,128,2048]{2,1,0:T(8,128)(2,1)}, bf16[2,256,1024]{2,1,0:T(8,128)(2,1)}, bf16[2,256,1024]{2,1,0:T(8,128)(2,1)}) custom-call(bf16[4,128,2048]{2,1,0:T(8,128)(2,1)} %get-tuple-element.175.refs_0_.refs_2_, bf16[4,128,2048]{2,1,0:T(8,128)(2,1)} %collective-permute-done.5.refs_1_.refs_3_, ...), custom_call_target="tpu_custom_call" | custom-call | flops 2097152 | bytes 12582912 | tf_op jit(solution)/shard_map/merge/pallas_call | solution.py:684
  221.3 22.4 %ffn_block.5 = (bf16[768,1024]{1,0:T(8,128)(2,1)}, f32[768,1024]{1,0:T(8,128)}, bf16[4,128,2048]{2,1,0:T(8,128)(2,1)}, bf16[4,128,2048]{2,1,0:T(8,128)(2,1)}, bf...) custom-call(s32[5]{0:T(128)} %pad_add_fusion.chip_ref, ...), custom_call_target="tpu_custom_call", output_to_operand_aliasing={{2}: (11, {}), {3}: (12, {}), {4}: (13, {}), {5}: (14, {}),... | custom-call | flops 289910292480 | bytes 723517440 | tf_op jit(solution)/shard_map/ffn_block/pallas_call | solution.py:426
  251.1 9.1 %middle_back.1 = (f32[768,1024]{1,0:T(8,128)}, bf16[768,1024]{1,0:T(8,128)(2,1)}, bf16[768,1024]{1,0:T(8,128)(2,1)}, f32[1,1024]{1,0:T(1,128)}, f32[1,1024]{1,0:T(1,128)}) custom-call(f32[768,1024]{1,0:T(8,128)} %get-tuple-element.212.gn_ref, f32[768,1024]{1,0:T(8,128)} %get-tuple-element.171.acc_ref.mid_ref, bf16[768,1024]{1,0:T(8,128)(2,1)} %bitcast.103, ...), custom_call_target="tpu_custom_call" | custom-call | flops 48318382080 | bytes 487587840 | tf_op jit(solution)/shard_map/middle_back/pallas_call | solution.py:509
  269.9 7.4 %merge.10 = (bf16[2,128,2048]{2,1,0:T(8,128)(2,1)}, bf16[2,128,2048]{2,1,0:T(8,128)(2,1)}, bf16[2,256,1024]{2,1,0:T(8,128)(2,1)}, bf16[2,256,1024]{2,1,0:T(8,128)(2,1)}) custom-call(bf16[4,128,2048]{2,1,0:T(8,128)(2,1)} %get-tuple-element.195.refs_0_.refs_2_, bf16[4,128,2048]{2,1,0:T(8,128)(2,1)} %copy-done, ...), custom_call_target="tpu_custom_call" | custom-call | flops 2097152 | bytes 12582912 | tf_op jit(solution)/shard_map/merge/pallas_call | solution.py:684
  279.4 34.1 %attn_bwd.1 = (bf16[768,1024]{1,0:T(8,128)(2,1)}, bf16[3,1024,768]{2,1,0:T(8,128)(2,1)}, bf16[3,1024,768]{2,1,0:T(8,128)(2,1)}, f32[8,8,768]{2,1,0:T(8,128)}) custom-call(bf16[768,3072]{1,0:T(8,128)(2,1)} %project.4.q_ref.refs_2_.refs_5_, bf16[768,2048]{1,0:T(8,128)(2,1)} %project.5.refs_0_.refs_3_, bf16[768,2048]{1,0:T(8,128)(2,1)} %project.3.refs_1_.refs_4_, ...), custom_call_target="tpu_custom_call" | custom-call | flops 120795955200 | bytes 943718400 | tf_op jit(solution)/shard_map/attn_bwd/pallas_call | solution.py:292
  313.5 8.1 %norm_grad.3 = bf16[3,256,1024]{2,1,0:T(8,128)(2,1)} custom-call(bf16[3,1024,768]{2,1,0:T(8,128)(2,1)} %get-tuple-element.266.dk_ref.refs_5_, bf16[3,1024,768]{2,1,0:T(8,128)(2,1)} %get-tuple-element.267.dv_ref.refs_6_, bf16[1024,3072]{1,0:T(8,128)(2,1)} %all-gather.5.cloned.1.call-done.w_ref), custom_call_target="tpu_custom_call" | custom-call | flops 3221225472 | bytes 12582912 | tf_op jit(solution)/shard_map/norm_grad/pallas_call | solution.py:600
  330.0 13.5 %attn_weights.2 = (bf16[4,128,2048]{2,1,0:T(8,128)(2,1)}, bf16[4,128,2048]{2,1,0:T(8,128)(2,1)}) custom-call(bf16[3,1024,256]{2,1,0:T(8,128)(2,1)} %get-tuple-element.191.refs_0_, bf16[3,1024,256]{2,1,0:T(8,128)(2,1)} %get-tuple-element.192.refs_1_, bf16[3,1024,256]{2,1,0:T(8,128)(2,1)} %get-tuple-element.193.refs_2_, ...), custom_call_target="tpu_custom_call" | custom-call | flops 6442450944 | bytes 27262976 | tf_op jit(solution)/shard_map/attn_weights/pallas_call | solution.py:560
  353.8 13.5 %attn_weights.3 = (bf16[4,128,2048]{2,1,0:T(8,128)(2,1)}, bf16[4,128,2048]{2,1,0:T(8,128)(2,1)}) custom-call(bf16[3,1024,256]{2,1,0:T(8,128)(2,1)} %get-tuple-element.191.refs_0_, bf16[3,1024,256]{2,1,0:T(8,128)(2,1)} %get-tuple-element.192.refs_1_, bf16[3,1024,256]{2,1,0:T(8,128)(2,1)} %get-tuple-element.193.refs_2_, ...), custom_call_target="tpu_custom_call" | custom-call | flops 193273528320 | bytes 817889280 | tf_op jit(solution)/shard_map/attn_weights/pallas_call | solution.py:560
  367.3 7.5 %merge.15 = (bf16[2,128,2048]{2,1,0:T(8,128)(2,1)}, bf16[2,128,2048]{2,1,0:T(8,128)(2,1)}, bf16[2,128,2048]{2,1,0:T(8,128)(2,1)}, bf16[2,128,2048]{2,1,0:T(8,128)(2,1)}) custom-call(bf16[4,128,2048]{2,1,0:T(8,128)(2,1)} %get-tuple-element.248.refs_0_.refs_2_, bf16[4,128,2048]{2,1,0:T(8,128)(2,1)} %collective-permute-done.17.refs_1_.refs_3_, ...), custom_call_target="tpu_custom_call" | custom-call | flops 2097152 | bytes 12582912 | tf_op jit(solution)/shard_map/merge/pallas_call | solution.py:684
  376.8 23.2 %reduce-scatter.2.cloned.1.call-done = bf16[128,1024]{1,0:T(8,128)(2,1)} async-done(((bf16[512,1024]{1,0:T(8,128)(2,1)}), bf16[128,1024]{1,0:T(8,128)(2,1)}) %reduce-scatter.2.cloned.1.call-update) | async-done | bytes 262160 | tf_op jit(solution)/shard_map/reduce_scatter | solution.py:890
  400.2 8.5 %norm_grad.4 = bf16[3,256,1024]{2,1,0:T(8,128)(2,1)} custom-call(bf16[3,1024,768]{2,1,0:T(8,128)(2,1)} %get-tuple-element.266.dk_ref.refs_5_, bf16[3,1024,768]{2,1,0:T(8,128)(2,1)} %get-tuple-element.267.dv_ref.refs_6_, bf16[1024,3072]{1,0:T(8,128)(2,1)} %all-gather.5.cloned.1.call-done.w_ref, bf16[3,256,1024]{2,1,0:T(8,128)(2,1)} %collective-permute-done.23.refs_0_), custom_call_target="tpu_custom_call" | custom-call | flops 3221225472 | bytes 12582912 | tf_op jit(solution)/shard_map/norm_grad/pallas_call | solution.py:600
  421.3 16.3 %all-gather.11.cloned.1.call-done = bf16[512,1024]{1,0:T(8,128)(2,1)} async-done(((bf16[128,1024]{1,0:T(8,128)(2,1)}), bf16[512,1024]{1,0:T(8,128)(2,1)}) %all-gather.11.cloned.1.call-update) | async-done | bytes 1048592 | tf_op jit(solution)/shard_map/all_gather | solution.py:891
  442.3 10.2 %norm_grad.5 = f32[3,256,1024]{2,1,0:T(8,128)} custom-call(bf16[3,1024,768]{2,1,0:T(8,128)(2,1)} %get-tuple-element.266.dk_ref.refs_5_, bf16[3,1024,768]{2,1,0:T(8,128)(2,1)} %get-tuple-element.267.dv_ref.refs_6_, bf16[1024,3072]{1,0:T(8,128)(2,1)} %all-gather.5.cloned.1.call-done.w_ref, bf16[3,256,1024]{2,1,0:T(8,128)(2,1)} %bitcast.99), custom_call_target="tpu_custom_call" | custom-call | flops 4831838208 | bytes 12582912 | tf_op jit(solution)/shard_map/norm_grad/pallas_call | solution.py:600
  452.4 9.4 %collective-permute-done.24 = bf16[3,256,1024]{2,1,0:T(8,128)(2,1)} collective-permute-done((bf16[3,256,1024]{2,1,0:T(8,128)(2,1)}, bf16[3,256,1024]{2,1,0:T(8,128)(2,1)}, u32[]{:S(2)}, u32[]{:S(2)}) %collective-permute-start.24) | collective-permute-done | bytes 1572896 | tf_op jit(solution)/shard_map/ppermute | solution.py:898
  495.7 31.5 %all-reduce.7.cloned.1.call-done = (bf16[128,2048]{1,0:T(8,128)(2,1)}, bf16[128,2048]{1,0:T(8,128)(2,1)}) async-done(((bf16[128,2048]{1,0:T(8,128)(2,1)}, bf16[128,2048]{1,0:T(8,128)(2,1)}), (bf16[128,2048]{1,0:T(8,128)(2,1)}, bf16[128,2048]{1,0:T(8,128)(2,1)})) %all-reduce.7.cloned.1.call-update) | async-done | bytes 1048592 | tf_op jit(solution)/shard_map/psum | solution.py:865
  (241 shorter events, 151.6 us)
Async XLA Ops:
  7.2 66.5 %all-gather.5.cloned.1.call-start = ((), (), s32[]{:S(2)}) async-start(), calls=%async_computation.1 | async-start | bytes 7077888 | tf_op jit(solution)/shard_map/all_gather | solution.py:780
  9.4 133.7 %all-gather.7.cloned.1.call-start = ((), (), s32[]{:S(2)}) async-start(), calls=%async_computation.2 | async-start | bytes 11796480 | tf_op jit(solution)/shard_map/all_gather | solution.py:804
  16.8 171.2 %all-gather.9.cloned.1.call-start = ((), (), s32[]{:S(2)}) async-start(), calls=%async_computation.3 | async-start | bytes 9437184 | tf_op jit(solution)/shard_map/all_gather | solution.py:804
  19.0 38.8 %collective-permute-start = (bf16[3,256,1024]{2,1,0:T(8,128)(2,1)S(1)}, bf16[3,256,1024]{2,1,0:T(8,128)(2,1)}, u32[]{:S(2)}, u32[]{:S(2)}) collective-permute-start(bf16[3,256,1024]{2,1,0:T(8,128)(2,1)S(1)} %bitcast.89), channel_id=1, source_target_pairs={{0,1},{1,2},{2,3},{4,5},{5,6},{6,7},{8,9},{9,10},{10,11},{12,13},{... | collective-permute-start | bytes 4718600 | tf_op jit(solution)/shard_map/ppermute | solution.py:784
  25.8 324.2 %all-reduce.9.cloned.1.call-start = ((), (), s32[]{:S(2)}) async-start(), calls=%async_computation.7 | async-start | bytes 2097152 | tf_op jit(solution)/shard_map/psum | solution.py:865
  57.7 38.3 %collective-permute-start.4 = (bf16[3,256,1024]{2,1,0:T(8,128)(2,1)}, bf16[3,256,1024]{2,1,0:T(8,128)(2,1)}, u32[]{:S(2)}, u32[]{:S(2)}) collective-permute-start(bf16[3,256,1024]{2,1,0:T(8,128)(2,1)} %collective-permute-done.x_ref), channel_id=1, source_target_pairs={{0,1},{1,2},{2,3},{4,5},{5,6},{6,7},{8,9},{9,10},{10,11},{12,13},{... | collective-permute-start | bytes 4718600 | tf_op jit(solution)/shard_map/ppermute | solution.py:830
  187.4 23.2 %collective-permute-start.5 = (bf16[4,128,2048]{2,1,0:T(8,128)(2,1)}, bf16[4,128,2048]{2,1,0:T(8,128)(2,1)}, u32[]{:S(2)}, u32[]{:S(2)}) collective-permute-start(bf16[4,128,2048]{2,1,0:T(8,128)(2,1)} %get-tuple-element.176), channel_id=1, source_target_pairs={{0,4},{4,0},{8,12},{12,8},{16,20},{20,16},{24,28},{28,24},{1,5},{5... | collective-permute-start | bytes 6291464 | tf_op jit(solution)/shard_map/ppermute | solution.py:703
  187.5 23.1 %collective-permute-start.6 = (bf16[4,256,1024]{2,1,0:T(8,128)(2,1)}, bf16[4,256,1024]{2,1,0:T(8,128)(2,1)}, u32[]{:S(2)}, u32[]{:S(2)}) collective-permute-start(bf16[4,256,1024]{2,1,0:T(8,128)(2,1)} %get-tuple-element.178), channel_id=1, source_target_pairs={{0,4},{4,0},{8,12},{12,8},{16,20},{20,16},{24,28},{28,24},{1,5},{5... | collective-permute-start | bytes 6291464 | tf_op jit(solution)/shard_map/ppermute | solution.py:703
  218.2 26.1 %collective-permute-start.10 = (bf16[2,256,1024]{2,1,0:T(8,128)(2,1)}, bf16[2,256,1024]{2,1,0:T(8,128)(2,1)}, u32[]{:S(2)}, u32[]{:S(2)}) collective-permute-start(bf16[2,256,1024]{2,1,0:T(8,128)(2,1)} %get-tuple-element.206), channel_id=1, source_target_pairs={{0,16},{4,20},{8,24},{12,28},{16,0},{20,4},{24,8},{28,12},{1,17},{... | collective-permute-start | bytes 3145736 | tf_op jit(solution)/shard_map/ppermute | solution.py:712
  219.8 25.2 %collective-permute-start.9 = (bf16[2,128,2048]{2,1,0:T(8,128)(2,1)}, bf16[2,128,2048]{2,1,0:T(8,128)(2,1)}, u32[]{:S(2)}, u32[]{:S(2)}) collective-permute-start(bf16[2,128,2048]{2,1,0:T(8,128)(2,1)} %get-tuple-element.204), channel_id=1, source_target_pairs={{0,8},{4,12},{8,0},{12,4},{16,24},{20,28},{24,16},{28,20},{1,9},{5... | collective-permute-start | bytes 3145736 | tf_op jit(solution)/shard_map/ppermute | solution.py:712
  243.7 24.2 %collective-permute-start.7 = (bf16[4,128,2048]{2,1,0:T(8,128)(2,1)}, bf16[4,128,2048]{2,1,0:T(8,128)(2,1)S(1)}, u32[]{:S(2)}, u32[]{:S(2)}) collective-permute-start(bf16[4,128,2048]{2,1,0:T(8,128)(2,1)} %get-tuple-element.196), channel_id=1, source_target_pairs={{0,4},{4,0},{8,12},{12,8},{16,20},{20,16},{24,28},{28,24},{1,5},{5... | collective-permute-start | bytes 6291464 | tf_op jit(solution)/shard_map/ppermute | solution.py:703
  243.8 24.1 %collective-permute-start.8 = (bf16[4,256,1024]{2,1,0:T(8,128)(2,1)}, bf16[4,256,1024]{2,1,0:T(8,128)(2,1)S(1)}, u32[]{:S(2)}, u32[]{:S(2)}) collective-permute-start(bf16[4,256,1024]{2,1,0:T(8,128)(2,1)} %get-tuple-element.198), channel_id=1, source_target_pairs={{0,4},{4,0},{8,12},{12,8},{16,20},{20,16},{24,28},{28,24},{1,5},{5... | collective-permute-start | bytes 6291464 | tf_op jit(solution)/shard_map/ppermute | solution.py:703
  277.3 44.3 %collective-permute-start.11 = (bf16[2,128,2048]{2,1,0:T(8,128)(2,1)}, bf16[2,128,2048]{2,1,0:T(8,128)(2,1)S(1)}, u32[]{:S(2)}, u32[]{:S(2)}) collective-permute-start(bf16[2,128,2048]{2,1,0:T(8,128)(2,1)} %get-tuple-element.215), channel_id=1, source_target_pairs={{0,8},{4,12},{8,0},{12,4},{16,24},{20,28},{24,16},{28,20},{1,9},{5... | collective-permute-start | bytes 3145736 | tf_op jit(solution)/shard_map/ppermute | solution.py:712
  278.4 43.2 %collective-permute-start.12 = (bf16[2,256,1024]{2,1,0:T(8,128)(2,1)}, bf16[2,256,1024]{2,1,0:T(8,128)(2,1)S(1)}, u32[]{:S(2)}, u32[]{:S(2)}) collective-permute-start(bf16[2,256,1024]{2,1,0:T(8,128)(2,1)} %get-tuple-element.217), channel_id=1, source_target_pairs={{0,16},{4,20},{8,24},{12,28},{16,0},{20,4},{24,8},{28,12},{1,17},{... | collective-permute-start | bytes 3145736 | tf_op jit(solution)/shard_map/ppermute | solution.py:712
  279.4 120.6 %reduce-scatter.2.cloned.1.call-start = ((), (), s32[]{:S(2)}) async-start(), calls=%async_computation.4 | async-start | bytes 1310720 | tf_op jit(solution)/shard_map/reduce_scatter | solution.py:890
  343.5 23.8 %collective-permute-start.18 = (bf16[4,128,2048]{2,1,0:T(8,128)(2,1)}, bf16[4,128,2048]{2,1,0:T(8,128)(2,1)}, u32[]{:S(2)}, u32[]{:S(2)}) collective-permute-start(bf16[4,128,2048]{2,1,0:T(8,128)(2,1)} %get-tuple-element.251), channel_id=1, source_target_pairs={{0,4},{4,0},{8,12},{12,8},{16,20},{20,16},{24,28},{28,24},{1,5},{5... | collective-permute-start | bytes 6291464 | tf_op jit(solution)/shard_map/ppermute | solution.py:703
  343.5 56.7 %collective-permute-start.23 = (bf16[3,256,1024]{2,1,0:T(8,128)(2,1)}, bf16[3,256,1024]{2,1,0:T(8,128)(2,1)}, u32[]{:S(2)}, u32[]{:S(2)}) collective-permute-start(bf16[3,256,1024]{2,1,0:T(8,128)(2,1)} %norm_grad.3), channel_id=1, source_target_pairs={{1,0},{2,1},{3,2},{5,4},{6,5},{7,6},{9,8},{10,9},{11,10},{13,12},{... | collective-permute-start | bytes 4718600 | tf_op jit(solution)/shard_map/ppermute | solution.py:884
  353.2 84.5 %all-gather.11.cloned.1.call-start = ((), (), s32[]{:S(2)}) async-start(), calls=%async_computation.5 | async-start | bytes 1310720 | tf_op jit(solution)/shard_map/all_gather | solution.py:891
  374.8 35.3 %collective-permute-start.19 = (bf16[2,128,2048]{2,1,0:T(8,128)(2,1)}, bf16[2,128,2048]{2,1,0:T(8,128)(2,1)S(1)}, u32[]{:S(2)}, u32[]{:S(2)}) collective-permute-start(bf16[2,128,2048]{2,1,0:T(8,128)(2,1)} %get-tuple-element.257), channel_id=1, source_target_pairs={{0,8},{4,12},{8,0},{12,4},{16,24},{20,28},{24,16},{28,20},{1,9},{5... | collective-permute-start | bytes 3145736 | tf_op jit(solution)/shard_map/ppermute | solution.py:712
  375.9 34.3 %collective-permute-start.20 = (bf16[2,128,2048]{2,1,0:T(8,128)(2,1)}, bf16[2,128,2048]{2,1,0:T(8,128)(2,1)S(1)}, u32[]{:S(2)}, u32[]{:S(2)}) collective-permute-start(bf16[2,128,2048]{2,1,0:T(8,128)(2,1)} %get-tuple-element.259), channel_id=1, source_target_pairs={{0,16},{4,20},{8,24},{12,28},{16,0},{20,4},{24,8},{28,12},{1,17},{... | collective-permute-start | bytes 3145736 | tf_op jit(solution)/shard_map/ppermute | solution.py:712
  400.0 127.2 %all-reduce.7.cloned.1.call-start = ((), (), s32[]{:S(2)}) async-start(), calls=%async_computation.6 | async-start | bytes 2097152 | tf_op jit(solution)/shard_map/psum | solution.py:865
  408.7 53.1 %collective-permute-start.24 = (bf16[3,256,1024]{2,1,0:T(8,128)(2,1)}, bf16[3,256,1024]{2,1,0:T(8,128)(2,1)}, u32[]{:S(2)}, u32[]{:S(2)}) collective-permute-start(bf16[3,256,1024]{2,1,0:T(8,128)(2,1)} %norm_grad.4), channel_id=1, source_target_pairs={{1,0},{2,1},{3,2},{5,4},{6,5},{7,6},{9,8},{10,9},{11,10},{13,12},{... | collective-permute-start | bytes 4718600 | tf_op jit(solution)/shard_map/ppermute | solution.py:898
  416.6 21.1 %collective-permute-start.21 = (bf16[1,128,2048]{2,1,0:T(8,128)(2,1)}, bf16[1,128,2048]{2,1,0:T(8,128)(2,1)S(1)}, u32[]{:S(2)}, u32[]{:S(2)}) collective-permute-start(bf16[1,128,2048]{2,1,0:T(8,128)(2,1)} %get-tuple-element.261), channel_id=1, source_target_pairs={{0,16},{4,20},{8,24},{12,28},{16,0},{20,4},{24,8},{28,12},{1,17},{... | collective-permute-start | bytes 1572872 | tf_op jit(solution)/shard_map/ppermute | solution.py:712
  418.0 19.7 %collective-permute-start.22 = (bf16[1,128,2048]{2,1,0:T(8,128)(2,1)}, bf16[1,128,2048]{2,1,0:T(8,128)(2,1)S(1)}, u32[]{:S(2)}, u32[]{:S(2)}) collective-permute-start(bf16[1,128,2048]{2,1,0:T(8,128)(2,1)} %get-tuple-element.263), channel_id=1, source_target_pairs={{0,8},{4,12},{8,0},{12,4},{16,24},{20,28},{24,16},{28,20},{1,9},{5... | collective-permute-start | bytes 1572872 | tf_op jit(solution)/shard_map/ppermute | solution.py:712
  (49 other events, 246.9 us)
Sparse Core Ops, SparseCore 0:
  9.9 48.8 all-gather.4
  61.3 63.2 all-gather.6
  126.5 54.3 all-gather.8
  279.5 54.1 all-reduce.8
  353.3 46.6 reduce-scatter.1
  401.4 36.1 all-gather.10
  474.2 52.9 all-reduce.6

commit v3 on v2

--- a/solution.py
+++ b/solution.py
@@ -15,7 +15,7 @@
 HIGHEST = lax.Precision.HIGHEST
 MIB = 1 << 20
 COST = 30.0
-LIGHT = 1.0
+LIGHT = 0.0
 
 ERFC_P = 0.4375
 ERFC_C = (
@@ -83,7 +83,7 @@
         out_specs=pl.BlockSpec((1, qb, kw), lambda h: (h, 0, 0)),
         out_shape=jax.ShapeDtypeStruct((heads, qb, kw), F32),
         compiler_params=params(),
-        cost_estimate=cost(0, heads * qb * kw * 4),
+        cost_estimate=cost(0, heads * qb * kw * 4, 0.0),
         name="bias_table",
     )(row[:, None, :])
 
@@ -145,7 +145,7 @@
     o_ref[...] = jnp.where(pl.program_id(0) < scaled, out * 0.125, out) if scaled else out
 
 
-def project(x, w, first, cols, scaled, bn=256):
+def project(x, w, first, cols, scaled, bn=1024):
     tokens, model = x.shape
     return pl.pallas_call(
         functools.partial(proj_kernel, scaled // bn),
@@ -174,66 +174,69 @@
 
 def attn_fwd_kernel(qb, n, q_ref, *refs):
     bias_ref, mask_ref, o_ref, inv_ref, e_ref = refs[2 * n :]
-    k = jnp.concatenate([r[...] for r in refs[:n]], axis=0)
-    v = jnp.concatenate([r[...] for r in refs[n : 2 * n]], axis=0)
     blocks = q_ref.shape[0] // qb
     kw = bias_ref.shape[-1]
     even = lax.broadcasted_iota(jnp.int32, (qb, 128), 1) < 64
-    for b in range(blocks):
-        rows = slice(b * qb, (b + 1) * qb)
-        keys = slice(b * qb, b * qb + kw)
-        scores = dot_nt(split_pair(q_ref[rows], even), k[keys])
-        mask = mask_ref[0, b]
-        scores = jnp.concatenate(
-            [scores[:qb] + (bias_ref[0] + mask), scores[qb:] + (bias_ref[1] + mask)], axis=0
-        )
-        peak = jnp.max(scores, axis=-1, keepdims=True)
-        expo = jnp.exp(scores - peak)
-        inv = 1.0 / jnp.sum(expo, axis=-1, keepdims=True)
-        expo = expo.astype(BF16)
-        e_ref[0, 0, b] = expo
-        inv = join_pair(jnp.broadcast_to(inv, (2 * qb, 128)), even)
-        mixed = join_pair(dot_nn(expo, v[keys]), even)
-        inv_ref[rows] = inv
-        o_ref[rows] = (mixed * inv).astype(BF16)
-
-
-def key_specs(n, size, pairs, first):
-    near = [pl.BlockSpec((size, 128), lambda r, p: (r, p))] * (n - 1)
-    far = [pl.BlockSpec((size, 128), lambda r, p: (r, p + pairs))] * (n - 1)
-    return [
-        *near,
-        pl.BlockSpec((size, 128), lambda r, p: (r, p + first)),
-        *far,
-        pl.BlockSpec((size, 128), lambda r, p: (r, p + pairs + first)),
-    ]
+
+    @pl.loop(0, q_ref.shape[1] // 128)
+    def _(pair):
+        cols = pl.ds(pl.multiple_of(pair * 128, 128), 128)
+        k = jnp.concatenate([r[:, cols] for r in refs[:n]], axis=0)
+        v = jnp.concatenate([r[:, cols] for r in refs[n : 2 * n]], axis=0)
+        raw = [
+            dot_nt(split_pair(q_ref[b * qb : (b + 1) * qb, cols], even), k[b * qb : b * qb + kw]) for b in range(blocks)
+        ]
+        for b, scores in enumerate(raw):
+            rows = slice(b * qb, (b + 1) * qb)
+            keys = slice(b * qb, b * qb + kw)
+            mask = mask_ref[0, b]
+            scores = jnp.concatenate(
+                [scores[:qb] + (bias_ref[2 * pair] + mask), scores[qb:] + (bias_ref[2 * pair + 1] + mask)], axis=0
+            )
+            peak = jnp.max(scores, axis=-1, keepdims=True)
+            expo = jnp.exp(scores - peak)
+            inv = 1.0 / jnp.sum(expo, axis=-1, keepdims=True)
+            expo = expo.astype(BF16)
+            e_ref[0, pair, b] = expo
+            inv = join_pair(jnp.broadcast_to(inv, (2 * qb, 128)), even)
+            mixed = join_pair(dot_nn(expo, v[keys]), even)
+            inv_ref[rows, cols] = inv
+            o_ref[rows, cols] = (mixed * inv).astype(BF16)
+
+
+def key_specs(n, size, cols, model, begin):
+    def at(first):
+        return pl.BlockSpec((size, cols), lambda r: (r, (first + begin) // cols))
+
+    return [*[at(0)] * (n - 1), at(model), *[at(model)] * (n - 1), at(2 * model)]
 
 
 def attn_fwd(kvs, bias, mask):
     heads, qb, kw = bias.shape
     pairs = heads // 2
+    model = heads * 64
     rows, blocks = mask.shape[:2]
     size = blocks * qb
     n = len(kvs)
-    q_shape = (rows * size, heads * 64)
     cells = rows * blocks * heads * qb * kw
+    tile = pl.BlockSpec((size, model), lambda r: (r, 0))
     return pl.pallas_call(
         functools.partial(attn_fwd_kernel, qb, n),
-        grid=(rows, pairs),
+        grid=(rows,),
         in_specs=[
-            pl.BlockSpec((size, 128), lambda r, p: (r, p)),
-            *key_specs(n, size, pairs, pairs),
-            pl.BlockSpec((2, qb, kw), lambda r, p: (p, 0, 0)),
-            pl.BlockSpec((1, blocks, qb, kw), lambda r, p: (r, 0, 0, 0)),
+            tile,
+            *key_specs(n, size, model, model, 0),
+            pl.BlockSpec((heads, qb, kw), lambda r: (0, 0, 0), pipeline_mode=pl.Buffered(1)),
+            pl.BlockSpec((1, blocks, qb, kw), lambda r: (r, 0, 0, 0)),
         ],
         out_specs=[
-            pl.BlockSpec((size, 128), lambda r, p: (r, p)),
-            pl.BlockSpec((size, 128), lambda r, p: (r, p)),
-            pl.BlockSpec((1, 1, blocks, 2 * qb, kw), lambda r, p: (r, p, 0, 0, 0)),
+            tile,
+            tile,
+            pl.BlockSpec((1, pairs, blocks, 2 * qb, kw), lambda r: (r, 0, 0, 0, 0)),
         ],
         out_shape=[
-            jax.ShapeDtypeStruct(q_shape, BF16),
-            jax.ShapeDtypeStruct(q_shape, F32),
+            jax.ShapeDtypeStruct((rows * size, model), BF16),
+            jax.ShapeDtypeStruct((rows * size, model), F32),
             jax.ShapeDtypeStruct((rows, pairs, blocks, 2 * qb, kw), BF16),
         ],
         compiler_params=params(),
@@ -243,80 +246,83 @@
 
 
 def attn_bwd_kernel(qb, width, n, q_ref, *refs):
-    e_ref, inv_ref, o_ref, g_ref, dq_ref, dk_ref, dv_ref, diag_ref, sums, dk_acc, dv_acc = refs[2 * n :]
-    k = jnp.concatenate([r[...] for r in refs[:n]], axis=0)
-    v = jnp.concatenate([r[...] for r in refs[n : 2 * n]], axis=0)
+    e_ref, inv_ref, o_ref, g_ref = refs[2 * n : 2 * n + 4]
+    dq_ref, dk_ref, dv_ref, diag_ref, sums, dk_acc, dv_acc = refs[-7:]
     blocks = q_ref.shape[0] // qb
     kw = e_ref.shape[-1]
-    row, pair = pl.program_id(0), pl.program_id(1)
+    row = pl.program_id(0)
     even = lax.broadcasted_iota(jnp.int32, (qb, 128), 1) < 64
-    dk_acc[...] = jnp.zeros_like(dk_acc)
-    dv_acc[...] = jnp.zeros_like(dv_acc)
 
     @pl.when(row == 0)
     def _():
-        sums[pair] = jnp.zeros(sums.shape[1:], F32)
-
-    for b in range(blocks):
-        rows = slice(b * qb, (b + 1) * qb)
-        keys = slice(b * qb, b * qb + kw)
-        grad = (g_ref[rows].astype(F32) * inv_ref[rows]).astype(BF16)
-        weigh = grad.astype(F32) * o_ref[rows].astype(F32)
-        delta = jnp.sum(split_pair(weigh, even), axis=-1, keepdims=True)
-        grad = split_pair(grad, even)
-        expo = e_ref[0, 0, b]
-        dscore = expo.astype(F32) * (dot_nt(grad, v[keys]) - delta)
-        sums[pair] += dscore
-        dscore = dscore.astype(BF16)
-        dq_ref[rows] = (join_pair(dot_nn(dscore, k[keys]), even) * 0.125).astype(BF16)
-        dk_acc[:, keys] += dot_tn(split_pair(q_ref[rows], even), dscore)
-        dv_acc[:, keys] += dot_tn(grad, expo)
-
-    dk_ref[0] = dk_acc[...].astype(BF16)
-    dv_ref[0] = dv_acc[...].astype(BF16)
-
-    @pl.when(row == pl.num_programs(0) - 1)
-    def _():
-        diag_ref[0, 0:1] = diagonal_sums(sums[pair, :qb], width)
-        diag_ref[0, 1:2] = diagonal_sums(sums[pair, qb:], width)
-
-
-def attn_bwd(kvs, e, inv, o, g, width):
+        sums[...] = jnp.zeros_like(sums)
+
+    @pl.loop(0, q_ref.shape[1] // 128)
+    def _(pair):
+        cols = pl.ds(pl.multiple_of(pair * 128, 128), 128)
+        k = jnp.concatenate([r[:, cols] for r in refs[:n]], axis=0)
+        v = jnp.concatenate([r[:, cols] for r in refs[n : 2 * n]], axis=0)
+        dk_acc[...] = jnp.zeros_like(dk_acc)
+        dv_acc[...] = jnp.zeros_like(dv_acc)
+        for b in range(blocks):
+            rows = slice(b * qb, (b + 1) * qb)
+            keys = slice(b * qb, b * qb + kw)
+            grad = (g_ref[rows, cols].astype(F32) * inv_ref[rows, cols]).astype(BF16)
+            weigh = grad.astype(F32) * o_ref[rows, cols].astype(F32)
+            delta = jnp.sum(split_pair(weigh, even), axis=-1, keepdims=True)
+            grad = split_pair(grad, even)
+            expo = e_ref[0, pair, b]
+            dscore = expo.astype(F32) * (dot_nt(grad, v[keys]) - delta)
+            sums[pair] += dscore
+            dscore = dscore.astype(BF16)
+            dq_ref[rows, cols] = (join_pair(dot_nn(dscore, k[keys]), even) * 0.125).astype(BF16)
+            dk_acc[:, keys] += dot_tn(split_pair(q_ref[rows, cols], even), dscore)
+            dv_acc[:, keys] += dot_tn(grad, expo)
+        dk_ref[0, cols, :] = dk_acc[...].astype(BF16)
+        dv_ref[0, cols, :] = dv_acc[...].astype(BF16)
+
+        @pl.when(row == pl.num_programs(0) - 1)
+        def _():
+            diag_ref[pair, 0:1] = diagonal_sums(sums[pair, :qb], width)
+            diag_ref[pair, 1:2] = diagonal_sums(sums[pair, qb:], width)
+
+
+def attn_bwd(kvs, e, inv, o, g, width, begin, end, grads=()):
     rows, pairs, blocks, qb2, kw = e.shape
     qb = qb2 // 2
     size = blocks * qb
     n = len(kvs)
     window = n * size
     model = o.shape[1]
-    cells = e.size
+    count = end - begin
+    cols = count * 128
+    at = begin // count
+    share = e.size * count // pairs
+    tile = pl.BlockSpec((size, cols), lambda r: (r, at))
+    side = pl.BlockSpec((1, cols, window), lambda r: (r, at, 0))
     return pl.pallas_call(
         functools.partial(attn_bwd_kernel, qb, width, n),
-        grid=(rows, pairs),
+        grid=(rows,),
         in_specs=[
-            pl.BlockSpec((size, 128), lambda r, p: (r, p)),
-            *key_specs(n, size, pairs, pairs),
-            pl.BlockSpec((1, 1, blocks, qb2, kw), lambda r, p: (r, p, 0, 0, 0)),
-            pl.BlockSpec((size, 128), lambda r, p: (r, p)),
-            pl.BlockSpec((size, 128), lambda r, p: (r, p)),
-            pl.BlockSpec((size, 128), lambda r, p: (r, p)),
-        ],
-        out_specs=[
-            pl.BlockSpec((size, 128), lambda r, p: (r, p)),
-            pl.BlockSpec((1, 128, window), lambda r, p: (r, p, 0)),
-            pl.BlockSpec((1, 128, window), lambda r, p: (r, p, 0)),
-            pl.BlockSpec((1, 8, width), lambda r, p: (p, 0, 0)),
-        ],
+            tile,
+            *key_specs(n, size, cols, model, begin * 128),
+            pl.BlockSpec((1, count, blocks, qb2, kw), lambda r: (r, at, 0, 0, 0)),
+            *[tile] * 3,
+            *[pl.BlockSpec(memory_space=pl.ANY)] * len(grads),
+        ],
+        out_specs=[tile, side, side, pl.BlockSpec((count, 8, width), lambda r: (at, 0, 0))],
         out_shape=[
             jax.ShapeDtypeStruct(o.shape, BF16),
             jax.ShapeDtypeStruct((rows, model, window), BF16),
             jax.ShapeDtypeStruct((rows, model, window), BF16),
             jax.ShapeDtypeStruct((pairs, 8, width), F32),
         ],
-        scratch_shapes=[pltpu.VMEM((pairs, qb2, kw), F32)] + [pltpu.VMEM((128, window), F32)] * 2,
+        scratch_shapes=[pltpu.VMEM((count, qb2, kw), F32)] + [pltpu.VMEM((128, window), F32)] * 2,
+        input_output_aliases={1 + 2 * n + 4 + i: i for i in range(len(grads))},
         compiler_params=params(),
-        cost_estimate=cost(cells * 512, cells * 4),
+        cost_estimate=cost(share * 512, share * 4),
         name="attn_bwd",
-    )(kvs[-1], *kvs, *kvs, e, inv, o, g)
+    )(kvs[-1], *kvs, *kvs, e, inv, o, g, *grads)
 
 
 def middle_kernel(order_ref, a_ref, w_ref, x_ref, gain_ref, shift_ref, mid_ref, norm_ref, turned_ref, mixed_ref, scratch):
@@ -477,13 +483,17 @@
     )(chips, n2, n2t, cot, acc, gin, w, b_up, w, w, b_down, *grads)
 
 
-def norm_back(field, gain, e):
+def standard(field):
     centre = field - jnp.mean(field, axis=-1, keepdims=True)
     rate = lax.rsqrt(jnp.mean(centre * centre, axis=-1, keepdims=True) + EPS)
-    n = centre * rate
+    return centre * rate, rate
+
+
+def norm_back(field, gain, e):
+    n, rate = standard(field)
     eg = e * gain
     grad = rate * (eg - jnp.mean(eg, axis=-1, keepdims=True) - n * jnp.mean(eg * n, axis=-1, keepdims=True))
-    return grad, jnp.sum(e * n, axis=0, keepdims=True), jnp.sum(e, axis=0, keepdims=True)
+    return grad, n
 
 
 def middle_back_kernel(gn_ref, mid_ref, cot_ref, w_ref, gain_ref, gm_ref, gb_ref, ga_ref, gg_ref, gs_ref):
@@ -492,9 +502,10 @@
         gg_ref[...] = jnp.zeros_like(gg_ref)
         gs_ref[...] = jnp.zeros_like(gs_ref)
 
-    grad, gg, gs = norm_back(mid_ref[...], gain_ref[...], gn_ref[...])
-    gg_ref[...] += gg
-    gs_ref[...] += gs
+    e = gn_ref[...]
+    grad, n = norm_back(mid_ref[...], gain_ref[...], e)
+    gg_ref[...] += jnp.sum(e * n, axis=0, keepdims=True)
+    gs_ref[...] += jnp.sum(e, axis=0, keepdims=True)
     grad = cot_ref[...].astype(F32) + grad
     gm_ref[...] = grad
     branch = grad.astype(BF16)
@@ -526,26 +537,39 @@
 
 def attn_weights_kernel(n, *refs):
     turned = refs[:n]
-    at_ref, dq_ref, dk_ref, dv_ref, gb_ref, first_ref, last_ref = refs[n:]
+    at_ref, dq_ref, dk_ref, dv_ref, gb_ref, small_ref = refs[n : n + 6]
+    sends, keeps = refs[n + 6 : n + 8], refs[n + 8 :]
     model = gb_ref.shape[1]
     rows, _, size = turned[0].shape
-    half, part = first_ref.shape[:2]
-
-    def store(ref, side, value):
-        ref[:, :, side * model : (side + 1) * model] = value.astype(BF16).reshape(half, part, model)
+    half = sends[0].shape[0]
+    part = sends[1].shape[1]
+
+    def store(field, side, value):
+        value = value.astype(BF16).reshape(half, part, model)
+        for step, outs in enumerate((sends, keeps)):
+
+            @pl.when(pl.program_id(0) == step)
+            def _():
+                outs[field][:, :part, side * model : (side + 1) * model] = value
 
     def over_window(ref):
         return sum(
             dot_nt(turned[b][r], ref[r, :, b * size : (b + 1) * size]) for r in range(rows) for b in range(n)
         )
 
-    store(first_ref, 0, sum(dot_nn(turned[-1][r], dq_ref[r]) for r in range(rows)))
-    store(first_ref, 1, over_window(dk_ref))
-    store(last_ref, 0, over_window(dv_ref))
-    store(last_ref, 1, dot_nn(at_ref[...], gb_ref[...]))
-
-
-def attn_weights(side, turned, mixed, dq, dk, dv, branch, shards):
+    for step, outs in enumerate((sends, keeps)):
+
+        @pl.when(pl.program_id(0) == step)
+        def _():
+            outs[0][:, part:, :] = small_ref[...]
+
+    store(0, 0, sum(dot_nn(turned[-1][r], dq_ref[r]) for r in range(rows)))
+    store(0, 1, over_window(dk_ref))
+    store(1, 0, over_window(dv_ref))
+    store(1, 1, dot_nn(at_ref[...], gb_ref[...]))
+
+
+def attn_weights(turned, mixed, dq, dk, dv, branch, small, shards):
     rows, model, size = turned[0].shape
     tokens = branch.shape[0]
     n = len(turned)
@@ -554,95 +578,103 @@
     part = model // shards
 
     def full(*shape):
-        return pl.BlockSpec(shape, lambda i: (0,) * len(shape))
-
-    out = jax.ShapeDtypeStruct((half, part, 2 * model), BF16)
+        return pl.BlockSpec(shape, lambda i: (0,) * len(shape), pipeline_mode=pl.Buffered(1))
+
+    large = n * rows > 32
+    buffers = pl.Buffered(1 if large else 2)
+    shapes = [(half, part + small.shape[1], 2 * model), (half, part, 2 * model)] * 2
     return pl.pallas_call(
         functools.partial(attn_weights_kernel, n),
-        grid=(1,),
+        grid=(2,),
         in_specs=[
-            *[pl.BlockSpec((rows, model // 2, size), lambda i: (0, side, 0))] * n,
-            pl.BlockSpec((model // 2, tokens), lambda i: (side, 0)),
+            *[pl.BlockSpec((rows, model // 2, size), lambda i: (0, i, 0), pipeline_mode=buffers)] * n,
+            pl.BlockSpec((model // 2, tokens), lambda i: (i, 0), pipeline_mode=buffers),
             full(rows, size, model),
             full(rows, model, window),
             full(rows, model, window),
             full(tokens, model),
-        ],
-        out_specs=[full(half, part, 2 * model)] * 2,
-        out_shape=[out, out],
-        compiler_params=params(),
-        cost_estimate=cost(2 * model * model * (tokens + rows * window), 2 * (4 * rows * model * window + 4 * model * model), COST if side else LIGHT),
+            pl.BlockSpec((half, *small.shape[1:]), lambda i: (i, 0, 0)),
+        ],
+        out_specs=[pl.BlockSpec(shape, lambda i: (0, 0, 0)) for shape in shapes],
+        out_shape=[jax.ShapeDtypeStruct(shape, BF16) for shape in shapes],
+        compiler_params=params(60 if large else 56),
+        cost_estimate=cost(4 * model * model * (tokens + rows * window), 8 * rows * model * window + 16 * model * model, LIGHT),
         name="attn_weights",
-    )(*turned, mixed, dq.reshape(rows, size, model), dk, dv, branch)
-
-
-def norm_grad_kernel(own, dk_ref, dv_ref, w_ref, *refs):
+    )(*turned, mixed, dq.reshape(rows, size, model), dk, dv, branch, small)
+
+
+def norm_grad_kernel(n, dq_ref, dk_ref, dv_ref, w_ref, *refs):
     model = w_ref.shape[0]
-    out_ref = refs[-1]
-    grad = dot_nn(w_ref[:, model : 2 * model], dk_ref[0]) + dot_nn(w_ref[:, 2 * model :], dv_ref[0])
-    if own:
-        out_ref[0] = grad.T + dot_nt(refs[0][0], w_ref[:, :model])
-    elif len(refs) == 2:
-        out_ref[0] = (grad.T + refs[0][0].astype(F32)).astype(BF16)
-    else:
-        out_ref[0] = grad.astype(BF16).T
-
-
-def norm_grad(dk, dv, w_attn, block, size, dq=None, carry=None):
-    rows, model, window = dk.shape
-    tile = pl.BlockSpec((1, size, model), lambda r: (r, 0, 0))
-    if size % 128 == 0 or size == window:
-        side = pl.BlockSpec((1, model, size), lambda r: (r, 0, block))
-    else:
-        side = pl.BlockSpec((1, model, size), lambda r: (r, 0, 0))
-        dk, dv = (lax.slice_in_dim(d, block * size, (block + 1) * size, axis=2) for d in (dk, dv))
-    more = [x.reshape(rows, size, model) for x in (dq, carry) if x is not None]
-    return pl.pallas_call(
-        functools.partial(norm_grad_kernel, dq is not None),
-        grid=(rows,),
-        in_specs=[
-            side,
-            side,
-            pl.BlockSpec((model, 3 * model), lambda r: (0, 0), pipeline_mode=pl.Buffered(1)),
-            *[tile] * len(more),
-        ],
-        out_specs=tile,
-        out_shape=jax.ShapeDtypeStruct((rows, size, model), F32 if dq is not None else BF16),
-        compiler_params=params(),
-        cost_estimate=cost((6 if dq is not None else 4) * rows * model * model * size, rows * model * size * 8 + 6 * model * model, LIGHT),
-        name="norm_grad",
-    )(dk, dv, w_attn, *more)
-
-
-def first_back_kernel(dn_ref, back_ref, x_ref, gm_ref, gain_ref, out_ref, gg_ref, gs_ref):
+    near, far, (own_ref, gg_ref, gs_ref) = refs[:n], refs[n : 2 * n - 1], refs[2 * n - 1 :]
+    size = own_ref.shape[1]
+
     @pl.when(pl.program_id(0) == 0)
     def _():
         gg_ref[...] = jnp.zeros_like(gg_ref)
         gs_ref[...] = jnp.zeros_like(gs_ref)
 
+    for b in range(n):
+        side = slice(b * size, (b + 1) * size)
+        grad = dot_nn(w_ref[:, model : 2 * model], dk_ref[0, :, side])
+        grad = (grad + dot_nn(w_ref[:, 2 * model :], dv_ref[0, :, side])).T
+        if b == n - 1:
+            grad += dot_nt(dq_ref[0], w_ref[:, :model])
+            own_ref[0] = grad
+        else:
+            far[b][0] = grad.astype(BF16)
+        normed, _ = standard(near[b][0].astype(F32))
+        gg_ref[...] += jnp.sum(grad * normed, axis=0, keepdims=True)
+        gs_ref[...] += jnp.sum(grad, axis=0, keepdims=True)
+
+
+def norm_grad(dq, dk, dv, w_attn, near):
+    rows, model, window = dk.shape
+    n = len(near)
+    size = window // n
+    tile = pl.BlockSpec((1, size, model), lambda r: (r, 0, 0))
+    line = pl.BlockSpec((1, model), lambda r: (0, 0))
+    side = pl.BlockSpec((1, model, window), lambda r: (r, 0, 0))
+    shape = (rows, size, model)
+    return pl.pallas_call(
+        functools.partial(norm_grad_kernel, n),
+        grid=(rows,),
+        in_specs=[
+            tile,
+            side,
+            side,
+            pl.BlockSpec((model, 3 * model), lambda r: (0, 0), pipeline_mode=pl.Buffered(1)),
+            *[tile] * n,
+        ],
+        out_specs=[*[tile] * n, line, line],
+        out_shape=[
+            *[jax.ShapeDtypeStruct(shape, BF16)] * (n - 1),
+            jax.ShapeDtypeStruct(shape, F32),
+            jax.ShapeDtypeStruct((1, model), F32),
+            jax.ShapeDtypeStruct((1, model), F32),
+        ],
+        compiler_params=params(),
+        cost_estimate=cost(2 * rows * model * model * (size + 2 * window), rows * model * window * 8 + 6 * model * model),
+        name="norm_grad",
+    )(dq.reshape(shape), dk, dv, w_attn, *[x.reshape(shape) for x in near])
+
+
+def first_back_kernel(dn_ref, back_ref, x_ref, gm_ref, gain_ref, out_ref):
     e = dn_ref[...] + back_ref[...].astype(F32)
-    grad, gg, gs = norm_back(x_ref[...].astype(F32), gain_ref[...], e)
-    gg_ref[...] += gg
-    gs_ref[...] += gs
+    grad, _ = norm_back(x_ref[...].astype(F32), gain_ref[...], e)
     out_ref[...] = (gm_ref[...] + grad).astype(BF16)
 
 
 def first_back(dn, back, x, gm, gain, bm):
     tokens, model = x.shape
     tile = pl.BlockSpec((bm, model), lambda i: (i, 0))
-    line = pl.BlockSpec((1, model), lambda i: (0, 0))
     return pl.pallas_call(
         first_back_kernel,
         grid=(tokens // bm,),
-        in_specs=[tile, tile, tile, tile, line],
-        out_specs=[tile, line, line],
-        out_shape=[
-            jax.ShapeDtypeStruct((tokens, model), BF16),
-            jax.ShapeDtypeStruct((1, model), F32),
-            jax.ShapeDtypeStruct((1, model), F32),
-        ],
+        in_specs=[tile, tile, tile, tile, pl.BlockSpec((1, model), lambda i: (0, 0))],
+        out_specs=tile,
+        out_shape=jax.ShapeDtypeStruct((tokens, model), BF16),
         compiler_params=params(),
-        cost_estimate=cost(20 * tokens * model, tokens * model * 14),
+        cost_estimate=cost(20 * tokens * model, tokens * model * 14, 0.0),
         name="first_back",
     )(dn, back, x, gm, gain)
 
@@ -665,7 +697,7 @@
     ins, in_specs, out_shape, out_specs = [], [], [], []
     count = pairs[0][0].shape[0]
     half = max(count // 2, 1)
-    tiles = 4
+    tiles = 2
     for (a, b), back in zip(pairs, backwards):
         _, rows, cols = a.shape
         shape = (1, rows // tiles, cols)
@@ -850,12 +882,8 @@
         middle, jnp.zeros((8, model), F32), w_ff[0], bias_a, begin=0, end=pairs, first=True, last=False
     )
     sum_a = ShardSum([us, ds], [uk, dk], shards)
-    part_out, part_grad, *grads = ffn(
-        part_out, part_grad, w_ff[1], bias_b, begin=0, end=pairs // 2, first=False, last=False
-    )
-    part_grad = sum_a.step(part_grad)
     outputs, grad_norm2, us, uk, ds, dk, grad_b_b = ffn(
-        part_out, part_grad, w_ff[1], bias_b, begin=pairs // 2, end=pairs, first=False, last=True, grads=grads
+        part_out, part_grad, w_ff[1], bias_b, begin=0, end=pairs, first=False, last=True
     )
     sum_b = ShardSum([us, ds], [uk, dk], shards)
     grad_b_up = jnp.stack([grad_b_a.reshape(shards, fine), grad_b_b.reshape(shards, fine)], axis=1)
@@ -864,43 +892,62 @@
     def total(fields):
         return lax.psum(tuple(fields), "seq")
 
-    if sum_a.stage < len(sum_a.bits):
-        grad_norm2 = sum_a.step(grad_norm2)
+    grad_norm2 = sum_a.step(grad_norm2)
     grad_middle, grad_branch, grad_attended, grad_gain2, grad_shift2 = middle_back(
         grad_norm2, middle, cot, w_ff[0], gain2, tile
     )
-    grad_attended = sum_b.step(grad_attended)
-    done_a = sum_a.finish()
-    grad_attended, done_a = lax.optimization_barrier((grad_attended, done_a))
+    backward = functools.partial(attn_bwd, kvs, expo, inv, attended)
+    half = heads // 4
+    grads = backward(grad_attended, width, 0, half)
+    if sum_a.stage < len(sum_a.bits):
+        grad_attended, grads, sum_b.flying = sum_a.step(grad_attended, grads, sum_b.flying)
+    landed, sum_a.flying = lax.optimization_barrier((sum_b.land(), sum_a.flying))
+    sum_b.launch(landed)
+    done_a, grad_attended, grads = lax.optimization_barrier((sum_a.finish(), grad_attended, grads))
+    grads = backward(grad_attended, width, half, heads // 2, grads)
+    if sum_b.stage < len(sum_b.bits):
+        grads = sum_b.step(grads)
     total_a = total(done_a)
-    grad_q, grad_k, grad_v, diagonal = attn_bwd(kvs, expo, inv, attended, grad_attended, width)
-    if sum_b.stage < len(sum_b.bits):
-        grad_q = sum_b.step(grad_q)
+    grad_q, grad_k, grad_v, diagonal = grads
     back = None
     down = [(i + 1, i) for i in range(ranges - 1)]
-    if hops:
-        grad_far = norm_grad(grad_k, grad_v, w_attn, 0, size)
-        grad_far, grad_q = lax.optimization_barrier((grad_far, grad_q))
-        back = lax.ppermute(grad_far, "seq", down)
-    first_send, last_send = attn_weights(0, turned, mixed_turned, grad_q, grad_k, grad_v, grad_branch, shards)
-    done_b = sum_b.finish()
-    done_b, grad_q, first_send, total_a = lax.optimization_barrier((done_b, grad_q, first_send, total_a))
-    up_b, down_b = done_b
+    up_b, down_b = sum_b.finish()
     total_b = jnp.concatenate([*jnp.split(up_b, up_b.shape[1] // model, axis=1), down_b], axis=0)
     total_b = lax.psum_scatter(total_b, "seq", scatter_dimension=0, tiled=True)
     total_b = lax.all_gather(total_b, "seq", axis=0, tiled=True)
-    first_keep, last_keep = attn_weights(1, turned, mixed_turned, grad_q, grad_k, grad_v, grad_branch, shards)
+    *far, grad_own, grad_gain1, grad_shift1 = norm_grad(grad_q, grad_k, grad_v, w_attn, near)
+    if hops:
+        back = lax.ppermute(far[0], "seq", down)
+    diagonal = diagonal[:, :2].reshape(heads, width)
+    grad_table = lax.dot_general(onehot.astype(F32), diagonal, (((0,), (1,)), ((), ())), precision=HIGHEST)
+    small = (grad_gain1, grad_shift1, grad_gain2, grad_shift2, grad_b_up, grad_b_down, grad_table)
+    small = jnp.concatenate([f.reshape(shards, -1) for f in small], axis=1).astype(BF16)
+    small_cols = -(-small.shape[1] // (2 * model)) * 2 * model
+    small = jnp.pad(small, ((0, 0), (0, small_cols - small.shape[1]))).reshape(shards, -1, 2 * model)
+    small = jnp.pad(small, ((0, 0), (0, 16 - small.shape[1]), (0, 0)))
+    small = jnp.take(small, order, axis=0)
+    grad_q, grad_own = lax.optimization_barrier((grad_q, grad_own))
+    first_send, last_send, first_keep, last_keep = attn_weights(
+        turned, mixed_turned, grad_q, grad_k, grad_v, grad_branch, small, shards
+    )
+    for hop in range(1, hops):
+        pieces = [(far[hop].reshape(1, tokens, model), back.reshape(1, tokens, model))]
+        back = merge(pieces, [False], True)[0].reshape(rows, size, model)
+        if hop < hops - 1:
+            back = lax.ppermute(back, "seq", down)
+    first_send, last_send, total_a, back = lax.optimization_barrier((first_send, last_send, total_a, back))
+    if hops > 1:
+        back = lax.ppermute(back, "seq", down)
     sum_c = ShardSum([first_send, last_send], [first_keep, last_keep], shards)
-    grad_k, grad_v, grad_q = sum_c.step(grad_k, grad_v, grad_q)
-    for hop in range(1, hops):
-        grad_far = norm_grad(grad_k, grad_v, w_attn, hop, size, carry=back)
-        grad_far, grad_q = lax.optimization_barrier((grad_far, grad_q))
-        back = lax.ppermute(grad_far, "seq", down)
-    grad_q, total_b = lax.optimization_barrier((grad_q, total_b))
-    grad_own = norm_grad(grad_k, grad_v, w_attn, hops, size, dq=grad_q)
+    while sum_c.stage < len(sum_c.bits):
+        sum_c.launch(sum_c.land())
+    sum_c.flying, total_b = lax.optimization_barrier((sum_c.flying, total_b))
     done_c = sum_c.finish()
-    done_c, total_b, grad_own = lax.optimization_barrier((done_c, total_b, grad_own))
-    grad_first, grad_last = (f.astype(F32) for f in total(done_c))
+    total_c = total(done_c)
+    (grad_own, total_b), _ = lax.optimization_barrier(((grad_own, total_b), done_c))
+    if back is None:
+        back = jnp.zeros((rows, size, model), BF16)
+    input_grad = first_back(grad_own.reshape(tokens, model), back.reshape(tokens, model), x, grad_middle, gain1, tile)
     up_a, down_a = (f.astype(F32) for f in total_a)
     total_b = total_b.astype(F32)
     count = up_b.shape[0] * (up_b.shape[1] // model)
@@ -908,19 +955,9 @@
     down_b = total_b[count:]
     grad_w_up = jnp.stack([up_a.reshape(-1, shards, fine), up_b.reshape(-1, shards, fine)], axis=2).reshape(w_up.shape)
     grad_w_down = jnp.concatenate([down_a, down_b], axis=0)
-    if back is None:
-        back = jnp.zeros((rows, size, model), BF16)
-    input_grad, grad_gain1, grad_shift1 = first_back(
-        grad_own.reshape(tokens, model), back.reshape(tokens, model), x, grad_middle, gain1, tile
-    )
-
-    diagonal = diagonal[:, :2].reshape(heads, width)
-    grad_table = lax.dot_general(onehot.astype(F32), diagonal, (((0,), (1,)), ((), ())), precision=HIGHEST)
-
-    small = (grad_gain1, grad_shift1, grad_gain2, grad_shift2, grad_b_up, grad_b_down, grad_table)
-    small = jnp.concatenate([s.reshape(shards, -1) for s in small], axis=1)
-    small = add_everywhere(small, (("fsdp", shards), ("seq", ranges)))
-    small = lax.dynamic_slice_in_dim(small, lax.axis_index("fsdp"), 1, 0)[0]
+    part = model // shards
+    small = total_c[0][part:].astype(F32).reshape(-1)
+    grad_first, grad_last = total_c[0][:part].astype(F32), total_c[1].astype(F32)
     finals, at = [], 0
     for v in vectors:
         finals.append(small[at : at + v.size].reshape(v.shape))

time: 547 us -> 522 us (0.954)
  Pallas kernels: 329 us -> 287 us
  waiting for transfers between devices: 104 us -> 124 us
  other arithmetic: 12.7 us -> 19.4 us
    ppermute x12, waiting for transfers between devices: 3.27 us -> 20.1 us  [launch(): self.flying.append((kept, flip('fsdp', self.shards, 1 << bit)(sent)))]
    pallas_call x6 -> x3, Pallas kernels: 86.7 us -> 73.7 us  [the longest x1 29.4 us: attn_fwd(): pl.pallas_call(functools.partial(attn_fwd_kernel, qb, n), grid=(rows,), i...]
    pallas_call x3 -> x2, Pallas kernels: 81 us -> 70.1 us  [ffn_block(): pl.pallas_call(functools.partial(ffn_kernel, bm, first, last), grid_spec=...]
    ppermute x8 -> x3, waiting for transfers between devices: 12.8 us -> 3.61 us  [add_everywhere(): field = field + flip(axis, count, bit)(field)]
    reduce_scatter x1, waiting for transfers between devices: 23.2 us -> 14.8 us  [per_device(): total_b = lax.psum_scatter(total_b, 'seq', scatter_dimension=0, tiled=True)]
    pallas_call x9 -> x10, Pallas kernels: 46.3 us -> 38.2 us  [merge(): pl.pallas_call(functools.partial(merge_kernel, len(out_shape)), grid=(hal...]
    pallas_call x3, Pallas kernels: 30.9 us -> 22.8 us  [project(): pl.pallas_call(functools.partial(proj_kernel, scaled // bn), grid=(cols /...]
    psum x2, waiting for transfers between devices: 31.5 us -> 39.2 us  [total(): return lax.psum(tuple(fields), 'seq')]
  transfers between devices with their start and end apart: 37 -> 32, of which waited for: 16 -> 16; matrix products, arithmetic and copies ran while one was open for 6% -> 7% of each run, Pallas kernels for 57% -> 55%
where the time goes in v3:
time: 522 us; the launch traced here: 515 us
  Pallas kernels  287 us (55%)
  waiting for transfers between devices  124 us (24%)
  local copies, waits for them, and re-layouts  34.7 us (7%)
  starting transfers between devices  34 us (7%)
  other arithmetic  19.4 us (4%)
  between operations  15.3 us (3%)
    pallas_call x2, Pallas kernels, ffn_block(): pl.pallas_call(functools.partial(ffn_kernel, bm, first, last), grid_spec=...  70.1 us
    psum x2, waiting for transfers between devices, total(): return lax.psum(tuple(fields), 'seq')  39.2 us
    pallas_call x10, Pallas kernels, merge(): pl.pallas_call(functools.partial(merge_kernel, len(out_shape)), grid=(hal...  38.2 us
    pallas_call x2, Pallas kernels, attn_bwd(): pl.pallas_call(functools.partial(attn_bwd_kernel, qb, width, n), grid=(ro...  32.2 us
    pallas_call x1, Pallas kernels, attn_fwd(): pl.pallas_call(functools.partial(attn_fwd_kernel, qb, n), grid=(rows,), i...  29.4 us
    pallas_call x1, Pallas kernels, attn_weights(): pl.pallas_call(functools.partial(attn_weights_kernel, n), grid=(2,), in_s...  24.6 us
    pallas_call x3, Pallas kernels, project(): pl.pallas_call(functools.partial(proj_kernel, scaled // bn), grid=(cols /...  22.8 us
    all_gather x1, waiting for transfers between devices, per_device(): total_b = lax.all_gather(total_b, 'seq', axis=0, tiled=True)  20.9 us
  transfers between devices with their start and end apart: 32, of which 16 were waited for; matrix products, arithmetic and copies ran while one was open for 7% of the time, Pallas kernels for 55%

profile of v3, /device:TPU:0, one launch (start us, length us, event | category | flops | bytes accessed | tf_op | source)
XLA Modules:
  0.0 515.2 jit_solution(719009722808808021)
XLA Ops:
  38.6 11.7 %bias_table.1.refs_6_ = f32[16,128,640]{2,1,0:T(8,128)} custom-call(f32[16,1,768]{2,1,0:T(1,128)} %broadcast_in_dim.75.row_ref), custom_call_target="tpu_custom_call" | custom-call | tf_op jit(solution)/shard_map/bias_table/pallas_call | solution.py:79
  57.7 6.2 %collective-permute-start.4 = (bf16[3,256,1024]{2,1,0:T(8,128)(2,1)}, bf16[3,256,1024]{2,1,0:T(8,128)(2,1)}, u32[]{:S(2)}, u32[]{:S(2)}) collective-permute-start(bf16[3,256,1024]{2,1,0:T(8,128)(2,1)} %collective-permute-done.x_ref.refs_1_), channel_id=1, source_target_pairs={{0,1},{1,2},{2,3},{4,5},{5,6},{6,7},{8,9},{9,10},{10,11},{12,13},{... | collective-permute-start | bytes 4718600 | tf_op jit(solution)/shard_map/ppermute | solution.py:862
  74.0 9.0 %project.4.q_ref.refs_2_.refs_5_ = bf16[768,3072]{1,0:T(8,128)(2,1)} custom-call(bf16[768,1024]{1,0:T(8,128)(2,1)} %bitcast.127, bf16[1024,3072]{1,0:T(8,128)(2,1)} %all-gather.5.cloned.1.call-done.w_ref), custom_call_target="tpu_custom_call" | custom-call | flops 144955146240 | bytes 377487360 | tf_op jit(solution)/shard_map/project/pallas_call | solution.py:150
  82.9 6.8 %project.3.refs_1_.refs_4_ = bf16[768,2048]{1,0:T(8,128)(2,1)} custom-call(bf16[768,1024]{1,0:T(8,128)(2,1)} %bitcast.128, bf16[1024,3072]{1,0:T(8,128)(2,1)} %all-gather.5.cloned.1.call-done.w_ref), custom_call_target="tpu_custom_call" | custom-call | flops 96636764160 | bytes 267386880 | tf_op jit(solution)/shard_map/project/pallas_call | solution.py:150
  89.8 6.3 %collective-permute-done.4.x_ref.refs_0_ = bf16[3,256,1024]{2,1,0:T(8,128)(2,1)} collective-permute-done((bf16[3,256,1024]{2,1,0:T(8,128)(2,1)}, bf16[3,256,1024]{2,1,0:T(8,128)(2,1)}, u32[]{:S(2)}, u32[]{:S(2)}) %collective-permute-start.4) | collective-permute-done | bytes 1572896 | tf_op jit(solution)/shard_map/ppermute | solution.py:862
  101.1 7.0 %project.5.refs_0_.refs_3_ = bf16[768,2048]{1,0:T(8,128)(2,1)} custom-call(bf16[768,1024]{1,0:T(8,128)(2,1)} %bitcast.129, bf16[1024,3072]{1,0:T(8,128)(2,1)} %all-gather.5.cloned.1.call-done.w_ref), custom_call_target="tpu_custom_call" | custom-call | flops 96636764160 | bytes 267386880 | tf_op jit(solution)/shard_map/project/pallas_call | solution.py:150
  108.1 29.4 %attn_fwd.1 = (bf16[768,1024]{1,0:T(8,128)(2,1)}, f32[768,1024]{1,0:T(8,128)}, bf16[3,8,2,256,640]{4,3,2,1,0:T(8,128)(2,1)}) custom-call(bf16[768,3072]{1,0:T(8,128)(2,1)} %project.4.q_ref.refs_2_.refs_5_, bf16[768,2048]{1,0:T(8,128)(2,1)} %project.5.refs_0_.refs_3_, bf16[768,2048]{1,0:T(8,128)(2,1)} %project.3.refs_1_.refs_4_, ...), custom_call_target="tpu_custom_call" | custom-call | flops 60397977600 | bytes 943718400 | tf_op jit(solution)/shard_map/attn_fwd/pallas_call | solution.py:223
  137.5 7.7 %middle_block.1 = (f32[768,1024]{1,0:T(8,128)}, bf16[768,1024]{1,0:T(8,128)(2,1)}, bf16[1024,768]{1,0:T(8,128)(2,1)}, bf16[1024,768]{1,0:T(8,128)(2,1)}) custom-call(s32[8]{0:T(128)} %broadcast_xor_fusion.order_ref, bf16[768,1024]{1,0:T(8,128)(2,1)} %get-tuple-element.173.a_ref.refs_8_, ...), custom_call_target="tpu_custom_call" | custom-call | flops 48318382080 | bytes 393216000 | tf_op jit(solution)/shard_map/middle_block/pallas_call | solution.py:352
  145.8 34.8 %ffn_block.2 = (f32[768,1024]{1,0:T(8,128)}, f32[768,1024]{1,0:T(8,128)}, bf16[4,128,2048]{2,1,0:T(8,128)(2,1)}, bf16[4,128,2048]{2,1,0:T(8,128)(2,1)}, bf16[4,2...) custom-call(s32[5]{0:T(128)} %pad_add_fusion.chip_ref, ...), custom_call_target="tpu_custom_call" | custom-call | flops 579820584960 | bytes 975175680 | tf_op jit(solution)/shard_map/ffn_block/pallas_call | solution.py:432
  181.2 35.3 %ffn_block.3 = (bf16[768,1024]{1,0:T(8,128)(2,1)}, f32[768,1024]{1,0:T(8,128)}, bf16[4,128,2048]{2,1,0:T(8,128)(2,1)}, bf16[4,128,2048]{2,1,0:T(8,128)(2,1)}, bf...) custom-call(s32[5]{0:T(128)} %pad_add_fusion.chip_ref, ...), custom_call_target="tpu_custom_call" | custom-call | flops 579820584960 | bytes 975175680 | tf_op jit(solution)/shard_map/ffn_block/pallas_call | solution.py:432
  217.1 5.8 %merge.10 = (bf16[2,128,2048]{2,1,0:T(8,128)(2,1)}, bf16[2,128,2048]{2,1,0:T(8,128)(2,1)}, bf16[2,256,1024]{2,1,0:T(8,128)(2,1)}, bf16[2,256,1024]{2,1,0:T(8,128)(2,1)}) custom-call(bf16[4,128,2048]{2,1,0:T(8,128)(2,1)} %get-tuple-element.183.refs_0_.refs_2_, bf16[4,128,2048]{2,1,0:T(8,128)(2,1)} %collective-permute-done.5.refs_1_.refs_3_, ...), custom_call_target="tpu_custom_call" | custom-call | tf_op jit(solution)/shard_map/merge/pallas_call | solution.py:716
  225.9 9.1 %middle_back.1 = (f32[768,1024]{1,0:T(8,128)}, bf16[768,1024]{1,0:T(8,128)(2,1)}, bf16[768,1024]{1,0:T(8,128)(2,1)}, f32[1,1024]{1,0:T(1,128)}, f32[1,1024]{1,0:T(1,128)}) custom-call(f32[768,1024]{1,0:T(8,128)} %get-tuple-element.200.gn_ref, f32[768,1024]{1,0:T(8,128)} %get-tuple-element.179.acc_ref.mid_ref, bf16[768,1024]{1,0:T(8,128)(2,1)} %bitcast.93, ...), custom_call_target="tpu_custom_call" | custom-call | flops 48318382080 | bytes 487587840 | tf_op jit(solution)/shard_map/middle_back/pallas_call | solution.py:520
  235.0 16.1 %attn_bwd.2 = (bf16[768,1024]{1,0:T(8,128)(2,1)}, bf16[3,1024,768]{2,1,0:T(8,128)(2,1)}, bf16[3,1024,768]{2,1,0:T(8,128)(2,1)}, f32[8,8,768]{2,1,0:T(8,128)}) custom-call(bf16[768,3072]{1,0:T(8,128)(2,1)} %project.4.q_ref.refs_2_.refs_5_, bf16[768,2048]{1,0:T(8,128)(2,1)} %project.5.refs_0_.refs_3_, bf16[768,2048]{1,0:T(8,128)(2,1)} %project.3.refs_1_.refs_4_, ...), custom_call_target="tpu_custom_call" | custom-call | flops 60397977600 | bytes 471859200 | tf_op jit(solution)/shard_map/attn_bwd/pallas_call | solution.py:303
  259.6 5.8 %merge.12 = (bf16[2,128,2048]{2,1,0:T(8,128)(2,1)}, bf16[2,128,2048]{2,1,0:T(8,128)(2,1)}, bf16[2,256,1024]{2,1,0:T(8,128)(2,1)}, bf16[2,256,1024]{2,1,0:T(8,128)(2,1)}) custom-call(bf16[4,128,2048]{2,1,0:T(8,128)(2,1)} %get-tuple-element.212.refs_0_.refs_2_, bf16[4,128,2048]{2,1,0:T(8,128)(2,1)} %collective-permute-done.9.refs_1_.refs_3_, ...), custom_call_target="tpu_custom_call" | custom-call | tf_op jit(solution)/shard_map/merge/pallas_call | solution.py:716
  275.5 16.1 %attn_bwd.3 = (bf16[768,1024]{1,0:T(8,128)(2,1)}, bf16[3,1024,768]{2,1,0:T(8,128)(2,1)}, bf16[3,1024,768]{2,1,0:T(8,128)(2,1)}, f32[8,8,768]{2,1,0:T(8,128)}) custom-call(bf16[768,3072]{1,0:T(8,128)(2,1)} %project.4.q_ref.refs_2_.refs_5_, ...), custom_call_target="tpu_custom_call", output_to_operand_aliasing={{0}: (11, {}), {1}: (12, {}), {2}: (13, {}), {3}: (14, {})} | custom-call | flops 60397977600 | bytes 471859200 | tf_op jit(solution)/shard_map/attn_bwd/pallas_call | solution.py:303
  304.8 19.7 %norm_grad.1 = (bf16[3,256,1024]{2,1,0:T(8,128)(2,1)}, bf16[3,256,1024]{2,1,0:T(8,128)(2,1)}, f32[3,256,1024]{2,1,0:T(8,128)}, f32[1,1024]{1,0:T(1,128)}, f32[1,1024]{1,0:T(1,128)}) custom-call(bf16[3,256,1024]{2,1,0:T(8,128)(2,1)} %bitcast.88, bf16[3,1024,768]{2,1,0:T(8,128)(2,1)} %get-tuple-element.253.dk_ref.refs_5_, ...), custom_call_target="tpu_custom_call" | custom-call | flops 338228674560 | bytes 754974720 | tf_op jit(solution)/shard_map/norm_grad/pallas_call | solution.py:638
  330.4 24.6 %attn_weights.1 = (bf16[4,144,2048]{2,1,0:T(8,128)(2,1)}, bf16[4,128,2048]{2,1,0:T(8,128)(2,1)}, bf16[4,144,2048]{2,1,0:T(8,128)(2,1)}, bf16[4,128,2048]{2,1,0:T(8,128)(2,1)}) custom-call(bf16[3,1024,256]{2,1,0:T(8,128)(2,1)} %get-tuple-element.257.refs_0_, bf16[3,1024,256]{2,1,0:T(8,128)(2,1)} %get-tuple-element.258.refs_1_, ...), custom_call_target="tpu_custom_call" | custom-call | tf_op jit(solution)/shard_map/attn_weights/pallas_call | solution.py:586
  355.1 6.8 %collective-permute-done.15 = bf16[3,256,1024]{2,1,0:T(8,128)(2,1)S(1)} collective-permute-done((bf16[3,256,1024]{2,1,0:T(8,128)(2,1)}, bf16[3,256,1024]{2,1,0:T(8,128)(2,1)S(1)}, u32[]{:S(2)}, u32[]{:S(2)}) %collective-permute-start.15) | collective-permute-done | bytes 1572896 | tf_op jit(solution)/shard_map/ppermute | solution.py:920
  375.3 6.1 %merge.16 = (bf16[2,144,2048]{2,1,0:T(8,128)(2,1)}, bf16[2,144,2048]{2,1,0:T(8,128)(2,1)}, bf16[2,128,2048]{2,1,0:T(8,128)(2,1)}, bf16[2,128,2048]{2,1,0:T(8,128)(2,1)}) custom-call(bf16[4,144,2048]{2,1,0:T(8,128)(2,1)} %get-tuple-element.270.refs_0_.refs_2_, bf16[4,144,2048]{2,1,0:T(8,128)(2,1)} %copy-done, ...), custom_call_target="tpu_custom_call" | custom-call | tf_op jit(solution)/shard_map/merge/pallas_call | solution.py:716
  384.4 14.8 %reduce-scatter.2.cloned.1.call-done = bf16[128,1024]{1,0:T(8,128)(2,1)} async-done(((bf16[512,1024]{1,0:T(8,128)(2,1)}), bf16[128,1024]{1,0:T(8,128)(2,1)}) %reduce-scatter.2.cloned.1.call-update) | async-done | bytes 262160 | tf_op jit(solution)/shard_map/reduce_scatter | solution.py:916
  400.5 7.5 %collective-permute-done.19.refs_5_.refs_7_ = bf16[2,128,2048]{2,1,0:T(8,128)(2,1)S(1)} collective-permute-done((bf16[2,128,2048]{2,1,0:T(8,128)(2,1)}, bf16[2,128,2048]{2,1,0:T(8,128)(2,1)S(1)}, u32[]{:S(2)}, u32[]{:S(2)}) %collective-permute-start.19) | collective-permute-done | bytes 1048608 | tf_op jit(solution)/shard_map/ppermute | solution.py:744
  417.4 20.9 %all-gather.11.cloned.1.call-done = bf16[512,1024]{1,0:T(8,128)(2,1)} async-done(((bf16[128,1024]{1,0:T(8,128)(2,1)}), bf16[512,1024]{1,0:T(8,128)(2,1)}) %all-gather.11.cloned.1.call-update) | async-done | bytes 1048592 | tf_op jit(solution)/shard_map/all_gather | solution.py:917
  454.3 6.5 %first_back.1 = bf16[768,1024]{1,0:T(8,128)(2,1)} custom-call(f32[768,1024]{1,0:T(8,128)} %bitcast.83, bf16[768,1024]{1,0:T(8,128)(2,1)} %bitcast.31.back_ref, bf16[768,1024]{1,0:T(8,128)(2,1)} %bitcast.78, f32[768,1024]{1,0:T(8,128)} %get-tuple-element.303.gm_ref, f32[1,1024]{1,0:T(1,128)} %bitcast.112), custom_call_target="tpu_custom_call" | custom-call | tf_op jit(solution)/shard_map/first_back/pallas_call | solution.py:670
  462.3 39.2 %all-reduce.9.cloned.1.call-done = (bf16[128,2048]{1,0:T(8,128)(2,1)}, bf16[144,2048]{1,0:T(8,128)(2,1)}) async-done(((bf16[128,2048]{1,0:T(8,128)(2,1)}, bf16[144,2048]{1,0:T(8,128)(2,1)}), (bf16[128,2048]{1,0:T(8,128)(2,1)}, bf16[144,2048]{1,0:T(8,128)(2,1)})) %all-reduce.9.cloned.1.call-update) | async-done | bytes 1114128 | tf_op jit(solution)/shard_map/psum | solution.py:893
  (253 shorter events, 146.7 us)
Async XLA Ops:
  7.2 66.8 %all-gather.5.cloned.1.call-start = ((), (), s32[]{:S(2)}) async-start(), calls=%async_computation.1 | async-start | bytes 7077888 | tf_op jit(solution)/shard_map/all_gather | solution.py:812
  9.4 128.1 %all-gather.7.cloned.1.call-start = ((), (), s32[]{:S(2)}) async-start(), calls=%async_computation.2 | async-start | bytes 11796480 | tf_op jit(solution)/shard_map/all_gather | solution.py:836
  16.7 164.4 %all-gather.9.cloned.1.call-start = ((), (), s32[]{:S(2)}) async-start(), calls=%async_computation.3 | async-start | bytes 9437184 | tf_op jit(solution)/shard_map/all_gather | solution.py:836
  18.9 38.8 %collective-permute-start = (bf16[3,256,1024]{2,1,0:T(8,128)(2,1)S(1)}, bf16[3,256,1024]{2,1,0:T(8,128)(2,1)}, u32[]{:S(2)}, u32[]{:S(2)}) collective-permute-start(bf16[3,256,1024]{2,1,0:T(8,128)(2,1)S(1)} %bitcast.79), channel_id=1, source_target_pairs={{0,1},{1,2},{2,3},{4,5},{5,6},{6,7},{8,9},{9,10},{10,11},{12,13},{... | collective-permute-start | bytes 4718600 | tf_op jit(solution)/shard_map/ppermute | solution.py:816
  25.8 340.1 %all-reduce.11.cloned.1.call-start = ((), (), s32[]{:S(2)}) async-start(), calls=%async_computation.7 | async-start | bytes 2097152 | tf_op jit(solution)/shard_map/psum | solution.py:893
  57.7 38.3 %collective-permute-start.4 = (bf16[3,256,1024]{2,1,0:T(8,128)(2,1)}, bf16[3,256,1024]{2,1,0:T(8,128)(2,1)}, u32[]{:S(2)}, u32[]{:S(2)}) collective-permute-start(bf16[3,256,1024]{2,1,0:T(8,128)(2,1)} %collective-permute-done.x_ref.refs_1_), channel_id=1, source_target_pairs={{0,1},{1,2},{2,3},{4,5},{5,6},{6,7},{8,9},{9,10},{10,11},{12,13},{... | collective-permute-start | bytes 4718600 | tf_op jit(solution)/shard_map/ppermute | solution.py:862
  180.6 36.5 %collective-permute-start.5 = (bf16[4,128,2048]{2,1,0:T(8,128)(2,1)}, bf16[4,128,2048]{2,1,0:T(8,128)(2,1)}, u32[]{:S(2)}, u32[]{:S(2)}) collective-permute-start(bf16[4,128,2048]{2,1,0:T(8,128)(2,1)} %get-tuple-element.184), channel_id=1, source_target_pairs={{0,4},{4,0},{8,12},{12,8},{16,20},{20,16},{24,28},{28,24},{1,5},{5... | collective-permute-start | bytes 6291464 | tf_op jit(solution)/shard_map/ppermute | solution.py:735
  180.7 36.4 %collective-permute-start.6 = (bf16[4,256,1024]{2,1,0:T(8,128)(2,1)}, bf16[4,256,1024]{2,1,0:T(8,128)(2,1)}, u32[]{:S(2)}, u32[]{:S(2)}) collective-permute-start(bf16[4,256,1024]{2,1,0:T(8,128)(2,1)} %get-tuple-element.186), channel_id=1, source_target_pairs={{0,4},{4,0},{8,12},{12,8},{16,20},{20,16},{24,28},{28,24},{1,5},{5... | collective-permute-start | bytes 6291464 | tf_op jit(solution)/shard_map/ppermute | solution.py:735
  216.5 39.9 %collective-permute-start.10 = (bf16[4,256,1024]{2,1,0:T(8,128)(2,1)}, bf16[4,256,1024]{2,1,0:T(8,128)(2,1)S(1)}, u32[]{:S(2)}, u32[]{:S(2)}) collective-permute-start(bf16[4,256,1024]{2,1,0:T(8,128)(2,1)} %get-tuple-element.211), channel_id=1, source_target_pairs={{0,4},{4,0},{8,12},{12,8},{16,20},{20,16},{24,28},{28,24},{1,5},{5... | collective-permute-start | bytes 6291464 | tf_op jit(solution)/shard_map/ppermute | solution.py:735
  216.7 39.8 %collective-permute-start.9 = (bf16[4,128,2048]{2,1,0:T(8,128)(2,1)}, bf16[4,128,2048]{2,1,0:T(8,128)(2,1)}, u32[]{:S(2)}, u32[]{:S(2)}) collective-permute-start(bf16[4,128,2048]{2,1,0:T(8,128)(2,1)} %get-tuple-element.209), channel_id=1, source_target_pairs={{0,4},{4,0},{8,12},{12,8},{16,20},{20,16},{24,28},{28,24},{1,5},{5... | collective-permute-start | bytes 6291464 | tf_op jit(solution)/shard_map/ppermute | solution.py:735
  222.9 28.2 %collective-permute-start.7 = (bf16[2,128,2048]{2,1,0:T(8,128)(2,1)}, bf16[2,128,2048]{2,1,0:T(8,128)(2,1)S(1)}, u32[]{:S(2)}, u32[]{:S(2)}) collective-permute-start(bf16[2,128,2048]{2,1,0:T(8,128)(2,1)} %get-tuple-element.193), channel_id=1, source_target_pairs={{0,8},{4,12},{8,0},{12,4},{16,24},{20,28},{24,16},{28,20},{1,9},{5... | collective-permute-start | bytes 3145736 | tf_op jit(solution)/shard_map/ppermute | solution.py:744
  224.5 26.6 %collective-permute-start.8 = (bf16[2,256,1024]{2,1,0:T(8,128)(2,1)}, bf16[2,256,1024]{2,1,0:T(8,128)(2,1)S(1)}, u32[]{:S(2)}, u32[]{:S(2)}) collective-permute-start(bf16[2,256,1024]{2,1,0:T(8,128)(2,1)} %get-tuple-element.195), channel_id=1, source_target_pairs={{0,16},{4,20},{8,24},{12,28},{16,0},{20,4},{24,8},{28,12},{1,17},{... | collective-permute-start | bytes 3145736 | tf_op jit(solution)/shard_map/ppermute | solution.py:744
  273.6 23.7 %collective-permute-start.13 = (bf16[2,128,2048]{2,1,0:T(8,128)(2,1)}, bf16[2,128,2048]{2,1,0:T(8,128)(2,1)S(1)}, u32[]{:S(2)}, u32[]{:S(2)}) collective-permute-start(bf16[2,128,2048]{2,1,0:T(8,128)(2,1)} %get-tuple-element.225), channel_id=1, source_target_pairs={{0,8},{4,12},{8,0},{12,4},{16,24},{20,28},{24,16},{28,20},{1,9},{5... | collective-permute-start | bytes 3145736 | tf_op jit(solution)/shard_map/ppermute | solution.py:744
  274.1 23.4 %collective-permute-start.14 = (bf16[2,256,1024]{2,1,0:T(8,128)(2,1)}, bf16[2,256,1024]{2,1,0:T(8,128)(2,1)S(1)}, u32[]{:S(2)}, u32[]{:S(2)}) collective-permute-start(bf16[2,256,1024]{2,1,0:T(8,128)(2,1)} %get-tuple-element.227), channel_id=1, source_target_pairs={{0,16},{4,20},{8,24},{12,28},{16,0},{20,4},{24,8},{28,12},{1,17},{... | collective-permute-start | bytes 3145736 | tf_op jit(solution)/shard_map/ppermute | solution.py:744
  275.4 123.7 %reduce-scatter.2.cloned.1.call-start = ((), (), s32[]{:S(2)}) async-start(), calls=%async_computation.4 | async-start | bytes 1310720 | tf_op jit(solution)/shard_map/reduce_scatter | solution.py:916
  302.6 63.3 %collective-permute-start.22 = (bf16[1,128,2048]{2,1,0:T(8,128)(2,1)}, bf16[1,128,2048]{2,1,0:T(8,128)(2,1)}, u32[]{:S(2)}, u32[]{:S(2)}) collective-permute-start(bf16[1,128,2048]{2,1,0:T(8,128)(2,1)} %get-tuple-element.289), channel_id=1, source_target_pairs={{0,16},{4,20},{8,24},{12,28},{16,0},{20,4},{24,8},{28,12},{1,17},{... | collective-permute-start | bytes 1572872 | tf_op jit(solution)/shard_map/ppermute | solution.py:744
  304.0 61.9 %collective-permute-start.23 = (bf16[1,256,1024]{2,1,0:T(8,128)(2,1)}, bf16[1,256,1024]{2,1,0:T(8,128)(2,1)}, u32[]{:S(2)}, u32[]{:S(2)}) collective-permute-start(bf16[1,256,1024]{2,1,0:T(8,128)(2,1)} %get-tuple-element.291), channel_id=1, source_target_pairs={{0,8},{4,12},{8,0},{12,4},{16,24},{20,28},{24,16},{28,20},{1,9},{5... | collective-permute-start | bytes 1572872 | tf_op jit(solution)/shard_map/ppermute | solution.py:744
  324.4 37.4 %collective-permute-start.15 = (bf16[3,256,1024]{2,1,0:T(8,128)(2,1)}, bf16[3,256,1024]{2,1,0:T(8,128)(2,1)S(1)}, u32[]{:S(2)}, u32[]{:S(2)}) collective-permute-start(bf16[3,256,1024]{2,1,0:T(8,128)(2,1)} %get-tuple-element.276), channel_id=1, source_target_pairs={{1,0},{2,1},{3,2},{5,4},{6,5},{7,6},{9,8},{10,9},{11,10},{13,12},{... | collective-permute-start | bytes 4718600 | tf_op jit(solution)/shard_map/ppermute | solution.py:920
  372.0 66.3 %all-gather.11.cloned.1.call-start = ((), (), s32[]{:S(2)}) async-start(), calls=%async_computation.5 | async-start | bytes 1310720 | tf_op jit(solution)/shard_map/all_gather | solution.py:917
  381.3 28.3 %collective-permute-start.18 = (bf16[2,144,2048]{2,1,0:T(8,128)(2,1)}, bf16[2,144,2048]{2,1,0:T(8,128)(2,1)S(1)}, u32[]{:S(2)}, u32[]{:S(2)}) collective-permute-start(bf16[2,144,2048]{2,1,0:T(8,128)(2,1)} %get-tuple-element.281), channel_id=1, source_target_pairs={{0,8},{4,12},{8,0},{12,4},{16,24},{20,28},{24,16},{28,20},{1,9},{5... | collective-permute-start | bytes 3538952 | tf_op jit(solution)/shard_map/ppermute | solution.py:744
  382.9 25.1 %collective-permute-start.19 = (bf16[2,128,2048]{2,1,0:T(8,128)(2,1)}, bf16[2,128,2048]{2,1,0:T(8,128)(2,1)S(1)}, u32[]{:S(2)}, u32[]{:S(2)}) collective-permute-start(bf16[2,128,2048]{2,1,0:T(8,128)(2,1)} %get-tuple-element.283), channel_id=1, source_target_pairs={{0,16},{4,20},{8,24},{12,28},{16,0},{20,4},{24,8},{28,12},{1,17},{... | collective-permute-start | bytes 3145736 | tf_op jit(solution)/shard_map/ppermute | solution.py:744
  399.2 102.3 %all-reduce.9.cloned.1.call-start = ((), (), s32[]{:S(2)}) async-start(), calls=%async_computation.6 | async-start | bytes 2228224 | tf_op jit(solution)/shard_map/psum | solution.py:893
  399.2 55.0 %collective-permute-start.24 = (bf16[3,256,1024]{2,1,0:T(8,128)(2,1)}, bf16[3,256,1024]{2,1,0:T(8,128)(2,1)}, u32[]{:S(2)}, u32[]{:S(2)}) collective-permute-start(bf16[3,256,1024]{2,1,0:T(8,128)(2,1)} %bitcast.94), channel_id=1, source_target_pairs={{1,0},{2,1},{3,2},{5,4},{6,5},{7,6},{9,8},{10,9},{11,10},{13,12},{... | collective-permute-start | bytes 4718600 | tf_op jit(solution)/shard_map/ppermute | solution.py:940
  414.4 23.9 %collective-permute-start.20 = (bf16[1,144,2048]{2,1,0:T(8,128)(2,1)}, bf16[1,144,2048]{2,1,0:T(8,128)(2,1)S(1)}, u32[]{:S(2)}, u32[]{:S(2)}) collective-permute-start(bf16[1,144,2048]{2,1,0:T(8,128)(2,1)} %get-tuple-element.285), channel_id=1, source_target_pairs={{0,16},{4,20},{8,24},{12,28},{16,0},{20,4},{24,8},{28,12},{1,17},{... | collective-permute-start | bytes 1769480 | tf_op jit(solution)/shard_map/ppermute | solution.py:744
  (51 other events, 362.7 us)
Sparse Core Ops, SparseCore 0:
  9.9 48.8 all-gather.4
  61.3 63.2 all-gather.6
  126.5 54.4 all-gather.8
  275.5 54.0 all-reduce.10
  372.1 26.9 reduce-scatter.1
  400.6 37.6 all-gather.10
  441.9 59.6 all-reduce.8
